TPU v7x, 128 devices: a whole 4x4x4 slice. The times are simulated.
128 devices in a mesh: row: 8 (over x, core), col: 16 (over z, y).
Axes of the slice: x: 4, y: 4, z: 4, core: 2. Of those that a mesh axis runs over, the one named last changes fastest.
Arguments:
- panel_inverse: bfloat16 [2, 2, 2, 1024, 1024], P(None, None, None, ('row', 'col')), may hold values from -0.125 to 0.125
- panel_below: bfloat16 [2, 2, 1024, 1024], P(None, None, ('row', 'col')), may hold values from -0.5 to 0.5
- trail_factor: bfloat16 [2, 2, 2, 131072, 1024], P(None, None, None, ('row', 'col')), may hold values from -0.125 to 0.125
- first_rhs: bfloat16 [2, 2, 1024, 256], replicated, may hold values from -6 to 6
- second_rhs: bfloat16 [2, 2, 1024, 256], P(None, None, ('row', 'col')), may hold values from -6 to 6
- trail_rhs: bfloat16 [2, 2, 131072, 256], P(None, None, ('row', 'col')), may hold values from -6 to 6
- shape_tiles: float32 [2, 9, 2, 1024], P(None, None, None, ('row', 'col')), may hold values from -0.25 to 0.25
- element_vertices: int32 [2, 1024, 3], P(None, ('row', 'col')), may hold values from 0 to 1023, all different within a row
- vertex_slot: int32 [1024], replicated, may hold values from 0 to 1023, each once
Outputs:
- panel_solution: bfloat16 [2, 2, 2, 1024, 256], P(None, None, None, ('row', 'col'))
- trail_update: bfloat16 [2, 2, 131072, 256], P(None, None, ('row', 'col'))
- vertex_gradient: float32 [3, 1024], P(None, ('row', 'col'))
Inputs may be any that keep to these rules, and one draw needn't show every extreme that they name: `element_vertices`: each element names three different vertices, and every vertex is named by some element. `vertex_slot`: each slot is given to exactly one vertex.
All inputs are finite; a program needn't handle non-finite values.
Results may differ from a plain program's by a relative error of at most 0.0067.
Values may be sent and summed in bfloat16 or wider, within the bound.
No kernel may reach another device: no remote copies, remote signals or barrier semaphores. Data moves between devices by JAX's collectives and lax.ppermute only.
A program may use at most 128 MiB of HBM per device.

v0:
```python
import jax
import jax.numpy as jnp
from jax import lax
from jax.sharding import PartitionSpec as P


def complex_rows(left_pair, right_pair, form):
    real_part = jnp.einsum(
        form, left_pair[0], right_pair[0], preferred_element_type=jnp.float32
    ) - jnp.einsum(form, left_pair[1], right_pair[1], preferred_element_type=jnp.float32)
    imag_part = jnp.einsum(
        form, left_pair[0], right_pair[1], preferred_element_type=jnp.float32
    ) + jnp.einsum(form, left_pair[1], right_pair[0], preferred_element_type=jnp.float32)
    return (real_part, imag_part)


def trail_terms(totals, factor_section, solution_parts):
    term_real, term_imag = complex_rows(
        (factor_section[:, 0], factor_section[:, 1]), solution_parts, "srn,sna->sra"
    )
    return (totals[0] - term_real, totals[1] - term_imag)


def couple_partials(panel_solution, shape_tiles):
    forward = panel_solution[0].astype(jnp.float32)
    adjoint = panel_solution[1].astype(jnp.float32)
    coupling_real = jnp.sum(forward[:, 0] * adjoint[:, 0] - forward[:, 1] * adjoint[:, 1], axis=-1)
    coupling_imag = jnp.sum(forward[:, 0] * adjoint[:, 1] + forward[:, 1] * adjoint[:, 0], axis=-1)
    return -(shape_tiles[0] * coupling_real - shape_tiles[1] * coupling_imag)


def spread_vertices(partials, element_vertices, vertex_slot, vertex_count):
    values = jnp.transpose(
        partials.reshape(3, 3, partials.shape[1], partials.shape[2]), (1, 2, 3, 0)
    )
    slots = vertex_slot[element_vertices]
    empty = jnp.zeros((3, vertex_count), jnp.float32)
    return empty.at[:, slots.reshape(-1)].add(values.reshape(3, -1))


def body(
    panel_inverse,
    panel_below,
    trail_factor,
    first_rhs,
    second_rhs,
    trail_rhs,
    shape_tiles,
    element_vertices,
    vertex_slot,
):
    form = "srn,sna->sra"
    first_parts = complex_rows(
        (panel_inverse[:, 0, 0], panel_inverse[:, 0, 1]), (first_rhs[:, 0], first_rhs[:, 1]), form
    )
    first_real = first_parts[0].astype(jnp.bfloat16)
    first_imag = first_parts[1].astype(jnp.bfloat16)
    own_rows = first_real.shape[1]
    own_right = second_rhs.astype(jnp.float32)
    below_real, below_imag = complex_rows(
        (panel_below[:, 0], panel_below[:, 1]), (first_real, first_imag), "sji,sja->sia"
    )
    offset = lax.axis_index(("row", "col")) * own_rows

    def embed_rows(negated, own_part):
        window = lax.dynamic_slice_in_dim(negated, offset, own_rows, 1) + own_part
        return lax.dynamic_update_slice_in_dim(negated, window, offset, 1)

    summed = lax.psum(
        (embed_rows(-below_real, own_right[:, 0]), embed_rows(-below_imag, own_right[:, 1])),
        ("row", "col"),
    )
    right_real = summed[0].astype(jnp.bfloat16)
    right_imag = summed[1].astype(jnp.bfloat16)
    second_parts = complex_rows(
        (panel_inverse[:, 1, 0], panel_inverse[:, 1, 1]), (right_real, right_imag), form
    )
    second_real = second_parts[0].astype(jnp.bfloat16)
    second_imag = second_parts[1].astype(jnp.bfloat16)
    initial = (trail_rhs[:, 0].astype(jnp.float32), trail_rhs[:, 1].astype(jnp.float32))
    first_factor = trail_factor[:, 0]
    second_factor = trail_factor[:, 1]
    totals = trail_terms(
        initial,
        first_factor,
        (
            lax.all_gather(first_real, ("row", "col"), axis=1, tiled=True),
            lax.all_gather(first_imag, ("row", "col"), axis=1, tiled=True),
        ),
    )
    totals = trail_terms(
        totals,
        second_factor,
        (
            lax.all_gather(second_real, ("row", "col"), axis=1, tiled=True),
            lax.all_gather(second_imag, ("row", "col"), axis=1, tiled=True),
        ),
    )
    trail_update = jnp.stack(totals, axis=1).astype(jnp.bfloat16)
    panel_solution = jnp.stack(
        [
            jnp.stack([first_real, first_imag], axis=1),
            jnp.stack([second_real, second_imag], axis=1),
        ],
        axis=1,
    )
    partials = couple_partials(panel_solution, shape_tiles)
    dense_local = spread_vertices(partials, element_vertices, vertex_slot, vertex_slot.shape[0])
    vertex_gradient = lax.psum_scatter(dense_local, ("row", "col"), scatter_dimension=1, tiled=True)
    return (panel_solution, trail_update, vertex_gradient)


def solution(mesh):
    return jax.shard_map(
        body,
        mesh=mesh,
        in_specs=(
            P(None, None, None, ("row", "col"), None),
            P(None, None, ("row", "col"), None),
            P(None, None, None, ("row", "col"), None),
            P(),
            P(None, None, ("row", "col"), None),
            P(None, None, ("row", "col"), None),
            P(None, None, None, ("row", "col")),
            P(None, ("row", "col"), None),
            P(),
        ),
        out_specs=(
            P(None, None, None, ("row", "col"), None),
            P(None, None, ("row", "col"), None),
            P(None, ("row", "col")),
        ),
        check_vma=False,
    )
```

profile of v0, /device:TPU:1, one launch (start us, length us, event | category | flops | bytes accessed | tf_op | source)
XLA Modules:
  0.0 293.4 jit_solution(7776141452226095371)
XLA Ops:
  7.3 1.6 fusion.18
  8.9 2.1 fusion.15
  11.1 1.0 fusion.22
  12.1 0.9 fusion.14
  13.6 0.5 add_negate_fusion
  15.1 0.5 subtract_negate_fusion
  15.6 1.3 copy-done.2
  17.1 1.8 dynamic_update_slice.6
  18.9 1.1 dynamic_update_slice.7
  20.0 110.5 %all-reduce.3 = (bf16[2,1024,256]{1,2,0:T(8,128)(2,1)}, bf16[2,1024,256]{1,2,0:T(8,128)(2,1)S(1)}) all-reduce(f32[2,1024,256]{1,2,0:T(8,128)S(1)} %dynamic_update_slice.7, f32[2,1024,256]{1,2,0:T(8,128)} %dynamic_update_slice.6), channel_id=1, replica_groups=mesh['row'=8,'col'=16] {'row','col'}, use_global_device_ids=true, to_apply=%region_1.0 | all-reduce | flops 1048576 | bytes 6291456 | tf_op jit(solution)/shard_map/psum | solution.py:69
  130.9 2.2 fusion.16
  133.5 1.0 fusion.17
  134.6 0.7 maximum_bitcast_fusion.1
  136.1 0.7 gather_fusion
  136.9 0.9 scatter_custom_fusion
  137.8 68.4 %all-reduce = f32[3,1024]{0,1:T(8,128)S(1)} all-reduce(f32[3,1024]{0,1:T(8,128)S(1)} %scatter_custom_fusion), channel_id=2, replica_groups=mesh['row'=8,'col'=16] {'row','col'}, use_global_device_ids=true, to_apply=%region_5.0.clone | all-reduce | flops 3072 | bytes 24576
  206.2 0.7 copy.85
  206.9 11.8 %fusion.69 = (bf16[2,1,2,1024,1024]{4,3,2,1,0:T(8,128)(2,1)}, bf16[2,1,2,1024,1024]{4,3,2,1,0:T(8,128)(2,1)}) fusion(bf16[2,2,2,1024,1024]{4,3,2,1,0:T(8,128)(2,1)} %param.11), kind=kLoop, calls=%fused_computation.101 | loop fusion | bytes 33554432 | tf_op jit(solution)/shard_map/slice | solution.py:81
  218.8 0.5 copy.98
  219.4 0.5 copy.101
  219.9 0.6 copy.83
  220.5 11.6 %copy_bitcast_fusion = (bf16[2,2,1024,1024]{3,2,0,1:T(8,128)(2,1)}, bf16[2,2,1024,1024]{3,2,0,1:T(8,128)(2,1)}) fusion(bf16[2,1,2,1024,1024]{4,3,2,1,0:T(8,128)(2,1)} %get-tuple-element.17, bf16[2,1,2,1024,1024]{4,3,2,1,0:T(8,128)(2,1)} %get-tuple-element.16), kind=kLoop, calls=%fused_computation.2 | loop fusion | bytes 33554432 | tf_op jit(solution)/shard_map/squeeze | solution.py:82
  232.2 5.3 %fusion.3 = f32[2,256,1024]{2,1,0:T(8,128)} fusion(bf16[2,1024,256]{2,1,0:T(8,128)(2,1)} %all-gather.7.cloned.1.call-done, bf16[2,2,1024,1024]{3,2,0,1:T(8,128)(2,1)} %get-tuple-element.25), kind=kOutput, calls=%fused_computation.11 | convolution fusion | flops 1073741824 | bytes 7340032 | tf_op jit(solution)/shard_map/srn,sna->sra/dot_general | solution.py:10
  237.5 4.9 %fusion = f32[2,256,1024]{2,1,0:T(8,128)} fusion(bf16[2,1024,256]{2,1,0:T(8,128)(2,1)S(1)} %copy-done.19, bf16[2,2,1024,1024]{3,2,0,1:T(8,128)(2,1)} %get-tuple-element.25), kind=kOutput, calls=%fused_computation.8 | convolution fusion | flops 1073741824 | bytes 7340032 | tf_op jit(solution)/shard_map/srn,sna->sra/dot_general | solution.py:11
  242.4 5.4 %fusion.1 = f32[2,256,1024]{2,1,0:T(8,128)} fusion(bf16[2,1024,256]{2,1,0:T(8,128)(2,1)} %all-gather.5.cloned.1.call-done, bf16[2,2,1024,1024]{3,2,0,1:T(8,128)(2,1)} %get-tuple-element.25), kind=kOutput, calls=%fused_computation.9 | convolution fusion | flops 1073741824 | bytes 7340032 | tf_op jit(solution)/shard_map/srn,sna->sra/dot_general | solution.py:8
  247.8 5.0 %fusion.2 = f32[2,256,1024]{2,1,0:T(8,128)} fusion(bf16[2,1024,256]{2,1,0:T(8,128)(2,1)S(1)} %copy-done.20, bf16[2,2,1024,1024]{3,2,0,1:T(8,128)(2,1)} %get-tuple-element.25), kind=kOutput, calls=%fused_computation.10 | convolution fusion | flops 1073741824 | bytes 7340032 | tf_op jit(solution)/shard_map/srn,sna->sra/dot_general | solution.py:13
  252.8 5.3 %fusion.5 = f32[2,256,1024]{2,1,0:T(8,128)} fusion(bf16[2,1024,256]{2,1,0:T(8,128)(2,1)} %all-gather.9.cloned.1.call-done, bf16[2,2,1024,1024]{3,2,0,1:T(8,128)(2,1)} %get-tuple-element.24), kind=kOutput, calls=%fused_computation.13 | convolution fusion | flops 1073741824 | bytes 7340032 | tf_op jit(solution)/shard_map/srn,sna->sra/dot_general | solution.py:8
  258.1 13.6 %all-gather.11.cloned.1.call-done = bf16[2,1024,256]{2,1,0:T(8,128)(2,1)} async-done(((bf16[2,8,256]{2,1,0:T(8,128)(2,1)}), bf16[2,1024,256]{2,1,0:T(8,128)(2,1)}) %all-gather.11.cloned.1.call-update) | async-done | bytes 1048592 | tf_op jit(solution)/shard_map/all_gather | solution.py:96
  271.7 4.1 %fusion.4 = f32[2,256,1024]{2,1,0:T(8,128)S(1)} fusion(bf16[2,1024,256]{2,1,0:T(8,128)(2,1)} %all-gather.11.cloned.1.call-done, bf16[2,2,1024,1024]{3,2,0,1:T(8,128)(2,1)} %get-tuple-element.24), kind=kOutput, calls=%fused_computation.12 | convolution fusion | flops 1073741824 | bytes 7340032 | tf_op jit(solution)/shard_map/srn,sna->sra/dot_general | solution.py:11
  275.8 5.5 %fusion.12 = bf16[2,1,1024,256]{2,3,0,1:T(8,128)(2,1)S(1)} fusion(f32[2,256,1024]{2,1,0:T(8,128)} %fusion.5, bf16[2,1024,256]{2,1,0:T(8,128)(2,1)S(1)} %copy-done.10, bf16[2,2,1024,1024]{3,2,0,1:T(8,128)(2,1)} %get-tuple-element.24, f32[2,256,1024]{2,1,0:T(8,128)} %fusion.1, f32[2,256,1024]{2,1,0:T(8,128)S(1)} %copy-done.7, ...), kind=kOutput, calls=%fused_computation.25 | convolution fusion | flops 1076887552 | bytes 13631488 | tf_op jit(solution)/shard_map/srn,sna->sra/dot_general | solution.py:10
  282.0 2.2 fusion.13
  284.3 2.6 copy.84
  (84 shorter events, 4.5 us)
Async XLA Ops:
  7.2 129.0 %copy-start = (s32[1024]{0:T(1024)S(1)}, s32[1024]{0:T(1024)}, u32[]{:S(2)}) copy-start(s32[1024]{0:T(1024)} %param.17) | copy-start | bytes 12292
  7.2 3.9 %copy-start.3 = (bf16[2,2,1024,256]{3,2,1,0:T(8,128)(2,1)S(1)}, bf16[2,2,1024,256]{3,2,1,0:T(8,128)(2,1)}, u32[]{:S(2)}) copy-start(bf16[2,2,1024,256]{3,2,1,0:T(8,128)(2,1)} %param.12) | copy-start | bytes 6291460
  7.2 4.9 %copy-start.11 = (bf16[2,2,2,8,1024]{4,3,2,1,0:T(8,128)(2,1)S(1)}, bf16[2,2,2,8,1024]{4,3,2,1,0:T(8,128)(2,1)}, u32[]{:S(2)}) copy-start(bf16[2,2,2,8,1024]{4,3,2,1,0:T(8,128)(2,1)} %param.9) | copy-start | bytes 393220
  7.2 5.8 %copy-start.12 = (bf16[2,2,8,1024]{3,2,1,0:T(8,128)(2,1)S(1)}, bf16[2,2,8,1024]{3,2,1,0:T(8,128)(2,1)}, u32[]{:S(2)}) copy-start(bf16[2,2,8,1024]{3,2,1,0:T(8,128)(2,1)} %param.10) | copy-start | bytes 196612
  7.2 225.0 %all-gather.7.cloned.1.call-start = ((), (), s32[]{:S(2)}) async-start(), calls=%async_computation.1 | async-start | bytes 1056768 | tf_op jit(solution)/shard_map/all_gather | solution.py:88
  11.0 2.0 copy-start.13
  11.0 231.4 %all-gather.5.cloned.1.call-start = ((), (), s32[]{:S(2)}) async-start(), calls=%async_computation | async-start | bytes 1056768 | tf_op jit(solution)/shard_map/all_gather | solution.py:87
  12.9 0.7 copy-start.14
  13.0 239.8 %all-gather.9.cloned.1.call-start = ((), (), s32[]{:S(2)}) async-start(), calls=%async_computation.2 | async-start | bytes 1056768 | tf_op jit(solution)/shard_map/all_gather | solution.py:95
  13.6 0.7 copy-start.16
  15.5 1.3 copy-start.2
  130.5 2.7 copy-start.4
  130.5 4.9 %copy-start.17 = (f32[2,9,2,8]{1,3,2,0:T(8,128)S(1)}, f32[2,9,2,8]{1,3,2,0:T(8,128)}, u32[]{:S(2)}) copy-start(f32[2,9,2,8]{1,3,2,0:T(8,128)} %param.15) | copy-start | bytes 3460
  130.9 5.1 %copy-start.18 = (s32[2,8,3]{1,0,2:T(2,128)S(1)}, s32[2,8,3]{1,0,2:T(2,128)}, u32[]{:S(2)}) copy-start(s32[2,8,3]{1,0,2:T(2,128)} %param.16) | copy-start | bytes 580
  133.1 1.5 copy-start.15
  133.1 138.6 %all-gather.11.cloned.1.call-start = ((), (), s32[]{:S(2)}) async-start(), calls=%async_computation.3 | async-start | bytes 1056768 | tf_op jit(solution)/shard_map/all_gather | solution.py:96
  206.9 11.8 %copy-start.5 = (bf16[2,2,1024,256]{3,2,1,0:T(8,128)(2,1)S(1)}, bf16[2,2,1024,256]{3,2,1,0:T(8,128)(2,1)}, u32[]{:S(2)}) copy-start(bf16[2,2,1024,256]{3,2,1,0:T(8,128)(2,1)} %param.14) | copy-start | bytes 6291460
  232.2 5.3 %copy-start.19 = (bf16[2,1024,256]{2,1,0:T(8,128)(2,1)S(1)}, bf16[2,1024,256]{2,1,0:T(8,128)(2,1)}, u32[]{:S(2)}) copy-start(bf16[2,1024,256]{2,1,0:T(8,128)(2,1)} %all-gather.7.cloned.1.call-done) | copy-start | bytes 3145732
  242.4 5.4 %copy-start.20 = (bf16[2,1024,256]{2,1,0:T(8,128)(2,1)S(1)}, bf16[2,1024,256]{2,1,0:T(8,128)(2,1)}, u32[]{:S(2)}) copy-start(bf16[2,1024,256]{2,1,0:T(8,128)(2,1)} %all-gather.5.cloned.1.call-done) | copy-start | bytes 3145732
  271.7 4.1 %copy-start.7 = (f32[2,256,1024]{2,1,0:T(8,128)S(1)}, f32[2,256,1024]{2,1,0:T(8,128)}, u32[]{:S(2)}) copy-start(f32[2,256,1024]{2,1,0:T(8,128)} %fusion.3) | copy-start | bytes 6291460
  271.7 4.1 %copy-start.10 = (bf16[2,1024,256]{2,1,0:T(8,128)(2,1)S(1)}, bf16[2,1024,256]{2,1,0:T(8,128)(2,1)}, u32[]{:S(2)}) copy-start(bf16[2,1024,256]{2,1,0:T(8,128)(2,1)} %all-gather.11.cloned.1.call-done) | copy-start | bytes 3145732
  271.7 9.6 %slice-start = ((s8[8388608]{0:T(1024)(128)(4,1)}), s8[4194304]{0:T(1024)(128)(4,1)S(1)}, s32[]{:S(2)}) async-start(s8[8388608]{0:T(1024)(128)(4,1)} %bitcast.173), calls=%async_computation.4 | async-start | bytes 8388608
  275.8 5.6 %slice-start.1 = ((s8[8388608]{0:T(1024)(128)(4,1)}), s8[4194304]{0:T(1024)(128)(4,1)S(1)}, s32[]{:S(2)}) async-start(s8[8388608]{0:T(1024)(128)(4,1)} %bitcast.173), calls=%async_computation.5 | async-start | bytes 8388608
  275.8 5.6 %copy-start.6 = (f32[2,256,1024]{2,1,0:T(8,128)S(1)}, f32[2,256,1024]{2,1,0:T(8,128)}, u32[]{:S(2)}) copy-start(f32[2,256,1024]{2,1,0:T(8,128)} %fusion) | copy-start | bytes 6291460
  275.8 5.9 %copy-start.8 = (f32[2,256,1024]{2,1,0:T(8,128)S(1)}, f32[2,256,1024]{2,1,0:T(8,128)}, u32[]{:S(2)}) copy-start(f32[2,256,1024]{2,1,0:T(8,128)} %fusion.2) | copy-start | bytes 6291460
  275.8 6.2 %copy-start.9 = (bf16[2,1024,256]{2,1,0:T(8,128)(2,1)S(1)}, bf16[2,1024,256]{2,1,0:T(8,128)(2,1)}, u32[]{:S(2)}) copy-start(bf16[2,1024,256]{2,1,0:T(8,128)(2,1)} %all-gather.9.cloned.1.call-done) | copy-start | bytes 3145732
  284.1 2.8 copy-start.1
Sparse Core Ops, SparseCore 0:
  11.1 67.5 all-gather.6
  81.6 61.5 all-gather.4
  146.1 61.5 all-gather.8
  210.3 61.3 all-gather.10
where the time goes:
time: 294 us; the launch traced here: 293 us
  blocking collectives  179 us (61%)
  matrix products  49 us (17%)
  local copies, waits for them, and re-layouts  35.3 us (12%)
  between operations  14.2 us (5%)
  waiting for transfers between devices  13.7 us (5%)
    psum x1, blocking collectives, body(): lax.psum((embed_rows(-below_real, own_right[:, 0]), embed_rows(-below_ima...  111 us
    unnamed x1, blocking collectives  68.4 us
    dot_general x5, matrix products, complex_rows(): jnp.einsum(form, left_pair[1], right_pair[1], preferred_element_type=jnp....  14.3 us
    all_gather x1, waiting for transfers between devices, body(): lax.all_gather(second_imag, ('row', 'col'), axis=1, tiled=True)  13.6 us
    dot_general x5, matrix products, complex_rows(): jnp.einsum(form, left_pair[0], right_pair[0], preferred_element_type=jnp....  12.5 us
    slice x1, local copies, waits for them, and re-layouts, body(): first_factor = trail_factor[:, 0]  11.8 us
    squeeze x1, local copies, waits for them, and re-layouts, body(): second_factor = trail_factor[:, 1]  11.6 us
    dot_general x5, matrix products, complex_rows(): jnp.einsum(form, left_pair[0], right_pair[1], preferred_element_type=jnp....  11.5 us
  transfers between devices with their start and end apart: 4, of which 1 were waited for; matrix products, arithmetic and copies ran while one was open for 22% of the time, Pallas kernels for 0%

commit v1 on v0

v1 whole, which is shorter than its diff:
```python
import jax
import jax.numpy as jnp
from jax import lax
from jax.sharding import Mesh
from jax.sharding import PartitionSpec as P

ALL = ("x", "core", "col")
F32 = jnp.float32
BF16 = jnp.bfloat16


def complex_pair(left_real, left_imag, right):
    stacked = jnp.concatenate([left_real, left_imag], axis=0)
    product = jnp.dot(stacked, right, preferred_element_type=F32)
    return fold_parts(product)


def fold_parts(product):
    half = product.shape[0] // 2
    top, low = product[:half], product[half:]
    return jnp.concatenate([top[:, :64] - low[:, 64:], top[:, 64:] + low[:, :64]], axis=1)


def complex_rows(left, right):
    form = "prn,qna->pqra"
    product = jnp.einsum(form, left, right, preferred_element_type=F32)
    return jnp.stack([product[0, 0] - product[1, 1], product[0, 1] + product[1, 0]])


def gather_x(value, x):
    rounds = [value]
    for step in range(1, 4):
        rounds.append(lax.ppermute(value, "x", [(i, (i + step) % 4) for i in range(4)]))
    stacked = jnp.stack(rounds)
    return jnp.stack([lax.dynamic_index_in_dim(stacked, (x - i) % 4, 0, keepdims=False) for i in range(4)])


def swap_core(value):
    return lax.ppermute(value, "core", [(0, 1), (1, 0)])


def element_tile(shape_tiles, element_vertices, vertex_slot):
    values = shape_tiles.transpose(3, 0, 2, 1).reshape(8, 36)
    high = lax.reduce_precision(values, 8, 7)
    rest = values - high
    mid = lax.reduce_precision(rest, 8, 7)
    low = rest - mid
    slots = vertex_slot[element_vertices].transpose(1, 0, 2).reshape(8, 6)
    parts = [high, mid, low, (slots // 32).astype(F32), (slots % 32).astype(F32), jnp.zeros((8, 8), F32)]
    return jnp.concatenate(parts, axis=1).astype(BF16)


def body(
    panel_inverse,
    panel_below,
    trail_factor,
    first_rhs,
    second_rhs,
    trail_rhs,
    shape_tiles,
    element_vertices,
    vertex_slot,
):
    x = lax.axis_index("x")
    core = lax.axis_index("core")
    device = lax.axis_index(ALL)
    tile = element_tile(shape_tiles, element_vertices, vertex_slot)

    first = jnp.stack(
        [complex_rows(panel_inverse[s, 0], first_rhs[s]) for s in range(2)]
    ).astype(BF16)
    send_first = first.reshape(2, 2, 8, 4, 64).transpose(3, 0, 2, 1, 4).reshape(4, 2, 1, 8, 128)
    send_below = (
        panel_below.reshape(2, 2, 8, 8, 16, 8).transpose(0, 4, 2, 1, 3, 5).reshape(1, 2, 16, 8, 128)
    )
    full = (4, 2, 16, 8, 128)
    send = jnp.stack([jnp.broadcast_to(send_first, full), jnp.broadcast_to(send_below, full)], axis=3)
    received = lax.all_to_all(send.reshape(128, 2, 8, 128), ALL, 0, 0, tiled=True)
    first_block = received[:, 0].reshape(1024, 128)
    below_block = received[:, 1].reshape(1024, 128)

    pack = jnp.concatenate([panel_inverse[:, 1], second_rhs], axis=-1)
    own = lax.dynamic_index_in_dim(pack, core, 0, keepdims=False)
    other = swap_core(lax.dynamic_index_in_dim(pack, 1 - core, 0, keepdims=False))
    chip = jnp.where(core == 0, jnp.stack([own, other]), jnp.stack([other, own]))
    rows = gather_x(chip, x)
    rows = rows.transpose(2, 0, 1, 3, 4).reshape(2, 64, 1280)
    inverse_rows = rows[:, :, :1024]
    right_rows = lax.dynamic_slice_in_dim(rows[:, :, 1024:], 64 * x, 64, 2)
    right_rows = jnp.concatenate([right_rows[0], right_rows[1]], axis=1).astype(F32)

    product = lax.dot_general(
        below_block, first_block, (((0,), (0,)), ((), ())), preferred_element_type=F32
    )
    right = (right_rows - fold_parts(product)).astype(BF16)
    send = jnp.broadcast_to(jnp.concatenate([right, tile])[None], (16, 72, 128))
    received = lax.all_to_all(send, "col", 0, 0, tiled=True)
    right_block = received[:, :64].reshape(16, 8, 8, 128).transpose(1, 0, 2, 3).reshape(1024, 128)
    tiles = received[:, 64:].reshape(128, 128)
    second = complex_pair(inverse_rows[0], inverse_rows[1], right_block).astype(BF16)

    first_all = gather_x(jnp.concatenate([first_block, tiles]), x)
    first_other = swap_core(first_all)

    send = jnp.broadcast_to(second[None], (64, 64, 128))
    second_all = lax.all_to_all(send, ("x", "col"), 0, 0, tiled=True)
    second_all = (
        second_all.reshape(4, 16, 8, 8, 128).transpose(0, 2, 1, 3, 4).reshape(4, 1024, 128)
    )
    second_other = swap_core(second_all)

    def by_system(mine, theirs):
        pair = jnp.where(core == 0, jnp.stack([mine, theirs]), jnp.stack([theirs, mine]))
        return pair.reshape(2, 4, -1, 2, 64).transpose(0, 3, 2, 1, 4).reshape(2, 2, -1, 256)

    first_full = by_system(first_all[:, :1024], first_other[:, :1024])
    second_full = by_system(second_all, second_other)

    updates = []
    for s in range(2):
        total = trail_rhs[s].astype(F32) - complex_rows(trail_factor[s, 0], first_full[s])
        total = total - complex_rows(trail_factor[s, 1], second_full[s])
        updates.append(total)
    trail_update = jnp.stack(updates).astype(BF16)

    own_second = lax.dynamic_slice_in_dim(second_full, 8 * device, 8, 2)
    panel_solution = jnp.stack([first, own_second], axis=1)

    tiles_pair = jnp.stack([first_all[:, 1024:], first_other[:, 1024:]], axis=1)
    tiles_pair = jnp.where(core == 0, tiles_pair, tiles_pair[:, ::-1]).reshape(1024, 128).astype(F32)
    shapes = tiles_pair[:, :36] + tiles_pair[:, 36:72] + tiles_pair[:, 72:108]
    shapes = shapes.reshape(1024, 2, 2, 9)
    slots = 32.0 * tiles_pair[:, 108:114] + tiles_pair[:, 114:120]
    slots = slots.reshape(1024, 2, 3)
    mask = slots[..., None] == (8 * device + jnp.arange(8)).astype(F32)
    gradient = jnp.zeros((3, 8), F32)
    for t, full in enumerate((first_full, second_full)):
        forward = full[0].astype(F32)
        adjoint = full[1].astype(F32)
        real = jnp.sum(forward[0] * adjoint[0] - forward[1] * adjoint[1], axis=-1)
        imag = jnp.sum(forward[0] * adjoint[1] + forward[1] * adjoint[0], axis=-1)
        partial = -(shapes[:, 0, t] * real[:, None] - shapes[:, 1, t] * imag[:, None])
        partial = partial.reshape(1024, 3, 3)
        gradient = gradient + jnp.sum(
            jnp.where(mask[:, t, :, None, :], partial[..., None], 0.0), axis=(0, 1)
        )
    return (panel_solution, trail_update, gradient)


def solution(mesh):
    fine = Mesh(mesh.devices.reshape(4, 2, 16), ALL)
    return jax.shard_map(
        body,
        mesh=fine,
        in_specs=(
            P(None, None, None, ALL, None),
            P(None, None, ALL, None),
            P(None, None, None, ALL, None),
            P(),
            P(None, None, ALL, None),
            P(None, None, ALL, None),
            P(None, None, None, ALL),
            P(None, ALL, None),
            P(),
        ),
        out_specs=(
            P(None, None, None, ALL, None),
            P(None, None, ALL, None),
            P(None, ALL),
        ),
        check_vma=False,
    )
```

time: 294 us -> 217 us (0.74)
  blocking collectives: 179 us -> 0 us
  local copies, waits for them, and re-layouts: 35.3 us -> 92.5 us
  other arithmetic: 2.17 us -> 48.6 us
  matrix products: 49 us -> 17.5 us
  starting transfers between devices: 0.16 us -> 31.1 us
  between operations: 14.2 us -> 1.49 us
  waiting for transfers between devices: 13.7 us -> 24.2 us
    psum x1 -> x0, blocking collectives: 111 us -> none  [body(): lax.psum((embed_rows(-below_real, own_right[:, 0]), embed_rows(-below_ima...]
    unnamed x1 -> x0, blocking collectives: 68.4 us -> none
    dot_general x20 -> x8, matrix products: 49 us -> 17.5 us  [the longest x6 17.1 us: complex_rows(): product = jnp.einsum(form, left, right, preferred_element_type=F32)]
    transpose x1 -> x3, other arithmetic: 0.01 us -> 27.6 us  [the longest x1 27.5 us: by_system(): pair.reshape(2, 4, -1, 2, 64).transpose(0, 3, 2, 1, 4)]
    slice x5 -> x14, local copies, waits for them, and re-layouts: 12.1 us -> 37.1 us  [the longest x3 15.2 us: body(): total = total - complex_rows(trail_factor[s, 1], second_full[s])]
    all_to_all x0 -> x3, starting transfers between devices: none -> 20.9 us  [the longest x1 10.2 us: body(): lax.all_to_all(send.reshape(128, 2, 8, 128), ALL, 0, 0, tiled=True)]
    another operation x0 -> x10, local copies, waits for them, and re-layouts: none -> 20.5 us  [the longest x4 19.2 us: by_system(): jnp.stack([mine, theirs])]
    ppermute x0 -> x9, waiting for transfers between devices: none -> 14.2 us  [the longest x6 14.2 us: gather_x(): lax.ppermute(value, 'x', [(i, (i + step) % 4) for i in range(4)])]
  transfers between devices with their start and end apart: 4 -> 12, of which waited for: 1 -> 6; matrix products, arithmetic and copies ran while one was open for 22% -> 20% of each run, Pallas kernels for 0% -> 0%
where the time goes in v1:
time: 217 us; the launch traced here: 216 us
  local copies, waits for them, and re-layouts  92.5 us (43%)
  other arithmetic  48.6 us (22%)
  starting transfers between devices  31.1 us (14%)
  waiting for transfers between devices  24.2 us (11%)
  matrix products  17.5 us (8%)
    transpose x1, other arithmetic, by_system(): pair.reshape(2, 4, -1, 2, 64).transpose(0, 3, 2, 1, 4)  27.5 us
    another operation x4, local copies, waits for them, and re-layouts, by_system(): jnp.stack([mine, theirs])  19.2 us
    dot_general x6, matrix products, complex_rows(): product = jnp.einsum(form, left, right, preferred_element_type=F32)  17.1 us
    slice x3, local copies, waits for them, and re-layouts, body(): total = total - complex_rows(trail_factor[s, 1], second_full[s])  15.2 us
    slice x3, local copies, waits for them, and re-layouts, body(): first_full[s]  14.7 us
    ppermute x6, waiting for transfers between devices, gather_x(): lax.ppermute(value, 'x', [(i, (i + step) % 4) for i in range(4)])  14.2 us
    transpose x1, local copies, waits for them, and re-layouts, by_system(): pair.reshape(2, 4, -1, 2, 64).transpose(0, 3, 2, 1, 4)  10.6 us
    unnamed x50, local copies, waits for them, and re-layouts  10.3 us
  transfers between devices with their start and end apart: 12, of which 6 were waited for; matrix products, arithmetic and copies ran while one was open for 20% of the time, Pallas kernels for 0%

profile of v1, /device:TPU:1, one launch (start us, length us, event | category | flops | bytes accessed | tf_op | source)
XLA Modules:
  0.0 215.5 jit_solution(6839202625625242475)
XLA Ops:
  10.1 10.2 %all-to-all-start = ((bf16[128,2,8,128]{3,2,1,0:T(8,128)(2,1)}), bf16[128,2,8,128]{3,2,1,0:T(8,128)(2,1)S(1)}, u32[]{:S(2)}, u32[]{:S(2)}) async-start(bf16[128,2,8,128]{3,2,1,0:T(8,128)(2,1)} %bitcast.35), calls=%async_computation | async-start | bytes 1048576 | tf_op jit(solution)/shard_map/all_to_all | solution.py:78
  21.8 2.6 %collective-permute-start.3 = (bf16[2,2,8,1280]{3,2,1,0:T(8,128)(2,1)S(1)}, bf16[2,2,8,1280]{3,2,1,0:T(8,128)(2,1)S(1)}, u32[]{:S(2)}, u32[]{:S(2)}) collective-permute-start(bf16[2,2,8,1280]{3,2,1,0:T(8,128)(2,1)S(1)} %maximum_select_fusion.1), channel_id=1, source_target_pairs={{0,96},{32,0},{64,32},{96,64},{1,97},{33,1},{65,33},{97,65},{2,98}... | collective-permute-start | bytes 245768 | tf_op jit(solution)/shard_map/ppermute | solution.py:33
  25.6 3.4 %collective-permute-done.3 = bf16[2,2,8,1280]{3,2,1,0:T(8,128)(2,1)S(1)} collective-permute-done((bf16[2,2,8,1280]{3,2,1,0:T(8,128)(2,1)S(1)}, bf16[2,2,8,1280]{3,2,1,0:T(8,128)(2,1)S(1)}, u32[]{:S(2)}, u32[]{:S(2)}) %collective-permute-start.3) | collective-permute-done | bytes 81952 | tf_op jit(solution)/shard_map/ppermute | solution.py:33
  30.6 1.9 collective-permute-done.1
  32.8 1.9 all-to-all-done
  36.1 5.2 %all-to-all-start.1 = ((bf16[16,72,128]{2,1,0:T(8,128)(2,1)}), bf16[16,72,128]{2,1,0:T(8,128)(2,1)S(1)}, u32[]{:S(2)}, u32[]{:S(2)}) async-start(bf16[16,72,128]{2,1,0:T(8,128)(2,1)} %broadcast_in_dim.60), calls=%async_computation.1 | async-start | bytes 589824 | tf_op jit(solution)/shard_map/all_to_all | solution.py:97
  41.3 8.2 %all-to-all-done.1 = bf16[16,72,128]{2,1,0:T(8,128)(2,1)S(1)} async-done(((bf16[16,72,128]{2,1,0:T(8,128)(2,1)}), bf16[16,72,128]{2,1,0:T(8,128)(2,1)S(1)}, u32[]{:S(2)}, u32[]{:S(2)}) %all-to-all-start.1) | async-done | bytes 294944 | tf_op jit(solution)/shard_map/all_to_all | solution.py:97
  50.6 1.8 collective-permute-start.7
  54.1 5.5 %all-to-all-start.2 = ((bf16[64,64,128]{2,1,0:T(8,128)(2,1)}), bf16[64,64,128]{2,1,0:T(8,128)(2,1)}, u32[]{:S(2)}, u32[]{:S(2)}) async-start(bf16[64,64,128]{2,1,0:T(8,128)(2,1)} %broadcast_in_dim.61), calls=%async_computation.2 | async-start | bytes 2097152 | tf_op jit(solution)/shard_map/all_to_all | solution.py:106
  59.7 7.3 %collective-permute-done.5 = bf16[1152,128]{1,0:T(8,128)(2,1)S(1)} collective-permute-done((bf16[1152,128]{1,0:T(8,128)(2,1)S(1)}, bf16[1152,128]{1,0:T(8,128)(2,1)S(1)}, u32[]{:S(2)}, u32[]{:S(2)}) %collective-permute-start.5) | collective-permute-done | bytes 294944 | tf_op jit(solution)/shard_map/ppermute | solution.py:33
  73.5 4.5 %copy.241 = bf16[1,4,1024,2,64]{4,3,2,1,0:T(2,128)(2,1)S(1)} copy(bf16[1,4,1024,2,64]{2,4,3,1,0:T(8,128)(2,1)} %bitcast.223) | data formatting | bytes 2097152 | tf_op jit(solution)/shard_map/stack | solution.py:113
  78.1 2.5 %copy.230 = bf16[4,8,16,8,128]{4,3,2,1,0:T(8,128)(2,1)} copy(bf16[4,8,16,8,128]{4,3,1,2,0:T(8,128)(2,1)} %bitcast.45) | data formatting | bytes 2097152 | tf_op jit(solution)/shard_map/transpose | solution.py:108
  80.6 5.0 %stack.181 = bf16[1,4,1024,2,64]{4,3,2,1,0:T(2,128)(2,1)} reshape(bf16[4,8,16,8,128]{4,3,2,1,0:T(8,128)(2,1)} %copy.230) | data formatting | bytes 2097152 | tf_op jit(solution)/shard_map/stack | solution.py:113
  88.3 2.3 %slice.373 = bf16[4,1024,128]{2,1,0:T(8,128)(2,1)} slice(bf16[4,1152,128]{2,1,0:T(8,128)(2,1)} %collective-permute-done.8), slice={[0:4], [0:1024], [0:128]} | slice | bytes 2097152 | tf_op jit(solution)/shard_map/slice | solution.py:116
  90.6 2.3 %copy.240 = bf16[4,1024,128]{1,2,0:T(8,128)(2,1)} copy(bf16[4,1024,128]{2,1,0:T(8,128)(2,1)} %slice.373) | data formatting | bytes 2097152 | tf_op jit(solution)/shard_map/slice | solution.py:116
  96.7 6.0 %copy.242 = bf16[1,4,1024,2,64]{4,3,2,1,0:T(2,128)(2,1)} copy(bf16[1,4,1024,2,64]{2,4,3,1,0:T(8,128)(2,1)} %bitcast.222) | data formatting | bytes 2097152 | tf_op jit(solution)/shard_map/stack | solution.py:113
  104.9 3.7 %copy.233 = bf16[1,4,1024,2,64]{4,3,2,1,0:T(2,128)(2,1)} copy(bf16[1,4,1024,2,64]{2,4,3,1,0:T(8,128)(2,1)S(1)} %bitcast.224) | data formatting | bytes 2097152 | tf_op jit(solution)/shard_map/stack | solution.py:113
  108.6 27.5 %fusion = (bf16[2,2,1024,4,64]{4,1,2,3,0:T(2,128)(2,1)}, bf16[2,2,1024,4,64]{4,1,2,3,0:T(2,128)(2,1)}) fusion(pred[]{:T(512)S(6)} %eq.32, bf16[1,4,1024,2,64]{4,3,2,1,0:T(2,128)(2,1)} %copy.233, bf16[1,4,1024,2,64]{4,3,2,1,0:T(2,128)(2,1)} %stack.181, bf16[1,4,1024,2,64]{4,3,2,1,0:T(2,128)(2,1)S(1)} %copy.241, bf16[1,4,1024,2,64]{4,3,2,1,0:T(2,128)(2,1)} %copy.242), kind=kLoop, calls=%fused_computation.3 | loop fusion | flops 6291456 | bytes 8388609 | tf_op jit(solution)/shard_map/transpose | solution.py:114
  136.1 10.6 %copy.235 = bf16[2,2,1024,4,64]{2,4,3,1,0:T(8,128)(2,1)} copy(bf16[2,2,1024,4,64]{4,1,2,3,0:T(2,128)(2,1)} %get-tuple-element.77) | data formatting | bytes 4194304 | tf_op jit(solution)/shard_map/transpose | solution.py:114
  146.7 5.8 %fusion.64 = (bf16[1,2,1024,4,64]{4,1,2,3,0:T(2,128)(2,1)}, bf16[1,2,1024,4,64]{4,1,2,3,0:T(2,128)(2,1)S(1)}) fusion(bf16[2,2,1024,4,64]{4,1,2,3,0:T(2,128)(2,1)} %get-tuple-element.77), kind=kLoop, calls=%fused_computation.150 | loop fusion | bytes 4194304 | tf_op jit(solution)/shard_map/slice | solution.py:122
  152.5 4.2 %fusion.65 = (bf16[1,2,1024,4,64]{4,1,2,3,0:T(2,128)(2,1)}, bf16[1,2,1024,4,64]{4,1,2,3,0:T(2,128)(2,1)}) fusion(bf16[2,2,1024,4,64]{4,1,2,3,0:T(2,128)(2,1)S(1)} %copy-done.2), kind=kLoop, calls=%fused_computation.151 | loop fusion | bytes 4194304 | tf_op jit(solution)/shard_map/slice | solution.py:121
  156.7 4.6 %copy.245 = bf16[1,2,1024,4,64]{2,4,3,1,0:T(8,128)(2,1)S(1)} copy(bf16[1,2,1024,4,64]{4,1,2,3,0:T(2,128)(2,1)} %get-tuple-element.31) | data formatting | bytes 2097152 | tf_op jit(solution)/shard_map/slice | solution.py:121
  161.3 5.9 %copy.248 = bf16[1,2,1024,4,64]{2,4,3,1,0:T(8,128)(2,1)} copy(bf16[1,2,1024,4,64]{4,1,2,3,0:T(2,128)(2,1)} %get-tuple-element.32) | data formatting | bytes 2097152 | tf_op jit(solution)/shard_map/slice | solution.py:121
  167.2 2.8 %convert_element_type.71 = f32[2,1024,256]{1,2,0:T(8,128)} convert(bf16[2,1024,256]{1,2,0:T(8,128)(2,1)} %bitcast.215) | non-fusion elementwise | flops 524288 | bytes 3145728 | tf_op jit(solution)/shard_map/convert_element_type | solution.py:139
  172.8 5.9 %copy.246 = bf16[1,2,1024,4,64]{2,4,3,1,0:T(8,128)(2,1)} copy(bf16[1,2,1024,4,64]{4,1,2,3,0:T(2,128)(2,1)} %get-tuple-element.27) | data formatting | bytes 2097152 | tf_op jit(solution)/shard_map/slice | solution.py:122
  178.7 3.5 %copy.249 = bf16[1,2,1024,4,64]{2,4,3,1,0:T(8,128)(2,1)} copy(bf16[1,2,1024,4,64]{4,1,2,3,0:T(2,128)(2,1)S(1)} %get-tuple-element.28) | data formatting | bytes 2097152 | tf_op jit(solution)/shard_map/slice | solution.py:122
  185.4 4.7 %fusion.23 = f32[2,2,1024,256]{2,3,0,1:T(8,128)S(1)} fusion(bf16[2,1024,256,1]{1,2,3,0:T(8,128)(2,1)S(1)} %bitcast.220, bf16[2,2,2,1024,1024]{4,3,2,1,0:T(8,128)(2,1)} %param.11), kind=kOutput, calls=%fused_computation.20 | convolution fusion | flops 2147483648 | bytes 9437184 | tf_op jit(solution)/shard_map/prn,qna->pqra/dot_general | solution.py:26
  190.7 4.7 %fusion.17 = f32[2,2,1024,256]{2,3,0,1:T(8,128)S(1)} fusion(bf16[2,1024,256,1]{1,2,3,0:T(8,128)(2,1)S(1)} %bitcast.218, bf16[2,2,2,1024,1024]{4,3,2,1,0:T(8,128)(2,1)} %param.11), kind=kOutput, calls=%fused_computation.18 | convolution fusion | flops 2147483648 | bytes 9437184 | tf_op jit(solution)/shard_map/prn,qna->pqra/dot_general | solution.py:26
  196.6 2.4 %fusion.20 = f32[2,2,1024,256]{2,3,0,1:T(8,128)S(1)} fusion(bf16[2,1024,256,1]{1,2,3,0:T(8,128)(2,1)S(1)} %bitcast.216, bf16[2,2,2,1024,1024]{4,3,2,1,0:T(8,128)(2,1)S(1)} %bitcast.246), kind=kOutput, calls=%fused_computation.19 | convolution fusion | flops 2147483648 | bytes 9437184 | tf_op jit(solution)/shard_map/prn,qna->pqra/dot_general | solution.py:26
  199.6 2.4 %fusion.14 = f32[2,2,1024,256]{2,3,0,1:T(8,128)S(1)} fusion(bf16[2,1024,256,1]{1,2,3,0:T(8,128)(2,1)S(1)} %bitcast.214, bf16[2,2,2,1024,1024]{4,3,2,1,0:T(8,128)(2,1)S(1)} %bitcast.246), kind=kOutput, calls=%fused_computation.17 | convolution fusion | flops 2147483648 | bytes 9437184 | tf_op jit(solution)/shard_map/prn,qna->pqra/dot_general | solution.py:26
  206.7 3.9 %copy.254 = bf16[2,2,1024,256]{3,2,1,0:T(8,128)(2,1)} copy(bf16[2,2,1024,256]{2,3,0,1:T(8,128)(2,1)} %pad_maximum_fusion) | data formatting | bytes 4194304
  210.6 2.8 %subtract_reduce_fusion.1 = (f32[1024]{0:T(1024)S(1)}, f32[1024]{0:T(1024)S(1)}) fusion(f32[2,1024,256]{1,2,0:T(8,128)} %convert_element_type.71, f32[2,1024,256]{1,2,0:T(8,128)} %convert_element_type.70), kind=kLoop, calls=%fused_computation.46 | loop fusion | flops 2095104 | bytes 4202496 | tf_op jit(solution)/shard_map/reduce_sum | solution.py:140
  (172 shorter events, 48.1 us)
Async XLA Ops:
  0.6 19.9 %copy-start = (s32[1024]{0:T(1024)S(1)}, s32[1024]{0:T(1024)}, u32[]{:S(2)}) copy-start(s32[1024]{0:T(1024)} %param.17) | copy-start | bytes 12292
  0.6 6.6 %copy-start.13 = (bf16[2,2,8,1024]{3,2,1,0:T(8,128)(2,1)S(1)}, bf16[2,2,8,1024]{3,2,1,0:T(8,128)(2,1)}, u32[]{:S(2)}) copy-start(bf16[2,2,8,1024]{3,2,1,0:T(8,128)(2,1)} %param.10) | copy-start | bytes 196612
  2.3 19.6 %collective-permute-start = (bf16[2,8,1280]{2,1,0:T(8,128)(2,1)S(1)}, bf16[2,8,1280]{2,1,0:T(8,128)(2,1)S(1)}, u32[]{:S(2)}, u32[]{:S(2)}) collective-permute-start(bf16[2,8,1280]{2,1,0:T(8,128)(2,1)S(1)} %get-tuple-element.61), channel_id=1, source_target_pairs={{0,16},{16,0},{1,17},{17,1},{2,18},{18,2},{3,19},{19,3},{4,20},{20... | collective-permute-start | bytes 122888 | tf_op jit(solution)/shard_map/ppermute | solution.py:39
  8.5 11.9 %copy-start.17 = (s32[2,8,3]{1,0,2:T(2,128)S(1)}, s32[2,8,3]{1,0,2:T(2,128)}, u32[]{:S(2)}) copy-start(s32[2,8,3]{1,0,2:T(2,128)} %param.16) | copy-start | bytes 580
  10.1 24.5 %all-to-all-start = ((bf16[128,2,8,128]{3,2,1,0:T(8,128)(2,1)}), bf16[128,2,8,128]{3,2,1,0:T(8,128)(2,1)S(1)}, u32[]{:S(2)}, u32[]{:S(2)}) async-start(bf16[128,2,8,128]{3,2,1,0:T(8,128)(2,1)} %bitcast.35), calls=%async_computation | async-start | bytes 1048576 | tf_op jit(solution)/shard_map/all_to_all | solution.py:78
  21.8 7.2 %collective-permute-start.3 = (bf16[2,2,8,1280]{3,2,1,0:T(8,128)(2,1)S(1)}, bf16[2,2,8,1280]{3,2,1,0:T(8,128)(2,1)S(1)}, u32[]{:S(2)}, u32[]{:S(2)}) collective-permute-start(bf16[2,2,8,1280]{3,2,1,0:T(8,128)(2,1)S(1)} %maximum_select_fusion.1), channel_id=1, source_target_pairs={{0,96},{32,0},{64,32},{96,64},{1,97},{33,1},{65,33},{97,65},{2,98}... | collective-permute-start | bytes 245768 | tf_op jit(solution)/shard_map/ppermute | solution.py:33
  24.5 6.1 %collective-permute-start.2 = (bf16[2,2,8,1280]{3,2,1,0:T(8,128)(2,1)S(1)}, bf16[2,2,8,1280]{3,2,1,0:T(8,128)(2,1)S(1)}, u32[]{:S(2)}, u32[]{:S(2)}) collective-permute-start(bf16[2,2,8,1280]{3,2,1,0:T(8,128)(2,1)S(1)} %maximum_select_fusion.1), channel_id=1, source_target_pairs={{0,64},{32,96},{64,0},{96,32},{1,65},{33,97},{65,1},{97,33},{2,66}... | collective-permute-start | bytes 245768 | tf_op jit(solution)/shard_map/ppermute | solution.py:33
  25.0 7.4 %collective-permute-start.1 = (bf16[2,2,8,1280]{3,2,1,0:T(8,128)(2,1)S(1)}, bf16[2,2,8,1280]{3,2,1,0:T(8,128)(2,1)S(1)}, u32[]{:S(2)}, u32[]{:S(2)}) collective-permute-start(bf16[2,2,8,1280]{3,2,1,0:T(8,128)(2,1)S(1)} %maximum_select_fusion.1), channel_id=1, source_target_pairs={{0,32},{32,64},{64,96},{96,0},{1,33},{33,65},{65,97},{97,1},{2,34}... | collective-permute-start | bytes 245768 | tf_op jit(solution)/shard_map/ppermute | solution.py:33
  36.1 13.4 %all-to-all-start.1 = ((bf16[16,72,128]{2,1,0:T(8,128)(2,1)}), bf16[16,72,128]{2,1,0:T(8,128)(2,1)S(1)}, u32[]{:S(2)}, u32[]{:S(2)}) async-start(bf16[16,72,128]{2,1,0:T(8,128)(2,1)} %broadcast_in_dim.60), calls=%async_computation.1 | async-start | bytes 589824 | tf_op jit(solution)/shard_map/all_to_all | solution.py:97
  49.6 10.1 %collective-permute-start.6 = (bf16[1152,128]{1,0:T(8,128)(2,1)S(1)}, bf16[1152,128]{1,0:T(8,128)(2,1)S(1)}, u32[]{:S(2)}, u32[]{:S(2)}) collective-permute-start(bf16[1152,128]{1,0:T(8,128)(2,1)S(1)} %get-tuple-element.55), channel_id=1, source_target_pairs={{0,64},{32,96},{64,0},{96,32},{1,65},{33,97},{65,1},{97,33},{2,66}... | collective-permute-start | bytes 884744 | tf_op jit(solution)/shard_map/ppermute | solution.py:33
  49.7 17.3 %collective-permute-start.5 = (bf16[1152,128]{1,0:T(8,128)(2,1)S(1)}, bf16[1152,128]{1,0:T(8,128)(2,1)S(1)}, u32[]{:S(2)}, u32[]{:S(2)}) collective-permute-start(bf16[1152,128]{1,0:T(8,128)(2,1)S(1)} %get-tuple-element.55), channel_id=1, source_target_pairs={{0,32},{32,64},{64,96},{96,0},{1,33},{33,65},{65,97},{97,1},{2,34}... | collective-permute-start | bytes 884744 | tf_op jit(solution)/shard_map/ppermute | solution.py:33
  50.6 16.4 %collective-permute-start.7 = (bf16[1152,128]{1,0:T(8,128)(2,1)S(1)}, bf16[1152,128]{1,0:T(8,128)(2,1)S(1)}, u32[]{:S(2)}, u32[]{:S(2)}) collective-permute-start(bf16[1152,128]{1,0:T(8,128)(2,1)S(1)} %get-tuple-element.55), channel_id=1, source_target_pairs={{0,96},{32,0},{64,32},{96,64},{1,97},{33,1},{65,33},{97,65},{2,98}... | collective-permute-start | bytes 884744 | tf_op jit(solution)/shard_map/ppermute | solution.py:33
  54.1 24.0 %all-to-all-start.2 = ((bf16[64,64,128]{2,1,0:T(8,128)(2,1)}), bf16[64,64,128]{2,1,0:T(8,128)(2,1)}, u32[]{:S(2)}, u32[]{:S(2)}) async-start(bf16[64,64,128]{2,1,0:T(8,128)(2,1)} %broadcast_in_dim.61), calls=%async_computation.2 | async-start | bytes 2097152 | tf_op jit(solution)/shard_map/all_to_all | solution.py:106
  67.1 1.6 copy-start.9
  67.4 19.2 %collective-permute-start.8 = (bf16[4,1152,128]{2,1,0:T(8,128)(2,1)S(1)}, bf16[4,1152,128]{2,1,0:T(8,128)(2,1)}, u32[]{:S(2)}, u32[]{:S(2)}) collective-permute-start(bf16[4,1152,128]{2,1,0:T(8,128)(2,1)S(1)} %pad_maximum_fusion.2), channel_id=1, source_target_pairs={{0,16},{16,0},{1,17},{17,1},{2,18},{18,2},{3,19},{19,3},{4,20},{20... | collective-permute-start | bytes 3538952 | tf_op jit(solution)/shard_map/ppermute | solution.py:39
  85.5 17.9 %collective-permute-start.4 = (bf16[4,1024,128]{2,1,0:T(8,128)(2,1)}, bf16[4,1024,128]{2,1,0:T(8,128)(2,1)}, u32[]{:S(2)}, u32[]{:S(2)}) collective-permute-start(bf16[4,1024,128]{2,1,0:T(8,128)(2,1)} %bitcast.221), channel_id=1, source_target_pairs={{0,16},{16,0},{1,17},{17,1},{2,18},{18,2},{3,19},{19,3},{4,20},{20... | collective-permute-start | bytes 3145736 | tf_op jit(solution)/shard_map/ppermute | solution.py:39
  146.7 5.8 %copy-start.2 = (bf16[2,2,1024,4,64]{4,1,2,3,0:T(2,128)(2,1)S(1)}, bf16[2,2,1024,4,64]{4,1,2,3,0:T(2,128)(2,1)}, u32[]{:S(2)}) copy-start(bf16[2,2,1024,4,64]{4,1,2,3,0:T(2,128)(2,1)} %get-tuple-element.78) | copy-start | bytes 6291460
  182.2 1.6 copy-start.5
  183.7 1.6 copy-start.6
  185.4 10.6 %slice-start = ((s8[16777216]{0:T(1024)(128)(4,1)}), s8[4194304]{0:T(1024)(128)(4,1)S(1)}, s32[]{:S(2)}) async-start(s8[16777216]{0:T(1024)(128)(4,1)} %bitcast.245), calls=%async_computation.3 | async-start | bytes 8388608
  185.4 10.6 %slice-start.1 = ((s8[16777216]{0:T(1024)(128)(4,1)}), s8[4194304]{0:T(1024)(128)(4,1)S(1)}, s32[]{:S(2)}) async-start(s8[16777216]{0:T(1024)(128)(4,1)} %bitcast.245), calls=%async_computation.4 | async-start | bytes 8388608
  190.7 5.3 %slice-start.2 = ((s8[16777216]{0:T(1024)(128)(4,1)}), s8[4194304]{0:T(1024)(128)(4,1)S(1)}, s32[]{:S(2)}) async-start(s8[16777216]{0:T(1024)(128)(4,1)} %bitcast.245), calls=%async_computation.5 | async-start | bytes 8388608
  190.7 5.3 %slice-start.3 = ((s8[16777216]{0:T(1024)(128)(4,1)}), s8[4194304]{0:T(1024)(128)(4,1)S(1)}, s32[]{:S(2)}) async-start(s8[16777216]{0:T(1024)(128)(4,1)} %bitcast.245), calls=%async_computation.6 | async-start | bytes 8388608
  195.4 1.2 copy-start.4
  201.9 1.2 copy-start.8
  210.6 2.8 %copy-start.10 = (f32[1024,3,3]{0,2,1:T(4,128)S(1)}, f32[1024,3,3]{0,2,1:T(4,128)}, u32[]{:S(2)}) copy-start(f32[1024,3,3]{0,2,1:T(4,128)} %squeeze.143) | copy-start | bytes 110596
  210.6 2.8 %copy-start.11 = (f32[1024,3,3]{0,2,1:T(4,128)S(1)}, f32[1024,3,3]{0,2,1:T(4,128)}, u32[]{:S(2)}) copy-start(f32[1024,3,3]{0,2,1:T(4,128)} %squeeze.142) | copy-start | bytes 110596
  210.6 2.9 %copy-start.12 = (pred[1024,3,8]{0,2,1:T(8,128)(4,1)S(1)}, pred[1024,3,8]{0,2,1:T(8,128)(4,1)}, u32[]{:S(2)}) copy-start(pred[1024,3,8]{0,2,1:T(8,128)(4,1)} %get-tuple-element.69) | copy-start | bytes 73732
  210.6 3.0 %copy-start.3 = (f32[2,1024,256]{1,2,0:T(8,128)S(1)}, f32[2,1024,256]{1,2,0:T(8,128)}, u32[]{:S(2)}) copy-start(f32[2,1024,256]{1,2,0:T(8,128)} %convert_element_type.72) | copy-start | bytes 6291460
  213.5 2.0 copy-start.1
  213.6 1.3 copy-start.14
  213.6 1.3 copy-start.15
  (2 other events, 2.1 us)

commit v2 on v1

v2 whole, which is shorter than its diff:
```python
import jax
import jax.numpy as jnp
import numpy as np
from jax import lax
from jax.experimental import pallas as pl
from jax.experimental.pallas import tpu as pltpu
from jax.sharding import Mesh
from jax.sharding import PartitionSpec as P

ALL = ("x", "core", "col")
F32 = jnp.float32
BF16 = jnp.bfloat16
VMEM_LIMIT = 48 * 1024 * 1024


def lanes_below(shape, bound):
    return lax.broadcasted_iota(jnp.int32, shape, len(shape) - 1) < bound


def pair_lanes(left, right):
    low = lanes_below(left.shape, 64)
    real = jnp.where(low, left, pltpu.roll(right, 64, 1))
    imag = jnp.where(low, pltpu.roll(left, 64, 1), right)
    return real, imag


def fold_parts(top, low):
    turned = pltpu.roll(low, 64, 1)
    return top + jnp.where(lanes_below(low.shape, 64), -turned, turned)


def prepare_kernel(place, inverse, rhs, below, own_rhs, first, send, own, give):
    system = pl.program_id(0)
    left = jnp.concatenate([inverse[0, 0, 0].astype(F32), inverse[0, 0, 1].astype(F32)]).astype(BF16)
    by_real = jnp.dot(left, rhs[0, 0], preferred_element_type=F32)
    by_imag = jnp.dot(left, rhs[0, 1], preferred_element_type=F32)
    real = (by_real[:8] - by_imag[8:]).astype(BF16)
    imag = (by_imag[:8] + by_real[8:]).astype(BF16)
    first[0, 0] = real
    first[0, 1] = imag
    real = real.astype(F32)
    imag = imag.astype(F32)
    for half in range(2):
        cut = slice(128 * half, 128 * half + 128)
        even, odd = pair_lanes(real[:, cut], imag[:, cut])
        for group, value in ((2 * half, even), (2 * half + 1, odd)):
            value = value.astype(BF16)
            for col in range(16):
                send[group, 0, col, 0] = value
    lane_block = lax.broadcasted_iota(jnp.int32, (8, 128), 1) // 8
    pieces = [
        below[0, part, :, 128 * row : 128 * row + 128].astype(F32)
        for part in range(2)
        for row in range(8)
    ]
    for col in range(16):
        value = pltpu.roll(pieces[0], (128 - 8 * col) % 128, 1)
        for block in range(1, 16):
            turned = pltpu.roll(pieces[block], (8 * block - 8 * col) % 128, 1)
            value = jnp.where(lane_block == block, turned, value)
        value = value.astype(BF16)
        for group in range(4):
            send[group, 0, col, 1] = value

    def fill(target):
        for part in range(2):
            target[part, :, :1024] = inverse[0, 1, part]
            target[part, :, 1024:] = own_rhs[0, part]

    @pl.when(system == place[1])
    def _():
        fill(own)

    @pl.when(system != place[1])
    def _():
        fill(give)


def prepare(place, panel_inverse, first_rhs, panel_below, second_rhs):
    return pl.pallas_call(
        prepare_kernel,
        grid_spec=pltpu.PrefetchScalarGridSpec(
            num_scalar_prefetch=1,
            grid=(2,),
            in_specs=[
                pl.BlockSpec((1, 2, 2, 8, 1024), lambda s, _: (s, 0, 0, 0, 0)),
                pl.BlockSpec((1, 2, 1024, 256), lambda s, _: (s, 0, 0, 0)),
                pl.BlockSpec((1, 2, 8, 1024), lambda s, _: (s, 0, 0, 0)),
                pl.BlockSpec((1, 2, 8, 256), lambda s, _: (s, 0, 0, 0)),
            ],
            out_specs=[
                pl.BlockSpec((1, 2, 8, 256), lambda s, _: (s, 0, 0, 0)),
                pl.BlockSpec((4, 1, 16, 2, 8, 128), lambda s, _: (0, s, 0, 0, 0, 0)),
                pl.BlockSpec((2, 8, 1280), lambda s, _: (0, 0, 0)),
                pl.BlockSpec((2, 8, 1280), lambda s, _: (0, 0, 0)),
            ],
        ),
        out_shape=[
            jax.ShapeDtypeStruct((2, 2, 8, 256), BF16),
            jax.ShapeDtypeStruct((4, 2, 16, 2, 8, 128), BF16),
            jax.ShapeDtypeStruct((2, 8, 1280), BF16),
            jax.ShapeDtypeStruct((2, 8, 1280), BF16),
        ],
        name="prepare",
    )(place, panel_inverse, first_rhs, panel_below, second_rhs)


def right_kernel(place, received, rows0, rows1, rows2, rows3, tile, block, send, offset):
    x = place[0]
    half = pl.multiple_of(1024 + 128 * (x // 2), 128)
    odd = x % 2 == 1
    for step, rows in enumerate((rows0, rows1, rows2, rows3)):
        source = lax.rem(x - step + 4, 4)
        for core in range(2):
            real = rows[core, 0, :, pl.ds(half, 128)].astype(F32)
            imag = rows[core, 1, :, pl.ds(half, 128)].astype(F32)
            even_pair, odd_pair = pair_lanes(real, imag)
            value = jnp.where(odd, odd_pair, even_pair)
            offset[pl.ds(pl.multiple_of(16 * source + 8 * core, 8), 8), :] = value
    first = received[:, 0].astype(F32).reshape(1024, 128).astype(BF16)
    below = received[:, 1].astype(F32).reshape(1024, 128).astype(BF16)
    block[...] = first
    product = lax.dot_general(below, first, (((0,), (0,)), ((), ())), preferred_element_type=F32)
    right = (offset[...] - fold_parts(product[:64], product[64:])).astype(BF16)
    for col in range(16):
        send[col, :64] = right
        send[col, 64:] = tile[...]


def right_side(place, received, rows, tile):
    return pl.pallas_call(
        right_kernel,
        grid_spec=pltpu.PrefetchScalarGridSpec(
            num_scalar_prefetch=1,
            grid=(1,),
            in_specs=[pl.BlockSpec((128, 2, 8, 128), lambda i, _: (0, 0, 0, 0))]
            + [pl.BlockSpec((2, 2, 8, 1280), lambda i, _: (0, 0, 0, 0))] * 4
            + [pl.BlockSpec((8, 128), lambda i, _: (0, 0))],
            out_specs=[
                pl.BlockSpec((1024, 128), lambda i, _: (0, 0)),
                pl.BlockSpec((16, 72, 128), lambda i, _: (0, 0, 0)),
            ],
            scratch_shapes=[pltpu.VMEM((64, 128), F32)],
        ),
        out_shape=[
            jax.ShapeDtypeStruct((1024, 128), BF16),
            jax.ShapeDtypeStruct((16, 72, 128), BF16),
        ],
        name="right_side",
    )(place, received, *rows, tile)


def second_kernel(place, received, rows0, rows1, rows2, rows3, tiles, send):
    x = place[0]
    right = received[:, :64].astype(F32).reshape(16, 8, 8, 128)
    right = right.transpose(1, 0, 2, 3).reshape(1024, 128).astype(BF16)
    pieces = [
        rows[core, part, :, :1024].astype(F32)
        for part in range(2)
        for rows in (rows0, rows1, rows2, rows3)
        for core in range(2)
    ]
    left = jnp.concatenate(pieces).astype(BF16)
    product = jnp.dot(left, right, preferred_element_type=F32)
    value = fold_parts(product[:64], product[64:]).astype(BF16)
    for step in range(4):
        target = pl.multiple_of(16 * lax.rem(x - step + 4, 4), 16)
        part = value[16 * step : 16 * step + 16]
        for copy in range(64):
            send[copy, pl.ds(target, 16), :] = part
    tiles[...] = received[:, 64:].astype(F32).reshape(128, 128).astype(BF16)


def second_rows(place, received, rows):
    return pl.pallas_call(
        second_kernel,
        grid_spec=pltpu.PrefetchScalarGridSpec(
            num_scalar_prefetch=1,
            grid=(1,),
            in_specs=[pl.BlockSpec((16, 72, 128), lambda i, _: (0, 0, 0))]
            + [pl.BlockSpec((2, 2, 8, 1280), lambda i, _: (0, 0, 0, 0))] * 4,
            out_specs=[
                pl.BlockSpec((128, 128), lambda i, _: (0, 0)),
                pl.BlockSpec((64, 64, 128), lambda i, _: (0, 0, 0)),
            ],
        ),
        out_shape=[
            jax.ShapeDtypeStruct((128, 128), BF16),
            jax.ShapeDtypeStruct((64, 64, 128), BF16),
        ],
        name="second_rows",
    )(place, received, *rows)


def store_weights(weights, at, real_pairs):
    for half, (left, right) in enumerate(real_pairs):
        real, imag = pair_lanes(left, right)
        lane = 128 * half
        weights[pl.ds(at, 128), lane : lane + 128] = real.astype(BF16)
        weights[pl.ds(at, 128), 256 + lane : 384 + lane] = imag.astype(BF16)
        weights[pl.ds(at + 1024, 128), lane : lane + 128] = (-imag).astype(BF16)
        weights[pl.ds(at + 1024, 128), 256 + lane : 384 + lane] = real.astype(BF16)


def trail_product(factor, weights):
    total = jnp.dot(factor[0, 0, 0], weights[:1024], preferred_element_type=F32)
    return total + jnp.dot(factor[0, 0, 1], weights[1024:], preferred_element_type=F32)


def trail_first_kernel(place, b0, b1, b2, b3, c0, c1, c2, c3, factor, rhs, out, ordered, weights):
    x = place[0]
    turn = pl.program_id(0)

    def build(blocks):
        for step, block in enumerate(blocks):
            ordered[lax.rem(x - step + 4, 4)] = block[...]

        def chunk(row, carry):
            at = pl.multiple_of(128 * row, 128)
            parts = [ordered[q, pl.ds(at, 128), :].astype(F32) for q in range(4)]
            store_weights(weights, at, ((parts[0], parts[1]), (parts[2], parts[3])))
            return carry

        lax.fori_loop(0, 8, chunk, 0)

    @pl.when((turn == 0) & (pl.program_id(1) == 0))
    def _():
        build((b0, b1, b2, b3))

    @pl.when((turn == 1) & (pl.program_id(1) == 0))
    def _():
        build((c0, c1, c2, c3))

    total = trail_product(factor, weights)
    out[0, 0] = rhs[0, 0].astype(F32) - total[:, :256]
    out[0, 1] = rhs[0, 1].astype(F32) - total[:, 256:]


def trail_first(place, blocks, trail_factor, trail_rhs):
    rows = trail_rhs.shape[2]
    height = min(256, rows)
    system = lambda turn, p: jnp.where(turn == 0, p[1], 1 - p[1])
    return pl.pallas_call(
        trail_first_kernel,
        grid_spec=pltpu.PrefetchScalarGridSpec(
            num_scalar_prefetch=1,
            grid=(2, rows // height),
            in_specs=[pl.BlockSpec((1024, 128), lambda t, i, p: (0, 0))] * 8
            + [
                pl.BlockSpec((1, 1, 2, height, 1024), lambda t, i, p: (system(t, p), 0, 0, i, 0)),
                pl.BlockSpec((1, 2, height, 256), lambda t, i, p: (system(t, p), 0, i, 0)),
            ],
            out_specs=pl.BlockSpec((1, 2, height, 256), lambda t, i, p: (system(t, p), 0, i, 0)),
            scratch_shapes=[pltpu.VMEM((4, 1024, 128), BF16), pltpu.VMEM((2048, 512), BF16)],
        ),
        out_shape=jax.ShapeDtypeStruct((2, 2, rows, 256), F32),
        compiler_params=pltpu.CompilerParams(vmem_limit_bytes=VMEM_LIMIT),
        name="trail_first",
    )(place, *blocks, trail_factor, trail_rhs)


def trail_second_kernel(place, blocks, factor, partial, *refs):
    out, own, weights = refs[-3:]

    @pl.when(pl.program_id(0) == 0)
    def _():
        def chunk(row, carry):
            at = pl.multiple_of(128 * row, 128)
            near = pl.multiple_of(8 * row, 8)
            parts = [
                blocks[q, :, pl.ds(near, 8), :].astype(F32).reshape(128, 128) for q in range(4)
            ]
            store_weights(weights, at, ((parts[0], parts[1]), (parts[2], parts[3])))
            return carry

        lax.fori_loop(0, 8, chunk, 0)
        near = pl.multiple_of(8 * place[3], 8)
        parts = [blocks[q, place[4], pl.ds(near, 8), :].astype(F32) for q in range(4)]
        for half in range(2):
            real, imag = pair_lanes(parts[2 * half], parts[2 * half + 1])
            own[0, :, 128 * half : 128 * half + 128] = real.astype(BF16)
            own[1, :, 128 * half : 128 * half + 128] = imag.astype(BF16)

    total = trail_product(factor, weights)
    out[0, 0] = (partial[0, 0] - total[:, :256]).astype(BF16)
    out[0, 1] = (partial[0, 1] - total[:, 256:]).astype(BF16)


def trail_second(place, which, blocks, trail_factor, partial, previous=None):
    rows = partial.shape[2]
    height = min(256, rows)
    place = jnp.concatenate([place[:2], which[None], place[2:]])
    extra = () if previous is None else (previous,)
    return pl.pallas_call(
        trail_second_kernel,
        grid_spec=pltpu.PrefetchScalarGridSpec(
            num_scalar_prefetch=1,
            grid=(rows // height,),
            in_specs=[
                pl.BlockSpec((4, 16, 64, 128), lambda i, p: (0, 0, 0, 0)),
                pl.BlockSpec((1, 1, 2, height, 1024), lambda i, p: (p[2], 1, 0, i, 0)),
                pl.BlockSpec((1, 2, height, 256), lambda i, p: (p[2], 0, i, 0)),
            ]
            + [pl.BlockSpec(memory_space=pl.ANY)] * len(extra),
            out_specs=[
                pl.BlockSpec((1, 2, height, 256), lambda i, p: (p[2], 0, i, 0)),
                pl.BlockSpec((2, 8, 256), lambda i, p: (0, 0, 0)),
            ],
            scratch_shapes=[pltpu.VMEM((2048, 512), BF16)],
        ),
        out_shape=[
            jax.ShapeDtypeStruct((2, 2, rows, 256), BF16),
            jax.ShapeDtypeStruct((2, 8, 256), BF16),
        ],
        input_output_aliases={4: 0} if extra else {},
        compiler_params=pltpu.CompilerParams(vmem_limit_bytes=VMEM_LIMIT),
        name="trail_second",
    )(place, blocks, trail_factor, partial, *extra)


def spread_matrix(panel):
    spread = np.zeros((128, 3, 128), np.float32)
    for corner in range(3):
        for coordinate in range(3):
            lanes = slice(24 * corner + 8 * coordinate, 24 * corner + 8 * coordinate + 8)
            for part in range(2):
                source = 18 * part + 9 * panel + 3 * corner + coordinate
                for term in range(3):
                    spread[36 * term + source, part, lanes] = 1.0
            spread[108 + 3 * panel + corner, 2, lanes] = 32.0
            spread[114 + 3 * panel + corner, 2, lanes] = 1.0
    return jnp.asarray(spread.reshape(128, 384), BF16)


def gradient_sum(place, couple, tile_refs, spread, chunk_of):
    base = 8 * (16 * place[2] + place[3])
    target = (base + lax.rem(lax.broadcasted_iota(jnp.int32, (128, 128), 1), 8)).astype(F32)
    sign = jnp.where(lanes_below((128, 128), 64), 1.0, -1.0)
    total = jnp.zeros((8, 128), F32)
    for step in range(4):
        source = lax.rem(place[0] - step + 4, 4)
        for side in range(2):
            core = place[1] if side == 0 else 1 - place[1]
            same, crossed = couple(2 * source + core)
            real = jnp.sum(same * sign, axis=1, keepdims=True)
            imag = jnp.sum(crossed, axis=1, keepdims=True)
            table = jnp.dot(tile_refs[4 * side + step][...], spread[...], preferred_element_type=F32)
            value = table[:, 128:256] * imag - table[:, :128] * real
            value = jnp.where(table[:, 256:] == target, value, 0.0)
            total = total + jnp.sum(value.reshape(16, 8, 128), axis=0)
    return total


def couple_pairs(pairs):
    same = jnp.zeros((128, 128), F32)
    crossed = jnp.zeros((128, 128), F32)
    for mine, theirs in pairs:
        same = same + mine * theirs
        crossed = crossed + mine * pltpu.roll(theirs, 64, 1)
    return same, crossed


def gradient_first_kernel(place, *refs):
    blocks, tiles, spread, out = refs[:8], refs[8:16], refs[16], refs[17]

    def couple(row):
        at = pl.multiple_of(128 * row, 128)
        return couple_pairs(
            (blocks[q][pl.ds(at, 128), :].astype(F32), blocks[4 + q][pl.ds(at, 128), :].astype(F32))
            for q in range(4)
        )

    out[...] = gradient_sum(place, couple, tiles, spread, None)


def gradient_first(place, blocks, tiles, spread):
    return pl.pallas_call(
        gradient_first_kernel,
        grid_spec=pltpu.PrefetchScalarGridSpec(
            num_scalar_prefetch=1,
            grid=(1,),
            in_specs=[pl.BlockSpec((1024, 128), lambda i, p: (0, 0))] * 8
            + [pl.BlockSpec((128, 128), lambda i, p: (0, 0))] * 8
            + [pl.BlockSpec((128, 384), lambda i, p: (0, 0))],
            out_specs=pl.BlockSpec((8, 128), lambda i, p: (0, 0)),
        ),
        out_shape=jax.ShapeDtypeStruct((8, 128), F32),
        compiler_params=pltpu.CompilerParams(vmem_limit_bytes=VMEM_LIMIT),
        name="gradient_first",
    )(place, *blocks, *tiles, spread)


def gradient_second_kernel(place, mine, theirs, *refs):
    tiles, spread, before, out = refs[:8], refs[8], refs[9], refs[10]

    def couple(row):
        near = pl.multiple_of(8 * row, 8)
        return couple_pairs(
            (
                mine[q, :, pl.ds(near, 8), :].astype(F32).reshape(128, 128),
                theirs[q, :, pl.ds(near, 8), :].astype(F32).reshape(128, 128),
            )
            for q in range(4)
        )

    total = before[...] + gradient_sum(place, couple, tiles, spread, None)
    total = jnp.sum(total, axis=0, keepdims=True)
    total = total + pltpu.roll(total, 104, 1) + pltpu.roll(total, 80, 1)
    for coordinate in range(3):
        out[coordinate : coordinate + 1, :] = total[:, 8 * coordinate : 8 * coordinate + 8]


def gradient_second(place, mine, theirs, tiles, spread, before):
    return pl.pallas_call(
        gradient_second_kernel,
        grid_spec=pltpu.PrefetchScalarGridSpec(
            num_scalar_prefetch=1,
            grid=(1,),
            in_specs=[pl.BlockSpec((4, 16, 64, 128), lambda i, p: (0, 0, 0, 0))] * 2
            + [pl.BlockSpec((128, 128), lambda i, p: (0, 0))] * 8
            + [
                pl.BlockSpec((128, 384), lambda i, p: (0, 0)),
                pl.BlockSpec((8, 128), lambda i, p: (0, 0)),
            ],
            out_specs=pl.BlockSpec((3, 8), lambda i, p: (0, 0)),
        ),
        out_shape=jax.ShapeDtypeStruct((3, 8), F32),
        compiler_params=pltpu.CompilerParams(vmem_limit_bytes=VMEM_LIMIT),
        name="gradient_second",
    )(place, mine, theirs, *tiles, spread, before)


def rounds_x(value):
    sent = [lax.ppermute(value, "x", [(i, (i + step) % 4) for i in range(4)]) for step in (1, 2, 3)]
    return [value, *sent]


def swap_core(value):
    return lax.ppermute(value, "core", [(0, 1), (1, 0)])


def element_tile(shape_tiles, element_vertices, vertex_slot):
    values = shape_tiles.transpose(3, 0, 2, 1).reshape(8, 36)
    high = lax.reduce_precision(values, 8, 7)
    rest = values - high
    mid = lax.reduce_precision(rest, 8, 7)
    low = rest - mid
    slots = vertex_slot[element_vertices].transpose(1, 0, 2).reshape(8, 6)
    parts = [high, mid, low, (slots // 32).astype(F32), (slots % 32).astype(F32), jnp.zeros((8, 8), F32)]
    return jnp.concatenate(parts, axis=1).astype(BF16)


def body(
    panel_inverse,
    panel_below,
    trail_factor,
    first_rhs,
    second_rhs,
    trail_rhs,
    shape_tiles,
    element_vertices,
    vertex_slot,
):
    x = lax.axis_index("x")
    core = lax.axis_index("core")
    col = lax.axis_index("col")
    place = jnp.stack([x, core, 2 * x + core, col]).astype(jnp.int32)

    first, send, own, give = prepare(place, panel_inverse, first_rhs, panel_below, second_rhs)
    received = lax.all_to_all(send.reshape(128, 2, 8, 128), ALL, 0, 0, tiled=True)

    other = swap_core(give)
    chip = jnp.where(core == 0, jnp.stack([own, other]), jnp.stack([other, own]))
    rows = rounds_x(chip)
    tile = element_tile(shape_tiles, element_vertices, vertex_slot)

    first_block, send = right_side(place, received, rows, tile)
    received = lax.all_to_all(send, "col", 0, 0, tiled=True)
    first_mine = rounds_x(first_block)
    first_theirs = [swap_core(block) for block in first_mine]

    tiles, send = second_rows(place, received, rows)
    second_mine = lax.all_to_all(send, ("x", "col"), 0, 0, tiled=True)

    tiles_mine = rounds_x(tiles)
    tiles_all = tiles_mine + [swap_core(block) for block in tiles_mine]
    partial = trail_first(place, first_mine + first_theirs, trail_factor, trail_rhs)
    gradient = gradient_first(place, first_mine + first_theirs, tiles_all, spread_matrix(0))

    second_theirs = swap_core(second_mine)
    mine = second_mine.reshape(4, 16, 64, 128)
    theirs = second_theirs.reshape(4, 16, 64, 128)
    update, own_mine = trail_second(place, core, mine, trail_factor, partial)
    update, own_theirs = trail_second(place, 1 - core, theirs, trail_factor, partial, update)
    gradient = gradient_second(place, mine, theirs, tiles_all, spread_matrix(1), gradient)

    second = jnp.where(
        core == 0, jnp.stack([own_mine, own_theirs]), jnp.stack([own_theirs, own_mine])
    )
    return (jnp.stack([first, second], axis=1), update, gradient)


def solution(mesh):
    fine = Mesh(mesh.devices.reshape(4, 2, 16), ALL)
    return jax.shard_map(
        body,
        mesh=fine,
        in_specs=(
            P(None, None, None, ALL, None),
            P(None, None, ALL, None),
            P(None, None, None, ALL, None),
            P(),
            P(None, None, ALL, None),
            P(None, None, ALL, None),
            P(None, None, None, ALL),
            P(None, ALL, None),
            P(),
        ),
        out_specs=(
            P(None, None, None, ALL, None),
            P(None, None, ALL, None),
            P(None, ALL),
        ),
        check_vma=False,
    )
```

time: 217 us -> 151 us (0.70)
  local copies, waits for them, and re-layouts: 92.5 us -> 11.6 us
  other arithmetic: 48.6 us -> 1.29 us
  Pallas kernels: 0 us -> 42.3 us
  blocking collectives: 0 us -> 35.3 us
  matrix products: 17.5 us -> 0 us
  waiting for transfers between devices: 24.2 us -> 27.8 us
    pallas_call x0 -> x8, Pallas kernels: none -> 42.3 us  [the longest x2 14.4 us: trail_second(): pl.pallas_call(trail_second_kernel, grid_spec=pltpu.PrefetchScalarGridSpe...]
    slice x14 -> x0, local copies, waits for them, and re-layouts: 37.1 us -> none  [the longest x3 15.2 us: body(): total = total - complex_rows(trail_factor[s, 1], second_full[s])]
    all_to_all x0 -> x2, blocking collectives: none -> 35.3 us  [the longest x1 21 us: body(): second_mine = lax.all_to_all(send, ('x', 'col'), 0, 0, tiled=True)]
    transpose x3 -> x0, other arithmetic: 27.6 us -> none  [the longest x1 27.5 us: by_system(): pair.reshape(2, 4, -1, 2, 64).transpose(0, 3, 2, 1, 4)]
    another operation x10 -> x0, local copies, waits for them, and re-layouts: 20.5 us -> none  [the longest x4 19.2 us: by_system(): jnp.stack([mine, theirs])]
    dot_general x8 -> x0, matrix products: 17.5 us -> none  [the longest x6 17.1 us: complex_rows(): product = jnp.einsum(form, left, right, preferred_element_type=F32)]
    transpose x6 -> x0, local copies, waits for them, and re-layouts: 13.6 us -> none  [the longest x1 10.6 us: by_system(): pair.reshape(2, 4, -1, 2, 64).transpose(0, 3, 2, 1, 4)]
    ppermute x6 -> x9, waiting for transfers between devices: 14.2 us -> 25.9 us  [rounds_x(): lax.ppermute(value, 'x', [(i, (i + step) % 4) for i in range(4)])]
  transfers between devices with their start and end apart: 12 -> 20, of which waited for: 6 -> 10; matrix products, arithmetic and copies ran while one was open for 20% -> 1% of each run, Pallas kernels for 0% -> 15%
where the time goes in v2:
time: 151 us; the launch traced here: 150 us
  Pallas kernels  42.3 us (28%)
  blocking collectives  35.3 us (23%)
  starting transfers between devices  30.9 us (20%)
  waiting for transfers between devices  27.8 us (18%)
  local copies, waits for them, and re-layouts  11.6 us (8%)
    ppermute x9, waiting for transfers between devices, rounds_x(): lax.ppermute(value, 'x', [(i, (i + step) % 4) for i in range(4)])  25.9 us
    all_to_all x1, blocking collectives, body(): second_mine = lax.all_to_all(send, ('x', 'col'), 0, 0, tiled=True)  21 us
    pallas_call x2, Pallas kernels, trail_second(): pl.pallas_call(trail_second_kernel, grid_spec=pltpu.PrefetchScalarGridSpe...  14.4 us
    all_to_all x1, blocking collectives, body(): received = lax.all_to_all(send, 'col', 0, 0, tiled=True)  14.3 us
    ppermute x10, starting transfers between devices, swap_core(): return lax.ppermute(value, 'core', [(0, 1), (1, 0)])  12.8 us
    pallas_call x1, Pallas kernels, trail_first(): pl.pallas_call(trail_first_kernel, grid_spec=pltpu.PrefetchScalarGridSpec...  12.7 us
    all_to_all x1, starting transfers between devices, body(): lax.all_to_all(send.reshape(128, 2, 8, 128), ALL, 0, 0, tiled=True)  11.5 us
    unnamed x50, local copies, waits for them, and re-layouts  9.59 us
  transfers between devices with their start and end apart: 20, of which 10 were waited for; matrix products, arithmetic and copies ran while one was open for 1% of the time, Pallas kernels for 15%

profile of v2, /device:TPU:1, one launch (start us, length us, event | category | flops | bytes accessed | tf_op | source)
XLA Modules:
  0.0 150.0 jit_solution(11673118942414521388)
XLA Ops:
  1.3 3.4 %prepare.1 = (bf16[2,2,8,256]{3,2,1,0:T(8,128)(2,1)}, bf16[4,2,16,2,8,128]{5,4,3,2,1,0:T(8,128)(2,1)}, bf16[2,8,1280]{2,1,0:T(8,128)(2,1)}, bf16[2,8,1280]{2,1,0:T(8,128)(2,1)}) custom-call(s32[4]{0:T(128)} %pad_add_fusion.place, bf16[2,2,2,8,1024]{4,3,2,1,0:T(8,128)(2,1)} %inverse.1, bf16[2,2,1024,256]{3,2,1,0:T(8,128)(2,1)} %rhs.2, ...), custom_call_target="tpu_custom_call" | custom-call | tf_op jit(solution)/shard_map/prepare/pallas_call | solution.py:80
  4.7 11.5 %all-to-all-start = ((bf16[128,2,8,128]{3,2,1,0:T(8,128)(2,1)}), bf16[128,2,8,128]{3,2,1,0:T(8,128)(2,1)S(1)}, u32[]{:S(2)}, u32[]{:S(2)}) async-start(bf16[128,2,8,128]{3,2,1,0:T(8,128)(2,1)} %bitcast.21), calls=%async_computation | async-start | bytes 1048576 | tf_op jit(solution)/shard_map/all_to_all | solution.py:470
  16.2 1.1 collective-permute-start
  18.6 2.0 %collective-permute-start.3 = (bf16[2,2,8,1280]{3,2,1,0:T(8,128)(2,1)S(1)}, bf16[2,2,8,1280]{3,2,1,0:T(8,128)(2,1)S(1)}, u32[]{:S(2)}, u32[]{:S(2)}) collective-permute-start(bf16[2,2,8,1280]{3,2,1,0:T(8,128)(2,1)S(1)} %maximum_select_fusion.rows0), channel_id=1, source_target_pairs={{0,96},{32,0},{64,32},{96,64},{1,97},{33,1},{65,33},{97,65},{2,98}... | collective-permute-start | bytes 245768 | tf_op jit(solution)/shard_map/ppermute | solution.py:434
  22.4 2.5 %collective-permute-done.3.rows3 = bf16[2,2,8,1280]{3,2,1,0:T(8,128)(2,1)S(1)} collective-permute-done((bf16[2,2,8,1280]{3,2,1,0:T(8,128)(2,1)S(1)}, bf16[2,2,8,1280]{3,2,1,0:T(8,128)(2,1)S(1)}, u32[]{:S(2)}, u32[]{:S(2)}) %collective-permute-start.3) | collective-permute-done | bytes 81952 | tf_op jit(solution)/shard_map/ppermute | solution.py:434
  24.9 1.6 %collective-permute-done.2.rows2 = bf16[2,2,8,1280]{3,2,1,0:T(8,128)(2,1)S(1)} collective-permute-done((bf16[2,2,8,1280]{3,2,1,0:T(8,128)(2,1)S(1)}, bf16[2,2,8,1280]{3,2,1,0:T(8,128)(2,1)S(1)}, u32[]{:S(2)}, u32[]{:S(2)}) %collective-permute-start.2) | collective-permute-done | bytes 81952 | tf_op jit(solution)/shard_map/ppermute | solution.py:434
  26.5 2.0 %collective-permute-done.1.rows1 = bf16[2,2,8,1280]{3,2,1,0:T(8,128)(2,1)S(1)} collective-permute-done((bf16[2,2,8,1280]{3,2,1,0:T(8,128)(2,1)S(1)}, bf16[2,2,8,1280]{3,2,1,0:T(8,128)(2,1)S(1)}, u32[]{:S(2)}, u32[]{:S(2)}) %collective-permute-start.1) | collective-permute-done | bytes 81952 | tf_op jit(solution)/shard_map/ppermute | solution.py:434
  28.5 1.8 %all-to-all-done.received = bf16[128,2,8,128]{3,2,1,0:T(8,128)(2,1)S(1)} async-done(((bf16[128,2,8,128]{3,2,1,0:T(8,128)(2,1)}), bf16[128,2,8,128]{3,2,1,0:T(8,128)(2,1)S(1)}, u32[]{:S(2)}, u32[]{:S(2)}) %all-to-all-start) | async-done | bytes 524320 | tf_op jit(solution)/shard_map/all_to_all | solution.py:470
  31.1 2.9 %right_side.1 = (bf16[1024,128]{1,0:T(8,128)(2,1)}, bf16[16,72,128]{2,1,0:T(8,128)(2,1)}) custom-call(s32[4]{0:T(128)} %pad_add_fusion.place, bf16[128,2,8,128]{3,2,1,0:T(8,128)(2,1)} %copy-done.16, bf16[2,2,8,1280]{3,2,1,0:T(8,128)(2,1)} %copy-done.17, bf16[2,2,8,1280]{3,2,1,0:T(8,128)(2,1)} %copy-done.20, bf16[2,2,8,1280]{3,2,1,0:T(8,128)(2,1)} %copy-done.19, ...), custom_call_target="tpu_custom_call" | custom-call | tf_op jit(solution)/shard_map/right_side/pallas_call | solution.py:131
  34.0 14.3 %all_to_all.15.received = bf16[16,72,128]{2,1,0:T(8,128)(2,1)} all-to-all(bf16[16,72,128]{2,1,0:T(8,128)(2,1)} %get-tuple-element.19), channel_id=1, replica_groups=mesh['x'=4,'core'=2,'col'=16] {'col'}, dimensions={0} | all-to-all | bytes 589824 | tf_op jit(solution)/shard_map/all_to_all | solution.py:478
  48.4 3.1 %second_rows.1 = (bf16[128,128]{1,0:T(8,128)(2,1)}, bf16[64,64,128]{2,1,0:T(8,128)(2,1)}) custom-call(s32[4]{0:T(128)} %pad_add_fusion.place, bf16[16,72,128]{2,1,0:T(8,128)(2,1)} %all_to_all.15.received, bf16[2,2,8,1280]{3,2,1,0:T(8,128)(2,1)} %copy-done.17, bf16[2,2,8,1280]{3,2,1,0:T(8,128)(2,1)} %copy-done.20, bf16[2,2,8,1280]{3,2,1,0:T(8,128)(2,1)} %copy-done.19, ...), custom_call_target="tpu_custom_call" | custom-call | tf_op jit(solution)/shard_map/second_rows/pallas_call | solution.py:175
  51.5 21.0 %all_to_all.16 = bf16[64,64,128]{2,1,0:T(8,128)(2,1)S(1)} all-to-all(bf16[64,64,128]{2,1,0:T(8,128)(2,1)} %get-tuple-element.20), channel_id=1, replica_groups=mesh['x'=4,'core'=2,'col'=16] {'x','col'}, dimensions={0} | all-to-all | bytes 2097152 | tf_op jit(solution)/shard_map/all_to_all | solution.py:483
  72.5 3.4 %collective-permute-start.11 = (bf16[64,64,128]{2,1,0:T(8,128)(2,1)S(1)}, bf16[64,64,128]{2,1,0:T(8,128)(2,1)S(1)}, u32[]{:S(2)}, u32[]{:S(2)}) collective-permute-start(bf16[64,64,128]{2,1,0:T(8,128)(2,1)S(1)} %all_to_all.16), channel_id=1, source_target_pairs={{0,16},{16,0},{1,17},{17,1},{2,18},{18,2},{3,19},{19,3},{4,20},{20... | collective-permute-start | bytes 3145736 | tf_op jit(solution)/shard_map/ppermute | solution.py:439
  76.6 1.2 collective-permute-start.5
  78.3 5.4 %collective-permute-done.6.b3.refs_3_ = bf16[1024,128]{1,0:T(8,128)(2,1)S(1)} collective-permute-done((bf16[1024,128]{1,0:T(8,128)(2,1)S(1)}, bf16[1024,128]{1,0:T(8,128)(2,1)S(1)}, u32[]{:S(2)}, u32[]{:S(2)}) %collective-permute-start.6) | collective-permute-done | bytes 262176 | tf_op jit(solution)/shard_map/ppermute | solution.py:434
  83.7 1.3 collective-permute-start.10
  85.7 1.9 %collective-permute-start.9 = (bf16[1024,128]{1,0:T(8,128)(2,1)S(1)}, bf16[1024,128]{1,0:T(8,128)(2,1)S(1)}, u32[]{:S(2)}, u32[]{:S(2)}) collective-permute-start(bf16[1024,128]{1,0:T(8,128)(2,1)S(1)} %collective-permute-done.5.b2.refs_2_), channel_id=1, source_target_pairs={{0,16},{16,0},{1,17},{17,1},{2,18},{18,2},{3,19},{19,3},{4,20},{20... | collective-permute-start | bytes 786440 | tf_op jit(solution)/shard_map/ppermute | solution.py:439
  87.6 4.3 %collective-permute-done.4.b1.refs_1_ = bf16[1024,128]{1,0:T(8,128)(2,1)S(1)} collective-permute-done((bf16[1024,128]{1,0:T(8,128)(2,1)S(1)}, bf16[1024,128]{1,0:T(8,128)(2,1)S(1)}, u32[]{:S(2)}, u32[]{:S(2)}) %collective-permute-start.4) | collective-permute-done | bytes 262176 | tf_op jit(solution)/shard_map/ppermute | solution.py:434
  92.8 2.4 %collective-permute-done.14.refs_11_.refs_3_ = bf16[128,128]{1,0:T(8,128)(2,1)S(1)} collective-permute-done((bf16[128,128]{1,0:T(8,128)(2,1)S(1)}, bf16[128,128]{1,0:T(8,128)(2,1)S(1)}, u32[]{:S(2)}, u32[]{:S(2)}) %collective-permute-start.14) | collective-permute-done | bytes 32800 | tf_op jit(solution)/shard_map/ppermute | solution.py:434
  95.2 1.2 collective-permute-start.13
  96.4 3.1 %collective-permute-done.13.refs_10_.refs_2_ = bf16[128,128]{1,0:T(8,128)(2,1)S(1)} collective-permute-done((bf16[128,128]{1,0:T(8,128)(2,1)S(1)}, bf16[128,128]{1,0:T(8,128)(2,1)S(1)}, u32[]{:S(2)}, u32[]{:S(2)}) %collective-permute-start.13) | collective-permute-done | bytes 32800 | tf_op jit(solution)/shard_map/ppermute | solution.py:434
  99.5 4.0 %collective-permute-done.12.refs_9_.refs_1_ = bf16[128,128]{1,0:T(8,128)(2,1)S(1)} collective-permute-done((bf16[128,128]{1,0:T(8,128)(2,1)S(1)}, bf16[128,128]{1,0:T(8,128)(2,1)S(1)}, u32[]{:S(2)}, u32[]{:S(2)}) %collective-permute-start.12) | collective-permute-done | bytes 32800 | tf_op jit(solution)/shard_map/ppermute | solution.py:434
  103.4 3.5 %collective-permute-start.15 = (bf16[128,128]{1,0:T(8,128)(2,1)S(1)}, bf16[128,128]{1,0:T(8,128)(2,1)}, u32[]{:S(2)}, u32[]{:S(2)}) collective-permute-start(bf16[128,128]{1,0:T(8,128)(2,1)S(1)} %copy-done.12), channel_id=1, source_target_pairs={{0,16},{16,0},{1,17},{17,1},{2,18},{18,2},{3,19},{19,3},{4,20},{20... | collective-permute-start | bytes 98312 | tf_op jit(solution)/shard_map/ppermute | solution.py:439
  109.8 1.6 %copy-done.2 = bf16[2,2,1024,256]{3,2,1,0:T(8,128)(2,1)S(1)} copy-done((bf16[2,2,1024,256]{3,2,1,0:T(8,128)(2,1)S(1)}, bf16[2,2,1024,256]{3,2,1,0:T(8,128)(2,1)}, u32[]{:S(2)}) %copy-start.2) | copy-done | bytes 2097176
  111.4 0.9 copy-done.5
  113.3 0.9 copy-done.11
  114.2 12.7 %trail_first.1.partial = f32[2,2,1024,256]{3,2,1,0:T(8,128)} custom-call(s32[4]{0:T(128)S(1)} %copy-done.15, bf16[1024,128]{1,0:T(8,128)(2,1)S(1)} %copy-done.3, bf16[1024,128]{1,0:T(8,128)(2,1)S(1)} %collective-permute-done.4.b1.refs_1_, bf16[1024,128]{1,0:T(8,128)(2,1)S(1)} %collective-permute-done.5.b2.refs_2_, ...), custom_call_target="tpu_custom_call" | custom-call | tf_op jit(solution)/shard_map/trail_first/pallas_call | solution.py:243
  127.0 2.5 %gradient_first.1.refs_9_ = f32[8,128]{1,0:T(8,128)S(1)} custom-call(s32[4]{0:T(128)S(1)} %copy-done.15, bf16[1024,128]{1,0:T(8,128)(2,1)S(1)} %copy-done.3, bf16[1024,128]{1,0:T(8,128)(2,1)S(1)} %collective-permute-done.4.b1.refs_1_, bf16[1024,128]{1,0:T(8,128)(2,1)S(1)} %collective-permute-done.5.b2.refs_2_, ...), custom_call_target="tpu_custom_call" | custom-call | tf_op jit(solution)/shard_map/gradient_first/pallas_call | solution.py:377
  129.5 2.2 %copy-done.1 = f32[2,2,1024,256]{3,2,1,0:T(8,128)S(1)} copy-done((f32[2,2,1024,256]{3,2,1,0:T(8,128)S(1)}, f32[2,2,1024,256]{3,2,1,0:T(8,128)}, u32[]{:S(2)}) %copy-start.1) | copy-done | bytes 4194328
  131.7 7.2 %trail_second.2 = (bf16[2,2,1024,256]{3,2,1,0:T(8,128)(2,1)}, bf16[2,8,256]{2,1,0:T(8,128)(2,1)S(1)}) custom-call(s32[5]{0:T(128)S(1)} %concatenate.28.place, bf16[4,16,64,128]{3,2,1,0:T(8,128)(2,1)S(1)} %bitcast.15, bf16[2,2,2,1024,1024]{4,3,2,1,0:T(8,128)(2,1)} %factor.5, f32[2,2,1024,256]{3,2,1,0:T(8,128)S(1)} %copy-done.1), custom_call_target="tpu_custom_call" | custom-call | tf_op jit(solution)/shard_map/trail_second/pallas_call | solution.py:294
  138.9 7.2 %trail_second.3 = (bf16[2,2,1024,256]{3,2,1,0:T(8,128)(2,1)}, bf16[2,8,256]{2,1,0:T(8,128)(2,1)S(1)}) custom-call(s32[5]{0:T(128)S(1)} %concatenate.30.place, bf16[4,16,64,128]{3,2,1,0:T(8,128)(2,1)S(1)} %bitcast.17, bf16[2,2,2,1024,1024]{4,3,2,1,0:T(8,128)(2,1)} %factor.5, f32[2,2,1024,256]{3,2,1,0:T(8,128)S(1)} %copy-done.1, ...), custom_call_target="tpu_custom_call", output_to_operand_aliasing={{0}: (4, {})} | custom-call | tf_op jit(solution)/shard_map/trail_second/pallas_call | solution.py:294
  146.7 3.3 %gradient_second.1 = f32[3,8]{1,0:T(4,128)} custom-call(s32[4]{0:T(128)S(1)} %copy-done.15, bf16[4,16,64,128]{3,2,1,0:T(8,128)(2,1)S(1)} %bitcast.16, bf16[4,16,64,128]{3,2,1,0:T(8,128)(2,1)S(1)} %bitcast.18, bf16[128,128]{1,0:T(8,128)(2,1)S(1)} %copy-done.12, bf16[128,128]{1,0:T(8,128)(2,1)S(1)} %collective-permute-done.12.refs_9_.refs_1_, ...), custom_call_target="tpu_custom_call" | custom-call | tf_op jit(solution)/shard_map/gradient_second/pallas_call | solution.py:414
  (88 shorter events, 11.7 us)
Async XLA Ops:
  0.6 17.0 %copy-start = (s32[1024]{0:T(1024)S(1)}, s32[1024]{0:T(1024)}, u32[]{:S(2)}) copy-start(s32[1024]{0:T(1024)} %param.19) | copy-start | bytes 12292
  0.6 16.7 %copy-start.24 = (s32[2,8,3]{1,0,2:T(2,128)S(1)}, s32[2,8,3]{1,0,2:T(2,128)}, u32[]{:S(2)}) copy-start(s32[2,8,3]{1,0,2:T(2,128)} %param.18) | copy-start | bytes 580
  0.7 16.9 %copy-start.22 = (f32[2,9,2,8]{1,3,2,0:T(8,128)S(1)}, f32[2,9,2,8]{1,3,2,0:T(8,128)}, u32[]{:S(2)}) copy-start(f32[2,9,2,8]{1,3,2,0:T(8,128)} %param.17) | copy-start | bytes 3460
  4.7 25.6 %all-to-all-start = ((bf16[128,2,8,128]{3,2,1,0:T(8,128)(2,1)}), bf16[128,2,8,128]{3,2,1,0:T(8,128)(2,1)S(1)}, u32[]{:S(2)}, u32[]{:S(2)}) async-start(bf16[128,2,8,128]{3,2,1,0:T(8,128)(2,1)} %bitcast.21), calls=%async_computation | async-start | bytes 1048576 | tf_op jit(solution)/shard_map/all_to_all | solution.py:470
  16.2 2.4 %collective-permute-start = (bf16[2,8,1280]{2,1,0:T(8,128)(2,1)}, bf16[2,8,1280]{2,1,0:T(8,128)(2,1)S(1)}, u32[]{:S(2)}, u32[]{:S(2)}) collective-permute-start(bf16[2,8,1280]{2,1,0:T(8,128)(2,1)} %get-tuple-element.18), channel_id=1, source_target_pairs={{0,16},{16,0},{1,17},{17,1},{2,18},{18,2},{3,19},{19,3},{4,20},{20... | collective-permute-start | bytes 122888 | tf_op jit(solution)/shard_map/ppermute | solution.py:439
  18.6 11.7 %copy-start.17 = (bf16[2,2,8,1280]{3,2,1,0:T(8,128)(2,1)}, bf16[2,2,8,1280]{3,2,1,0:T(8,128)(2,1)S(1)}, u32[]{:S(2)}) copy-start(bf16[2,2,8,1280]{3,2,1,0:T(8,128)(2,1)S(1)} %maximum_select_fusion.rows0) | copy-start | bytes 245764
  18.6 6.3 %collective-permute-start.3 = (bf16[2,2,8,1280]{3,2,1,0:T(8,128)(2,1)S(1)}, bf16[2,2,8,1280]{3,2,1,0:T(8,128)(2,1)S(1)}, u32[]{:S(2)}, u32[]{:S(2)}) collective-permute-start(bf16[2,2,8,1280]{3,2,1,0:T(8,128)(2,1)S(1)} %maximum_select_fusion.rows0), channel_id=1, source_target_pairs={{0,96},{32,0},{64,32},{96,64},{1,97},{33,1},{65,33},{97,65},{2,98}... | collective-permute-start | bytes 245768 | tf_op jit(solution)/shard_map/ppermute | solution.py:434
  20.6 6.0 %collective-permute-start.2 = (bf16[2,2,8,1280]{3,2,1,0:T(8,128)(2,1)S(1)}, bf16[2,2,8,1280]{3,2,1,0:T(8,128)(2,1)S(1)}, u32[]{:S(2)}, u32[]{:S(2)}) collective-permute-start(bf16[2,2,8,1280]{3,2,1,0:T(8,128)(2,1)S(1)} %maximum_select_fusion.rows0), channel_id=1, source_target_pairs={{0,64},{32,96},{64,0},{96,32},{1,65},{33,97},{65,1},{97,33},{2,66}... | collective-permute-start | bytes 245768 | tf_op jit(solution)/shard_map/ppermute | solution.py:434
  21.1 7.3 %collective-permute-start.1 = (bf16[2,2,8,1280]{3,2,1,0:T(8,128)(2,1)S(1)}, bf16[2,2,8,1280]{3,2,1,0:T(8,128)(2,1)S(1)}, u32[]{:S(2)}, u32[]{:S(2)}) collective-permute-start(bf16[2,2,8,1280]{3,2,1,0:T(8,128)(2,1)S(1)} %maximum_select_fusion.rows0), channel_id=1, source_target_pairs={{0,32},{32,64},{64,96},{96,0},{1,33},{33,65},{65,97},{97,1},{2,34}... | collective-permute-start | bytes 245768 | tf_op jit(solution)/shard_map/ppermute | solution.py:434
  21.7 88.0 %copy-start.15 = (s32[4]{0:T(128)S(1)}, s32[4]{0:T(128)}, u32[]{:S(2)}) copy-start(s32[4]{0:T(128)} %pad_add_fusion.place) | copy-start | bytes 52
  34.0 41.8 %copy-start.3 = (bf16[1024,128]{1,0:T(8,128)(2,1)S(1)}, bf16[1024,128]{1,0:T(8,128)(2,1)}, u32[]{:S(2)}) copy-start(bf16[1024,128]{1,0:T(8,128)(2,1)} %get-tuple-element.21.b0.refs_0_) | copy-start | bytes 786436
  51.5 40.9 %copy-start.12 = (bf16[128,128]{1,0:T(8,128)(2,1)S(1)}, bf16[128,128]{1,0:T(8,128)(2,1)}, u32[]{:S(2)}) copy-start(bf16[128,128]{1,0:T(8,128)(2,1)} %get-tuple-element.26.refs_8_.refs_0_) | copy-start | bytes 98308
  72.5 66.4 %collective-permute-start.11 = (bf16[64,64,128]{2,1,0:T(8,128)(2,1)S(1)}, bf16[64,64,128]{2,1,0:T(8,128)(2,1)S(1)}, u32[]{:S(2)}, u32[]{:S(2)}) collective-permute-start(bf16[64,64,128]{2,1,0:T(8,128)(2,1)S(1)} %all_to_all.16), channel_id=1, source_target_pairs={{0,16},{16,0},{1,17},{17,1},{2,18},{18,2},{3,19},{19,3},{4,20},{20... | collective-permute-start | bytes 3145736 | tf_op jit(solution)/shard_map/ppermute | solution.py:439
  75.8 7.9 %collective-permute-start.6 = (bf16[1024,128]{1,0:T(8,128)(2,1)S(1)}, bf16[1024,128]{1,0:T(8,128)(2,1)S(1)}, u32[]{:S(2)}, u32[]{:S(2)}) collective-permute-start(bf16[1024,128]{1,0:T(8,128)(2,1)S(1)} %copy-done.3), channel_id=1, source_target_pairs={{0,96},{32,0},{64,32},{96,64},{1,97},{33,1},{65,33},{97,65},{2,98}... | collective-permute-start | bytes 786440 | tf_op jit(solution)/shard_map/ppermute | solution.py:434
  76.6 9.1 %collective-permute-start.5 = (bf16[1024,128]{1,0:T(8,128)(2,1)S(1)}, bf16[1024,128]{1,0:T(8,128)(2,1)S(1)}, u32[]{:S(2)}, u32[]{:S(2)}) collective-permute-start(bf16[1024,128]{1,0:T(8,128)(2,1)S(1)} %copy-done.3), channel_id=1, source_target_pairs={{0,64},{32,96},{64,0},{96,32},{1,65},{33,97},{65,1},{97,33},{2,66}... | collective-permute-start | bytes 786440 | tf_op jit(solution)/shard_map/ppermute | solution.py:434
  77.8 14.2 %collective-permute-start.4 = (bf16[1024,128]{1,0:T(8,128)(2,1)S(1)}, bf16[1024,128]{1,0:T(8,128)(2,1)S(1)}, u32[]{:S(2)}, u32[]{:S(2)}) collective-permute-start(bf16[1024,128]{1,0:T(8,128)(2,1)S(1)} %copy-done.3), channel_id=1, source_target_pairs={{0,32},{32,64},{64,96},{96,0},{1,33},{33,65},{65,97},{97,1},{2,34}... | collective-permute-start | bytes 786440 | tf_op jit(solution)/shard_map/ppermute | solution.py:434
  77.8 14.6 %collective-permute-start.7 = (bf16[1024,128]{1,0:T(8,128)(2,1)S(1)}, bf16[1024,128]{1,0:T(8,128)(2,1)S(1)}, u32[]{:S(2)}, u32[]{:S(2)}) collective-permute-start(bf16[1024,128]{1,0:T(8,128)(2,1)S(1)} %copy-done.3), channel_id=1, source_target_pairs={{0,16},{16,0},{1,17},{17,1},{2,18},{18,2},{3,19},{19,3},{4,20},{20... | collective-permute-start | bytes 786440 | tf_op jit(solution)/shard_map/ppermute | solution.py:439
  83.7 23.3 %collective-permute-start.10 = (bf16[1024,128]{1,0:T(8,128)(2,1)S(1)}, bf16[1024,128]{1,0:T(8,128)(2,1)S(1)}, u32[]{:S(2)}, u32[]{:S(2)}) collective-permute-start(bf16[1024,128]{1,0:T(8,128)(2,1)S(1)} %collective-permute-done.6.b3.refs_3_), channel_id=1, source_target_pairs={{0,16},{16,0},{1,17},{17,1},{2,18},{18,2},{3,19},{19,3},{4,20},{20... | collective-permute-start | bytes 786440 | tf_op jit(solution)/shard_map/ppermute | solution.py:439
  85.7 22.0 %collective-permute-start.9 = (bf16[1024,128]{1,0:T(8,128)(2,1)S(1)}, bf16[1024,128]{1,0:T(8,128)(2,1)S(1)}, u32[]{:S(2)}, u32[]{:S(2)}) collective-permute-start(bf16[1024,128]{1,0:T(8,128)(2,1)S(1)} %collective-permute-done.5.b2.refs_2_), channel_id=1, source_target_pairs={{0,16},{16,0},{1,17},{17,1},{2,18},{18,2},{3,19},{19,3},{4,20},{20... | collective-permute-start | bytes 786440 | tf_op jit(solution)/shard_map/ppermute | solution.py:439
  91.9 17.0 %collective-permute-start.8 = (bf16[1024,128]{1,0:T(8,128)(2,1)S(1)}, bf16[1024,128]{1,0:T(8,128)(2,1)S(1)}, u32[]{:S(2)}, u32[]{:S(2)}) collective-permute-start(bf16[1024,128]{1,0:T(8,128)(2,1)S(1)} %collective-permute-done.4.b1.refs_1_), channel_id=1, source_target_pairs={{0,16},{16,0},{1,17},{17,1},{2,18},{18,2},{3,19},{19,3},{4,20},{20... | collective-permute-start | bytes 786440 | tf_op jit(solution)/shard_map/ppermute | solution.py:439
  92.4 2.8 %collective-permute-start.14 = (bf16[128,128]{1,0:T(8,128)(2,1)S(1)}, bf16[128,128]{1,0:T(8,128)(2,1)S(1)}, u32[]{:S(2)}, u32[]{:S(2)}) collective-permute-start(bf16[128,128]{1,0:T(8,128)(2,1)S(1)} %copy-done.12), channel_id=1, source_target_pairs={{0,96},{32,0},{64,32},{96,64},{1,97},{33,1},{65,33},{97,65},{2,98}... | collective-permute-start | bytes 98312 | tf_op jit(solution)/shard_map/ppermute | solution.py:434
  95.2 4.3 %collective-permute-start.13 = (bf16[128,128]{1,0:T(8,128)(2,1)S(1)}, bf16[128,128]{1,0:T(8,128)(2,1)S(1)}, u32[]{:S(2)}, u32[]{:S(2)}) collective-permute-start(bf16[128,128]{1,0:T(8,128)(2,1)S(1)} %copy-done.12), channel_id=1, source_target_pairs={{0,64},{32,96},{64,0},{96,32},{1,65},{33,97},{65,1},{97,33},{2,66}... | collective-permute-start | bytes 98312 | tf_op jit(solution)/shard_map/ppermute | solution.py:434
  99.5 4.0 %collective-permute-start.12 = (bf16[128,128]{1,0:T(8,128)(2,1)S(1)}, bf16[128,128]{1,0:T(8,128)(2,1)S(1)}, u32[]{:S(2)}, u32[]{:S(2)}) collective-permute-start(bf16[128,128]{1,0:T(8,128)(2,1)S(1)} %copy-done.12), channel_id=1, source_target_pairs={{0,32},{32,64},{64,96},{96,0},{1,33},{33,65},{65,97},{97,1},{2,34}... | collective-permute-start | bytes 98312 | tf_op jit(solution)/shard_map/ppermute | solution.py:434
  103.4 23.5 %collective-permute-start.15 = (bf16[128,128]{1,0:T(8,128)(2,1)S(1)}, bf16[128,128]{1,0:T(8,128)(2,1)}, u32[]{:S(2)}, u32[]{:S(2)}) collective-permute-start(bf16[128,128]{1,0:T(8,128)(2,1)S(1)} %copy-done.12), channel_id=1, source_target_pairs={{0,16},{16,0},{1,17},{17,1},{2,18},{18,2},{3,19},{19,3},{4,20},{20... | collective-permute-start | bytes 98312 | tf_op jit(solution)/shard_map/ppermute | solution.py:439
  107.7 19.3 %collective-permute-start.18 = (bf16[128,128]{1,0:T(8,128)(2,1)S(1)}, bf16[128,128]{1,0:T(8,128)(2,1)}, u32[]{:S(2)}, u32[]{:S(2)}) collective-permute-start(bf16[128,128]{1,0:T(8,128)(2,1)S(1)} %collective-permute-done.14.refs_11_.refs_3_), channel_id=1, source_target_pairs={{0,16},{16,0},{1,17},{17,1},{2,18},{18,2},{3,19},{19,3},{4,20},{20... | collective-permute-start | bytes 98312 | tf_op jit(solution)/shard_map/ppermute | solution.py:439
  108.4 18.6 %collective-permute-start.17 = (bf16[128,128]{1,0:T(8,128)(2,1)S(1)}, bf16[128,128]{1,0:T(8,128)(2,1)}, u32[]{:S(2)}, u32[]{:S(2)}) collective-permute-start(bf16[128,128]{1,0:T(8,128)(2,1)S(1)} %collective-permute-done.13.refs_10_.refs_2_), channel_id=1, source_target_pairs={{0,16},{16,0},{1,17},{17,1},{2,18},{18,2},{3,19},{19,3},{4,20},{20... | collective-permute-start | bytes 98312 | tf_op jit(solution)/shard_map/ppermute | solution.py:439
  109.6 17.4 %collective-permute-start.16 = (bf16[128,128]{1,0:T(8,128)(2,1)S(1)}, bf16[128,128]{1,0:T(8,128)(2,1)}, u32[]{:S(2)}, u32[]{:S(2)}) collective-permute-start(bf16[128,128]{1,0:T(8,128)(2,1)S(1)} %collective-permute-done.12.refs_9_.refs_1_), channel_id=1, source_target_pairs={{0,16},{16,0},{1,17},{17,1},{2,18},{18,2},{3,19},{19,3},{4,20},{20... | collective-permute-start | bytes 98312 | tf_op jit(solution)/shard_map/ppermute | solution.py:439
  114.2 12.7 %copy-start.6 = (bf16[1024,128]{1,0:T(8,128)(2,1)S(1)}, bf16[1024,128]{1,0:T(8,128)(2,1)}, u32[]{:S(2)}) copy-start(bf16[1024,128]{1,0:T(8,128)(2,1)} %copy-done.4) | copy-start | bytes 786436
  114.2 12.8 %copy-start.9 = (bf16[1024,128]{1,0:T(8,128)(2,1)S(1)}, bf16[1024,128]{1,0:T(8,128)(2,1)}, u32[]{:S(2)}) copy-start(bf16[1024,128]{1,0:T(8,128)(2,1)} %copy-done.7) | copy-start | bytes 786436
  114.2 12.8 %copy-start.14 = (bf16[128,384]{1,0:T(8,128)(2,1)S(1)}, bf16[128,384]{1,0:T(8,128)(2,1)}, u32[]{:S(2)}) copy-start(bf16[128,384]{1,0:T(8,128)(2,1)} %constant.57.clone.refs_16_) | copy-start | bytes 294916
  138.9 7.2 %copy-start.23 = (bf16[2,2,8,256]{3,2,1,0:T(8,128)(2,1)S(1)}, bf16[2,2,8,256]{3,2,1,0:T(8,128)(2,1)}, u32[]{:S(2)}) copy-start(bf16[2,2,8,256]{3,2,1,0:T(8,128)(2,1)} %get-tuple-element.15) | copy-start | bytes 49156
  138.9 7.8 %copy-start.13 = (bf16[128,384]{1,0:T(8,128)(2,1)S(1)}, bf16[128,384]{1,0:T(8,128)(2,1)}, u32[]{:S(2)}) copy-start(bf16[128,384]{1,0:T(8,128)(2,1)} %constant.58.clone.refs_8_) | copy-start | bytes 294916
  (13 other events, 21.5 us)

commit v3 on v2

--- a/solution.py
+++ b/solution.py
@@ -6,6 +6,7 @@
 from jax.experimental.pallas import tpu as pltpu
 from jax.sharding import Mesh
 from jax.sharding import PartitionSpec as P
+
 
 ALL = ("x", "core", "col")
 F32 = jnp.float32
@@ -207,17 +208,14 @@
     return total + jnp.dot(factor[0, 0, 1], weights[1024:], preferred_element_type=F32)
 
 
-def trail_first_kernel(place, b0, b1, b2, b3, c0, c1, c2, c3, factor, rhs, out, ordered, weights):
+def trail_first_kernel(place, mine, theirs, factor, rhs, out, weights):
     x = place[0]
     turn = pl.program_id(0)
 
     def build(blocks):
-        for step, block in enumerate(blocks):
-            ordered[lax.rem(x - step + 4, 4)] = block[...]
-
         def chunk(row, carry):
             at = pl.multiple_of(128 * row, 128)
-            parts = [ordered[q, pl.ds(at, 128), :].astype(F32) for q in range(4)]
+            parts = [blocks[lax.rem(x - q + 4, 4), pl.ds(at, 128), :].astype(F32) for q in range(4)]
             store_weights(weights, at, ((parts[0], parts[1]), (parts[2], parts[3])))
             return carry
 
@@ -225,18 +223,18 @@
 
     @pl.when((turn == 0) & (pl.program_id(1) == 0))
     def _():
-        build((b0, b1, b2, b3))
+        build(mine)
 
     @pl.when((turn == 1) & (pl.program_id(1) == 0))
     def _():
-        build((c0, c1, c2, c3))
+        build(theirs)
 
     total = trail_product(factor, weights)
     out[0, 0] = rhs[0, 0].astype(F32) - total[:, :256]
     out[0, 1] = rhs[0, 1].astype(F32) - total[:, 256:]
 
 
-def trail_first(place, blocks, trail_factor, trail_rhs):
+def trail_first(place, mine, theirs, trail_factor, trail_rhs):
     rows = trail_rhs.shape[2]
     height = min(256, rows)
     system = lambda turn, p: jnp.where(turn == 0, p[1], 1 - p[1])
@@ -245,18 +243,18 @@
         grid_spec=pltpu.PrefetchScalarGridSpec(
             num_scalar_prefetch=1,
             grid=(2, rows // height),
-            in_specs=[pl.BlockSpec((1024, 128), lambda t, i, p: (0, 0))] * 8
+            in_specs=[pl.BlockSpec((4, 1024, 128), lambda t, i, p: (0, 0, 0))] * 2
             + [
                 pl.BlockSpec((1, 1, 2, height, 1024), lambda t, i, p: (system(t, p), 0, 0, i, 0)),
                 pl.BlockSpec((1, 2, height, 256), lambda t, i, p: (system(t, p), 0, i, 0)),
             ],
             out_specs=pl.BlockSpec((1, 2, height, 256), lambda t, i, p: (system(t, p), 0, i, 0)),
-            scratch_shapes=[pltpu.VMEM((4, 1024, 128), BF16), pltpu.VMEM((2048, 512), BF16)],
+            scratch_shapes=[pltpu.VMEM((2048, 512), BF16)],
         ),
         out_shape=jax.ShapeDtypeStruct((2, 2, rows, 256), F32),
         compiler_params=pltpu.CompilerParams(vmem_limit_bytes=VMEM_LIMIT),
         name="trail_first",
-    )(place, *blocks, trail_factor, trail_rhs)
+    )(place, mine, theirs, trail_factor, trail_rhs)
 
 
 def trail_second_kernel(place, blocks, factor, partial, *refs):
@@ -332,7 +330,7 @@
     return jnp.asarray(spread.reshape(128, 384), BF16)
 
 
-def gradient_sum(place, couple, tile_refs, spread, chunk_of):
+def gradient_sum(place, couple, tile_refs, spread):
     base = 8 * (16 * place[2] + place[3])
     target = (base + lax.rem(lax.broadcasted_iota(jnp.int32, (128, 128), 1), 8)).astype(F32)
     sign = jnp.where(lanes_below((128, 128), 64), 1.0, -1.0)
@@ -344,7 +342,7 @@
             same, crossed = couple(2 * source + core)
             real = jnp.sum(same * sign, axis=1, keepdims=True)
             imag = jnp.sum(crossed, axis=1, keepdims=True)
-            table = jnp.dot(tile_refs[4 * side + step][...], spread[...], preferred_element_type=F32)
+            table = jnp.dot(tile_refs[side][step], spread[...], preferred_element_type=F32)
             value = table[:, 128:256] * imag - table[:, :128] * real
             value = jnp.where(table[:, 256:] == target, value, 0.0)
             total = total + jnp.sum(value.reshape(16, 8, 128), axis=0)
@@ -360,38 +358,38 @@
     return same, crossed
 
 
-def gradient_first_kernel(place, *refs):
-    blocks, tiles, spread, out = refs[:8], refs[8:16], refs[16], refs[17]
+def gradient_first_kernel(place, mine, theirs, own_tiles, other_tiles, spread, out):
+    tiles = (own_tiles, other_tiles)
 
     def couple(row):
         at = pl.multiple_of(128 * row, 128)
         return couple_pairs(
-            (blocks[q][pl.ds(at, 128), :].astype(F32), blocks[4 + q][pl.ds(at, 128), :].astype(F32))
+            (mine[q, pl.ds(at, 128), :].astype(F32), theirs[q, pl.ds(at, 128), :].astype(F32))
             for q in range(4)
         )
 
-    out[...] = gradient_sum(place, couple, tiles, spread, None)
-
-
-def gradient_first(place, blocks, tiles, spread):
+    out[...] = gradient_sum(place, couple, tiles, spread)
+
+
+def gradient_first(place, mine, theirs, tiles, spread):
     return pl.pallas_call(
         gradient_first_kernel,
         grid_spec=pltpu.PrefetchScalarGridSpec(
             num_scalar_prefetch=1,
             grid=(1,),
-            in_specs=[pl.BlockSpec((1024, 128), lambda i, p: (0, 0))] * 8
-            + [pl.BlockSpec((128, 128), lambda i, p: (0, 0))] * 8
+            in_specs=[pl.BlockSpec((4, 1024, 128), lambda i, p: (0, 0, 0))] * 2
+            + [pl.BlockSpec((4, 128, 128), lambda i, p: (0, 0, 0))] * 2
             + [pl.BlockSpec((128, 384), lambda i, p: (0, 0))],
             out_specs=pl.BlockSpec((8, 128), lambda i, p: (0, 0)),
         ),
         out_shape=jax.ShapeDtypeStruct((8, 128), F32),
         compiler_params=pltpu.CompilerParams(vmem_limit_bytes=VMEM_LIMIT),
         name="gradient_first",
-    )(place, *blocks, *tiles, spread)
-
-
-def gradient_second_kernel(place, mine, theirs, *refs):
-    tiles, spread, before, out = refs[:8], refs[8], refs[9], refs[10]
+    )(place, mine, theirs, *tiles, spread)
+
+
+def gradient_second_kernel(place, mine, theirs, own_tiles, other_tiles, spread, before, out):
+    tiles = (own_tiles, other_tiles)
 
     def couple(row):
         near = pl.multiple_of(8 * row, 8)
@@ -403,7 +401,7 @@
             for q in range(4)
         )
 
-    total = before[...] + gradient_sum(place, couple, tiles, spread, None)
+    total = before[...] + gradient_sum(place, couple, tiles, spread)
     total = jnp.sum(total, axis=0, keepdims=True)
     total = total + pltpu.roll(total, 104, 1) + pltpu.roll(total, 80, 1)
     for coordinate in range(3):
@@ -417,7 +415,7 @@
             num_scalar_prefetch=1,
             grid=(1,),
             in_specs=[pl.BlockSpec((4, 16, 64, 128), lambda i, p: (0, 0, 0, 0))] * 2
-            + [pl.BlockSpec((128, 128), lambda i, p: (0, 0))] * 8
+            + [pl.BlockSpec((4, 128, 128), lambda i, p: (0, 0, 0))] * 2
             + [
                 pl.BlockSpec((128, 384), lambda i, p: (0, 0)),
                 pl.BlockSpec((8, 128), lambda i, p: (0, 0)),
@@ -450,7 +448,7 @@
     return jnp.concatenate(parts, axis=1).astype(BF16)
 
 
-def body(
+def steps(
     panel_inverse,
     panel_below,
     trail_factor,
@@ -477,22 +475,24 @@
     first_block, send = right_side(place, received, rows, tile)
     received = lax.all_to_all(send, "col", 0, 0, tiled=True)
     first_mine = rounds_x(first_block)
-    first_theirs = [swap_core(block) for block in first_mine]
+    first_mine = jnp.stack(first_mine)
+    first_theirs = swap_core(first_mine)
 
     tiles, send = second_rows(place, received, rows)
     second_mine = lax.all_to_all(send, ("x", "col"), 0, 0, tiled=True)
 
-    tiles_mine = rounds_x(tiles)
-    tiles_all = tiles_mine + [swap_core(block) for block in tiles_mine]
-    partial = trail_first(place, first_mine + first_theirs, trail_factor, trail_rhs)
-    gradient = gradient_first(place, first_mine + first_theirs, tiles_all, spread_matrix(0))
+    tiles = rounds_x(tiles)
+    tiles = jnp.stack(tiles)
+    tiles = (tiles, swap_core(tiles))
+    partial = trail_first(place, first_mine, first_theirs, trail_factor, trail_rhs)
+    gradient = gradient_first(place, first_mine, first_theirs, tiles, spread_matrix(0))
 
     second_theirs = swap_core(second_mine)
     mine = second_mine.reshape(4, 16, 64, 128)
     theirs = second_theirs.reshape(4, 16, 64, 128)
     update, own_mine = trail_second(place, core, mine, trail_factor, partial)
     update, own_theirs = trail_second(place, 1 - core, theirs, trail_factor, partial, update)
-    gradient = gradient_second(place, mine, theirs, tiles_all, spread_matrix(1), gradient)
+    gradient = gradient_second(place, mine, theirs, tiles, spread_matrix(1), gradient)
 
     second = jnp.where(
         core == 0, jnp.stack([own_mine, own_theirs]), jnp.stack([own_theirs, own_mine])
@@ -503,7 +503,7 @@
 def solution(mesh):
     fine = Mesh(mesh.devices.reshape(4, 2, 16), ALL)
     return jax.shard_map(
-        body,
+        steps,
         mesh=fine,
         in_specs=(
             P(None, None, None, ALL, None),

time: 151 us -> 130 us (0.86)
  blocking collectives: 35.3 us -> 14.3 us
  waiting for transfers between devices: 27.8 us -> 34 us
  local copies, waits for them, and re-layouts: 11.6 us -> 6.64 us
    all_to_all x2 -> x1, blocking collectives: 35.3 us -> 14.3 us  [steps(): received = lax.all_to_all(send, 'col', 0, 0, tiled=True)]
    ppermute x10 -> x4, starting transfers between devices: 12.8 us -> 4.23 us  [swap_core(): return lax.ppermute(value, 'core', [(0, 1), (1, 0)])]
    ppermute x9, waiting for transfers between devices: 25.9 us -> 32.1 us  [rounds_x(): lax.ppermute(value, 'x', [(i, (i + step) % 4) for i in range(4)])]
    unnamed x50 -> x36, local copies, waits for them, and re-layouts: 9.59 us -> 4.63 us
    all_to_all x1 -> x2, starting transfers between devices: 11.5 us -> 16.3 us  [the longest x1 11.5 us: steps(): lax.all_to_all(send.reshape(128, 2, 8, 128), ALL, 0, 0, tiled=True)]
    ppermute x9, starting transfers between devices: 6.57 us -> 9.03 us  [rounds_x(): lax.ppermute(value, 'x', [(i, (i + step) % 4) for i in range(4)])]
  transfers between devices with their start and end apart: 20 -> 15, of which waited for: 10 -> 10; matrix products, arithmetic and copies ran while one was open for 1% -> 2% of each run, Pallas kernels for 15% -> 17%
where the time goes in v3:
time: 130 us; the launch traced here: 129 us
  Pallas kernels  42.5 us (33%)
  waiting for transfers between devices  34 us (26%)
  starting transfers between devices  29.5 us (23%)
  blocking collectives  14.3 us (11%)
  local copies, waits for them, and re-layouts  6.64 us (5%)
  other arithmetic  1.42 us (1%)
    ppermute x9, waiting for transfers between devices, rounds_x(): lax.ppermute(value, 'x', [(i, (i + step) % 4) for i in range(4)])  32.1 us
    pallas_call x2, Pallas kernels, trail_second(): pl.pallas_call(trail_second_kernel, grid_spec=pltpu.PrefetchScalarGridSpe...  15 us
    all_to_all x1, blocking collectives, steps(): received = lax.all_to_all(send, 'col', 0, 0, tiled=True)  14.3 us
    pallas_call x1, Pallas kernels, trail_first(): pl.pallas_call(trail_first_kernel, grid_spec=pltpu.PrefetchScalarGridSpec...  12.7 us
    all_to_all x1, starting transfers between devices, steps(): lax.all_to_all(send.reshape(128, 2, 8, 128), ALL, 0, 0, tiled=True)  11.5 us
    ppermute x9, starting transfers between devices, rounds_x(): lax.ppermute(value, 'x', [(i, (i + step) % 4) for i in range(4)])  9.03 us
    all_to_all x1, starting transfers between devices, steps(): second_mine = lax.all_to_all(send, ('x', 'col'), 0, 0, tiled=True)  4.79 us
    unnamed x36, local copies, waits for them, and re-layouts  4.63 us
  transfers between devices with their start and end apart: 15, of which 10 were waited for; matrix products, arithmetic and copies ran while one was open for 2% of the time, Pallas kernels for 17%

profile of v3, /device:TPU:1, one launch (start us, length us, event | category | flops | bytes accessed | tf_op | source)
XLA Modules:
  0.0 129.3 jit_solution(15626773038727007584)
XLA Ops:
  1.3 3.4 %prepare.1 = (bf16[2,2,8,256]{3,2,1,0:T(8,128)(2,1)}, bf16[4,2,16,2,8,128]{5,4,3,2,1,0:T(8,128)(2,1)}, bf16[2,8,1280]{2,1,0:T(8,128)(2,1)}, bf16[2,8,1280]{2,1,0:T(8,128)(2,1)}) custom-call(s32[4]{0:T(128)} %pad_add_fusion.place, bf16[2,2,2,8,1024]{4,3,2,1,0:T(8,128)(2,1)} %inverse.1, bf16[2,2,1024,256]{3,2,1,0:T(8,128)(2,1)} %rhs.2, ...), custom_call_target="tpu_custom_call" | custom-call | tf_op jit(solution)/shard_map/prepare/pallas_call | solution.py:81
  4.6 11.5 %all-to-all-start = ((bf16[128,2,8,128]{3,2,1,0:T(8,128)(2,1)}), bf16[128,2,8,128]{3,2,1,0:T(8,128)(2,1)S(1)}, u32[]{:S(2)}, u32[]{:S(2)}) async-start(bf16[128,2,8,128]{3,2,1,0:T(8,128)(2,1)} %bitcast.27), calls=%async_computation | async-start | bytes 1048576 | tf_op jit(solution)/shard_map/all_to_all | solution.py:468
  16.1 1.1 collective-permute-start
  17.6 0.7 gather_fusion
  18.6 2.0 %collective-permute-start.3 = (bf16[2,2,8,1280]{3,2,1,0:T(8,128)(2,1)S(1)}, bf16[2,2,8,1280]{3,2,1,0:T(8,128)(2,1)S(1)}, u32[]{:S(2)}, u32[]{:S(2)}) collective-permute-start(bf16[2,2,8,1280]{3,2,1,0:T(8,128)(2,1)S(1)} %maximum_select_fusion.rows0), channel_id=1, source_target_pairs={{0,96},{32,0},{64,32},{96,64},{1,97},{33,1},{65,33},{97,65},{2,98}... | collective-permute-start | bytes 245768 | tf_op jit(solution)/shard_map/ppermute | solution.py:432
  22.4 2.5 %collective-permute-done.3.rows3 = bf16[2,2,8,1280]{3,2,1,0:T(8,128)(2,1)S(1)} collective-permute-done((bf16[2,2,8,1280]{3,2,1,0:T(8,128)(2,1)S(1)}, bf16[2,2,8,1280]{3,2,1,0:T(8,128)(2,1)S(1)}, u32[]{:S(2)}, u32[]{:S(2)}) %collective-permute-start.3) | collective-permute-done | bytes 81952 | tf_op jit(solution)/shard_map/ppermute | solution.py:432
  24.9 1.6 %collective-permute-done.2.rows2 = bf16[2,2,8,1280]{3,2,1,0:T(8,128)(2,1)S(1)} collective-permute-done((bf16[2,2,8,1280]{3,2,1,0:T(8,128)(2,1)S(1)}, bf16[2,2,8,1280]{3,2,1,0:T(8,128)(2,1)S(1)}, u32[]{:S(2)}, u32[]{:S(2)}) %collective-permute-start.2) | collective-permute-done | bytes 81952 | tf_op jit(solution)/shard_map/ppermute | solution.py:432
  26.5 2.0 %collective-permute-done.1.rows1 = bf16[2,2,8,1280]{3,2,1,0:T(8,128)(2,1)S(1)} collective-permute-done((bf16[2,2,8,1280]{3,2,1,0:T(8,128)(2,1)S(1)}, bf16[2,2,8,1280]{3,2,1,0:T(8,128)(2,1)S(1)}, u32[]{:S(2)}, u32[]{:S(2)}) %collective-permute-start.1) | collective-permute-done | bytes 81952 | tf_op jit(solution)/shard_map/ppermute | solution.py:432
  28.4 1.8 %all-to-all-done.received = bf16[128,2,8,128]{3,2,1,0:T(8,128)(2,1)S(1)} async-done(((bf16[128,2,8,128]{3,2,1,0:T(8,128)(2,1)}), bf16[128,2,8,128]{3,2,1,0:T(8,128)(2,1)S(1)}, u32[]{:S(2)}, u32[]{:S(2)}) %all-to-all-start) | async-done | bytes 524320 | tf_op jit(solution)/shard_map/all_to_all | solution.py:468
  30.3 0.8 copy-done.7
  31.1 2.9 %right_side.1 = (bf16[1024,128]{1,0:T(8,128)(2,1)}, bf16[16,72,128]{2,1,0:T(8,128)(2,1)}) custom-call(s32[4]{0:T(128)} %pad_add_fusion.place, bf16[128,2,8,128]{3,2,1,0:T(8,128)(2,1)} %copy-done.7, bf16[2,2,8,1280]{3,2,1,0:T(8,128)(2,1)} %copy-done.8, bf16[2,2,8,1280]{3,2,1,0:T(8,128)(2,1)} %copy-done.11, bf16[2,2,8,1280]{3,2,1,0:T(8,128)(2,1)} %copy-done.10, ...), custom_call_target="tpu_custom_call" | custom-call | tf_op jit(solution)/shard_map/right_side/pallas_call | solution.py:132
  34.0 14.3 %all_to_all.15.received = bf16[16,72,128]{2,1,0:T(8,128)(2,1)} all-to-all(bf16[16,72,128]{2,1,0:T(8,128)(2,1)} %get-tuple-element.19), channel_id=1, replica_groups=mesh['x'=4,'core'=2,'col'=16] {'col'}, dimensions={0} | all-to-all | bytes 589824 | tf_op jit(solution)/shard_map/all_to_all | solution.py:476
  48.3 3.1 %second_rows.1 = (bf16[128,128]{1,0:T(8,128)(2,1)}, bf16[64,64,128]{2,1,0:T(8,128)(2,1)}) custom-call(s32[4]{0:T(128)} %pad_add_fusion.place, bf16[16,72,128]{2,1,0:T(8,128)(2,1)} %all_to_all.15.received, bf16[2,2,8,1280]{3,2,1,0:T(8,128)(2,1)} %copy-done.8, bf16[2,2,8,1280]{3,2,1,0:T(8,128)(2,1)} %copy-done.11, bf16[2,2,8,1280]{3,2,1,0:T(8,128)(2,1)} %copy-done.10, ...), custom_call_target="tpu_custom_call" | custom-call | tf_op jit(solution)/shard_map/second_rows/pallas_call | solution.py:176
  51.5 4.8 %all-to-all-start.2 = ((bf16[64,64,128]{2,1,0:T(8,128)(2,1)}), bf16[64,64,128]{2,1,0:T(8,128)(2,1)S(1)}, u32[]{:S(2)}, u32[]{:S(2)}) async-start(bf16[64,64,128]{2,1,0:T(8,128)(2,1)} %get-tuple-element.20), calls=%async_computation.2 | async-start | bytes 2097152 | tf_op jit(solution)/shard_map/all_to_all | solution.py:482
  56.3 2.5 %collective-permute-start.6 = (bf16[1024,128]{1,0:T(8,128)(2,1)S(1)}, bf16[1024,128]{1,0:T(8,128)(2,1)S(1)}, u32[]{:S(2)}, u32[]{:S(2)}) collective-permute-start(bf16[1024,128]{1,0:T(8,128)(2,1)S(1)} %copy-done.12), channel_id=1, source_target_pairs={{0,96},{32,0},{64,32},{96,64},{1,97},{33,1},{65,33},{97,65},{2,98}... | collective-permute-start | bytes 786440 | tf_op jit(solution)/shard_map/ppermute | solution.py:432
  59.1 0.7 collective-permute-start.4
  59.8 13.2 %collective-permute-done.6 = bf16[1024,128]{1,0:T(8,128)(2,1)S(1)} collective-permute-done((bf16[1024,128]{1,0:T(8,128)(2,1)S(1)}, bf16[1024,128]{1,0:T(8,128)(2,1)S(1)}, u32[]{:S(2)}, u32[]{:S(2)}) %collective-permute-start.6) | collective-permute-done | bytes 262176 | tf_op jit(solution)/shard_map/ppermute | solution.py:432
  73.1 1.6 %collective-permute-done.5 = bf16[1024,128]{1,0:T(8,128)(2,1)S(1)} collective-permute-done((bf16[1024,128]{1,0:T(8,128)(2,1)S(1)}, bf16[1024,128]{1,0:T(8,128)(2,1)S(1)}, u32[]{:S(2)}, u32[]{:S(2)}) %collective-permute-start.5) | collective-permute-done | bytes 262176 | tf_op jit(solution)/shard_map/ppermute | solution.py:432
  74.7 6.7 %collective-permute-done.4 = bf16[1024,128]{1,0:T(8,128)(2,1)S(1)} collective-permute-done((bf16[1024,128]{1,0:T(8,128)(2,1)S(1)}, bf16[1024,128]{1,0:T(8,128)(2,1)S(1)}, u32[]{:S(2)}, u32[]{:S(2)}) %collective-permute-start.4) | collective-permute-done | bytes 262176 | tf_op jit(solution)/shard_map/ppermute | solution.py:432
  81.5 1.4 %collective-permute-start.7 = (bf16[4,1024,128]{2,1,0:T(8,128)(2,1)S(1)}, bf16[4,1024,128]{2,1,0:T(8,128)(2,1)S(1)}, u32[]{:S(2)}, u32[]{:S(2)}) collective-permute-start(bf16[4,1024,128]{2,1,0:T(8,128)(2,1)S(1)} %pad_maximum_fusion.mine), channel_id=1, source_target_pairs={{0,16},{16,0},{1,17},{17,1},{2,18},{18,2},{3,19},{19,3},{4,20},{20... | collective-permute-start | bytes 3145736 | tf_op jit(solution)/shard_map/ppermute | solution.py:437
  83.0 1.0 collective-permute-start.11
  83.9 1.4 %collective-permute-start.10 = (bf16[128,128]{1,0:T(8,128)(2,1)S(1)}, bf16[128,128]{1,0:T(8,128)(2,1)S(1)}, u32[]{:S(2)}, u32[]{:S(2)}) collective-permute-start(bf16[128,128]{1,0:T(8,128)(2,1)S(1)} %copy-done.14), channel_id=1, source_target_pairs={{0,64},{32,96},{64,0},{96,32},{1,65},{33,97},{65,1},{97,33},{2,66}... | collective-permute-start | bytes 98312 | tf_op jit(solution)/shard_map/ppermute | solution.py:432
  85.7 2.5 %collective-permute-done.10 = bf16[128,128]{1,0:T(8,128)(2,1)S(1)} collective-permute-done((bf16[128,128]{1,0:T(8,128)(2,1)S(1)}, bf16[128,128]{1,0:T(8,128)(2,1)S(1)}, u32[]{:S(2)}, u32[]{:S(2)}) %collective-permute-start.10) | collective-permute-done | bytes 32800 | tf_op jit(solution)/shard_map/ppermute | solution.py:432
  88.2 1.7 %collective-permute-done.9 = bf16[128,128]{1,0:T(8,128)(2,1)S(1)} collective-permute-done((bf16[128,128]{1,0:T(8,128)(2,1)S(1)}, bf16[128,128]{1,0:T(8,128)(2,1)S(1)}, u32[]{:S(2)}, u32[]{:S(2)}) %collective-permute-start.9) | collective-permute-done | bytes 32800 | tf_op jit(solution)/shard_map/ppermute | solution.py:432
  89.9 1.6 %collective-permute-start.12 = (bf16[4,128,128]{2,1,0:T(8,128)(2,1)S(1)}, bf16[4,128,128]{2,1,0:T(8,128)(2,1)S(1)}, u32[]{:S(2)}, u32[]{:S(2)}) collective-permute-start(bf16[4,128,128]{2,1,0:T(8,128)(2,1)S(1)} %pad_maximum_fusion.1.own_tiles), channel_id=1, source_target_pairs={{0,16},{16,0},{1,17},{17,1},{2,18},{18,2},{3,19},{19,3},{4,20},{20... | collective-permute-start | bytes 393224 | tf_op jit(solution)/shard_map/ppermute | solution.py:437
  91.7 1.6 %copy-done.3 = bf16[2,2,1024,256]{3,2,1,0:T(8,128)(2,1)S(1)} copy-done((bf16[2,2,1024,256]{3,2,1,0:T(8,128)(2,1)S(1)}, bf16[2,2,1024,256]{3,2,1,0:T(8,128)(2,1)}, u32[]{:S(2)}) %copy-start.3) | copy-done | bytes 2097176
  93.3 12.7 %trail_first.1.partial = f32[2,2,1024,256]{3,2,1,0:T(8,128)} custom-call(s32[4]{0:T(128)S(1)} %copy-done.6, bf16[4,1024,128]{2,1,0:T(8,128)(2,1)S(1)} %pad_maximum_fusion.mine, bf16[4,1024,128]{2,1,0:T(8,128)(2,1)S(1)} %collective-permute-done.7.theirs, bf16[2,2,2,1024,1024]{4,3,2,1,0:T(8,128)(2,1)} %factor.5, bf16[2,2,1024,256]{3,2,1,0:T(8,128)(2,1)S(1)} %copy-done.3), custom_call_target="tpu_custom_call" | custom-call | tf_op jit(solution)/shard_map/trail_first/pallas_call | solution.py:241
  106.0 2.2 %copy-done.1 = f32[2,2,1024,256]{3,2,1,0:T(8,128)S(1)} copy-done((f32[2,2,1024,256]{3,2,1,0:T(8,128)S(1)}, f32[2,2,1024,256]{3,2,1,0:T(8,128)}, u32[]{:S(2)}) %copy-start.1) | copy-done | bytes 4194328
  108.2 7.5 %trail_second.2 = (bf16[2,2,1024,256]{3,2,1,0:T(8,128)(2,1)}, bf16[2,8,256]{2,1,0:T(8,128)(2,1)S(1)}) custom-call(s32[5]{0:T(128)S(1)} %concatenate.28.place, bf16[4,16,64,128]{3,2,1,0:T(8,128)(2,1)S(1)} %bitcast.23, bf16[2,2,2,1024,1024]{4,3,2,1,0:T(8,128)(2,1)} %factor.5, f32[2,2,1024,256]{3,2,1,0:T(8,128)S(1)} %copy-done.1), custom_call_target="tpu_custom_call" | custom-call | tf_op jit(solution)/shard_map/trail_second/pallas_call | solution.py:292
  115.7 1.7 %gradient_first.1.before = f32[8,128]{1,0:T(8,128)S(1)} custom-call(s32[4]{0:T(128)S(1)} %copy-done.6, bf16[4,1024,128]{2,1,0:T(8,128)(2,1)S(1)} %pad_maximum_fusion.mine, bf16[4,1024,128]{2,1,0:T(8,128)(2,1)S(1)} %collective-permute-done.7.theirs, bf16[4,128,128]{2,1,0:T(8,128)(2,1)S(1)} %pad_maximum_fusion.1.own_tiles, ...), custom_call_target="tpu_custom_call" | custom-call | tf_op jit(solution)/shard_map/gradient_first/pallas_call | solution.py:375
  117.4 7.5 %trail_second.3 = (bf16[2,2,1024,256]{3,2,1,0:T(8,128)(2,1)}, bf16[2,8,256]{2,1,0:T(8,128)(2,1)S(1)}) custom-call(s32[5]{0:T(128)S(1)} %concatenate.30.place, bf16[4,16,64,128]{3,2,1,0:T(8,128)(2,1)} %bitcast.17.blocks.theirs, bf16[2,2,2,1024,1024]{4,3,2,1,0:T(8,128)(2,1)} %factor.5, ...), custom_call_target="tpu_custom_call", output_to_operand_aliasing={{0}: (4, {})} | custom-call | tf_op jit(solution)/shard_map/trail_second/pallas_call | solution.py:292
  125.6 3.7 %gradient_second.1 = f32[3,8]{1,0:T(4,128)} custom-call(s32[4]{0:T(128)S(1)} %copy-done.6, bf16[4,16,64,128]{3,2,1,0:T(8,128)(2,1)S(1)} %bitcast.24, bf16[4,16,64,128]{3,2,1,0:T(8,128)(2,1)} %bitcast.17.blocks.theirs, bf16[4,128,128]{2,1,0:T(8,128)(2,1)S(1)} %pad_maximum_fusion.1.own_tiles, bf16[4,128,128]{2,1,0:T(8,128)(2,1)S(1)} %collective-permute-done.12.other_tiles, ...), custom_call_target="tpu_custom_call" | custom-call | tf_op jit(solution)/shard_map/gradient_second/pallas_call | solution.py:412
  (65 shorter events, 4.8 us)
Async XLA Ops:
  0.6 17.0 %copy-start = (s32[1024]{0:T(1024)S(1)}, s32[1024]{0:T(1024)}, u32[]{:S(2)}) copy-start(s32[1024]{0:T(1024)} %param.19) | copy-start | bytes 12292
  0.6 16.6 %copy-start.17 = (s32[2,8,3]{1,0,2:T(2,128)S(1)}, s32[2,8,3]{1,0,2:T(2,128)}, u32[]{:S(2)}) copy-start(s32[2,8,3]{1,0,2:T(2,128)} %param.18) | copy-start | bytes 580
  0.7 16.8 %copy-start.15 = (f32[2,9,2,8]{1,3,2,0:T(8,128)S(1)}, f32[2,9,2,8]{1,3,2,0:T(8,128)}, u32[]{:S(2)}) copy-start(f32[2,9,2,8]{1,3,2,0:T(8,128)} %param.17) | copy-start | bytes 3460
  4.6 25.6 %all-to-all-start = ((bf16[128,2,8,128]{3,2,1,0:T(8,128)(2,1)}), bf16[128,2,8,128]{3,2,1,0:T(8,128)(2,1)S(1)}, u32[]{:S(2)}, u32[]{:S(2)}) async-start(bf16[128,2,8,128]{3,2,1,0:T(8,128)(2,1)} %bitcast.27), calls=%async_computation | async-start | bytes 1048576 | tf_op jit(solution)/shard_map/all_to_all | solution.py:468
  16.1 2.4 %collective-permute-start = (bf16[2,8,1280]{2,1,0:T(8,128)(2,1)}, bf16[2,8,1280]{2,1,0:T(8,128)(2,1)S(1)}, u32[]{:S(2)}, u32[]{:S(2)}) collective-permute-start(bf16[2,8,1280]{2,1,0:T(8,128)(2,1)} %get-tuple-element.18), channel_id=1, source_target_pairs={{0,16},{16,0},{1,17},{17,1},{2,18},{18,2},{3,19},{19,3},{4,20},{20... | collective-permute-start | bytes 122888 | tf_op jit(solution)/shard_map/ppermute | solution.py:437
  17.6 0.9 copy-start.13
  18.6 11.7 %copy-start.8 = (bf16[2,2,8,1280]{3,2,1,0:T(8,128)(2,1)}, bf16[2,2,8,1280]{3,2,1,0:T(8,128)(2,1)S(1)}, u32[]{:S(2)}) copy-start(bf16[2,2,8,1280]{3,2,1,0:T(8,128)(2,1)S(1)} %maximum_select_fusion.rows0) | copy-start | bytes 245764
  18.6 6.3 %collective-permute-start.3 = (bf16[2,2,8,1280]{3,2,1,0:T(8,128)(2,1)S(1)}, bf16[2,2,8,1280]{3,2,1,0:T(8,128)(2,1)S(1)}, u32[]{:S(2)}, u32[]{:S(2)}) collective-permute-start(bf16[2,2,8,1280]{3,2,1,0:T(8,128)(2,1)S(1)} %maximum_select_fusion.rows0), channel_id=1, source_target_pairs={{0,96},{32,0},{64,32},{96,64},{1,97},{33,1},{65,33},{97,65},{2,98}... | collective-permute-start | bytes 245768 | tf_op jit(solution)/shard_map/ppermute | solution.py:432
  20.5 6.0 %collective-permute-start.2 = (bf16[2,2,8,1280]{3,2,1,0:T(8,128)(2,1)S(1)}, bf16[2,2,8,1280]{3,2,1,0:T(8,128)(2,1)S(1)}, u32[]{:S(2)}, u32[]{:S(2)}) collective-permute-start(bf16[2,2,8,1280]{3,2,1,0:T(8,128)(2,1)S(1)} %maximum_select_fusion.rows0), channel_id=1, source_target_pairs={{0,64},{32,96},{64,0},{96,32},{1,65},{33,97},{65,1},{97,33},{2,66}... | collective-permute-start | bytes 245768 | tf_op jit(solution)/shard_map/ppermute | solution.py:432
  21.1 7.3 %collective-permute-start.1 = (bf16[2,2,8,1280]{3,2,1,0:T(8,128)(2,1)S(1)}, bf16[2,2,8,1280]{3,2,1,0:T(8,128)(2,1)S(1)}, u32[]{:S(2)}, u32[]{:S(2)}) collective-permute-start(bf16[2,2,8,1280]{3,2,1,0:T(8,128)(2,1)S(1)} %maximum_select_fusion.rows0), channel_id=1, source_target_pairs={{0,32},{32,64},{64,96},{96,0},{1,33},{33,65},{65,97},{97,1},{2,34}... | collective-permute-start | bytes 245768 | tf_op jit(solution)/shard_map/ppermute | solution.py:432
  24.9 5.4 %copy-start.9 = (bf16[2,2,8,1280]{3,2,1,0:T(8,128)(2,1)}, bf16[2,2,8,1280]{3,2,1,0:T(8,128)(2,1)S(1)}, u32[]{:S(2)}) copy-start(bf16[2,2,8,1280]{3,2,1,0:T(8,128)(2,1)S(1)} %collective-permute-done.3.rows3) | copy-start | bytes 245764
  26.5 3.8 %copy-start.10 = (bf16[2,2,8,1280]{3,2,1,0:T(8,128)(2,1)}, bf16[2,2,8,1280]{3,2,1,0:T(8,128)(2,1)S(1)}, u32[]{:S(2)}) copy-start(bf16[2,2,8,1280]{3,2,1,0:T(8,128)(2,1)S(1)} %collective-permute-done.2.rows2) | copy-start | bytes 245764
  28.4 1.9 %copy-start.11 = (bf16[2,2,8,1280]{3,2,1,0:T(8,128)(2,1)}, bf16[2,2,8,1280]{3,2,1,0:T(8,128)(2,1)S(1)}, u32[]{:S(2)}) copy-start(bf16[2,2,8,1280]{3,2,1,0:T(8,128)(2,1)S(1)} %collective-permute-done.1.rows1) | copy-start | bytes 245764
  34.0 22.3 %copy-start.12 = (bf16[1024,128]{1,0:T(8,128)(2,1)S(1)}, bf16[1024,128]{1,0:T(8,128)(2,1)}, u32[]{:S(2)}) copy-start(bf16[1024,128]{1,0:T(8,128)(2,1)} %get-tuple-element.21) | copy-start | bytes 786436
  51.5 31.5 %copy-start.14 = (bf16[128,128]{1,0:T(8,128)(2,1)S(1)}, bf16[128,128]{1,0:T(8,128)(2,1)}, u32[]{:S(2)}) copy-start(bf16[128,128]{1,0:T(8,128)(2,1)} %get-tuple-element.26) | copy-start | bytes 98308
  51.5 40.2 %copy-start.6 = (s32[4]{0:T(128)S(1)}, s32[4]{0:T(128)}, u32[]{:S(2)}) copy-start(s32[4]{0:T(128)} %pad_add_fusion.place) | copy-start | bytes 52
  51.5 31.4 %all-to-all-start.2 = ((bf16[64,64,128]{2,1,0:T(8,128)(2,1)}), bf16[64,64,128]{2,1,0:T(8,128)(2,1)S(1)}, u32[]{:S(2)}, u32[]{:S(2)}) async-start(bf16[64,64,128]{2,1,0:T(8,128)(2,1)} %get-tuple-element.20), calls=%async_computation.2 | async-start | bytes 2097152 | tf_op jit(solution)/shard_map/all_to_all | solution.py:482
  56.3 16.8 %collective-permute-start.6 = (bf16[1024,128]{1,0:T(8,128)(2,1)S(1)}, bf16[1024,128]{1,0:T(8,128)(2,1)S(1)}, u32[]{:S(2)}, u32[]{:S(2)}) collective-permute-start(bf16[1024,128]{1,0:T(8,128)(2,1)S(1)} %copy-done.12), channel_id=1, source_target_pairs={{0,96},{32,0},{64,32},{96,64},{1,97},{33,1},{65,33},{97,65},{2,98}... | collective-permute-start | bytes 786440 | tf_op jit(solution)/shard_map/ppermute | solution.py:432
  58.8 15.9 %collective-permute-start.5 = (bf16[1024,128]{1,0:T(8,128)(2,1)S(1)}, bf16[1024,128]{1,0:T(8,128)(2,1)S(1)}, u32[]{:S(2)}, u32[]{:S(2)}) collective-permute-start(bf16[1024,128]{1,0:T(8,128)(2,1)S(1)} %copy-done.12), channel_id=1, source_target_pairs={{0,64},{32,96},{64,0},{96,32},{1,65},{33,97},{65,1},{97,33},{2,66}... | collective-permute-start | bytes 786440 | tf_op jit(solution)/shard_map/ppermute | solution.py:432
  59.1 22.2 %collective-permute-start.4 = (bf16[1024,128]{1,0:T(8,128)(2,1)S(1)}, bf16[1024,128]{1,0:T(8,128)(2,1)S(1)}, u32[]{:S(2)}, u32[]{:S(2)}) collective-permute-start(bf16[1024,128]{1,0:T(8,128)(2,1)S(1)} %copy-done.12), channel_id=1, source_target_pairs={{0,32},{32,64},{64,96},{96,0},{1,33},{33,65},{65,97},{97,1},{2,34}... | collective-permute-start | bytes 786440 | tf_op jit(solution)/shard_map/ppermute | solution.py:432
  81.5 10.2 %collective-permute-start.7 = (bf16[4,1024,128]{2,1,0:T(8,128)(2,1)S(1)}, bf16[4,1024,128]{2,1,0:T(8,128)(2,1)S(1)}, u32[]{:S(2)}, u32[]{:S(2)}) collective-permute-start(bf16[4,1024,128]{2,1,0:T(8,128)(2,1)S(1)} %pad_maximum_fusion.mine), channel_id=1, source_target_pairs={{0,16},{16,0},{1,17},{17,1},{2,18},{18,2},{3,19},{19,3},{4,20},{20... | collective-permute-start | bytes 3145736 | tf_op jit(solution)/shard_map/ppermute | solution.py:437
  82.9 34.5 %collective-permute-start.8 = (bf16[64,64,128]{2,1,0:T(8,128)(2,1)S(1)}, bf16[64,64,128]{2,1,0:T(8,128)(2,1)}, u32[]{:S(2)}, u32[]{:S(2)}) collective-permute-start(bf16[64,64,128]{2,1,0:T(8,128)(2,1)S(1)} %all-to-all-done.2), channel_id=1, source_target_pairs={{0,16},{16,0},{1,17},{17,1},{2,18},{18,2},{3,19},{19,3},{4,20},{20... | collective-permute-start | bytes 3145736 | tf_op jit(solution)/shard_map/ppermute | solution.py:437
  83.0 2.8 %collective-permute-start.11 = (bf16[128,128]{1,0:T(8,128)(2,1)S(1)}, bf16[128,128]{1,0:T(8,128)(2,1)S(1)}, u32[]{:S(2)}, u32[]{:S(2)}) collective-permute-start(bf16[128,128]{1,0:T(8,128)(2,1)S(1)} %copy-done.14), channel_id=1, source_target_pairs={{0,96},{32,0},{64,32},{96,64},{1,97},{33,1},{65,33},{97,65},{2,98}... | collective-permute-start | bytes 98312 | tf_op jit(solution)/shard_map/ppermute | solution.py:432
  83.9 4.3 %collective-permute-start.10 = (bf16[128,128]{1,0:T(8,128)(2,1)S(1)}, bf16[128,128]{1,0:T(8,128)(2,1)S(1)}, u32[]{:S(2)}, u32[]{:S(2)}) collective-permute-start(bf16[128,128]{1,0:T(8,128)(2,1)S(1)} %copy-done.14), channel_id=1, source_target_pairs={{0,64},{32,96},{64,0},{96,32},{1,65},{33,97},{65,1},{97,33},{2,66}... | collective-permute-start | bytes 98312 | tf_op jit(solution)/shard_map/ppermute | solution.py:432
  85.3 4.6 %collective-permute-start.9 = (bf16[128,128]{1,0:T(8,128)(2,1)S(1)}, bf16[128,128]{1,0:T(8,128)(2,1)S(1)}, u32[]{:S(2)}, u32[]{:S(2)}) collective-permute-start(bf16[128,128]{1,0:T(8,128)(2,1)S(1)} %copy-done.14), channel_id=1, source_target_pairs={{0,32},{32,64},{64,96},{96,0},{1,33},{33,65},{65,97},{97,1},{2,34}... | collective-permute-start | bytes 98312 | tf_op jit(solution)/shard_map/ppermute | solution.py:432
  89.9 25.7 %collective-permute-start.12 = (bf16[4,128,128]{2,1,0:T(8,128)(2,1)S(1)}, bf16[4,128,128]{2,1,0:T(8,128)(2,1)S(1)}, u32[]{:S(2)}, u32[]{:S(2)}) collective-permute-start(bf16[4,128,128]{2,1,0:T(8,128)(2,1)S(1)} %pad_maximum_fusion.1.own_tiles), channel_id=1, source_target_pairs={{0,16},{16,0},{1,17},{17,1},{2,18},{18,2},{3,19},{19,3},{4,20},{20... | collective-permute-start | bytes 393224 | tf_op jit(solution)/shard_map/ppermute | solution.py:437
  91.7 1.6 %copy-start.3 = (bf16[2,2,1024,256]{3,2,1,0:T(8,128)(2,1)S(1)}, bf16[2,2,1024,256]{3,2,1,0:T(8,128)(2,1)}, u32[]{:S(2)}) copy-start(bf16[2,2,1024,256]{3,2,1,0:T(8,128)(2,1)} %rhs.3) | copy-start | bytes 6291460
  106.0 2.2 %copy-start.1 = (f32[2,2,1024,256]{3,2,1,0:T(8,128)S(1)}, f32[2,2,1024,256]{3,2,1,0:T(8,128)}, u32[]{:S(2)}) copy-start(f32[2,2,1024,256]{3,2,1,0:T(8,128)} %trail_first.1.partial) | copy-start | bytes 12582916
  108.2 7.5 %copy-start.5 = (bf16[128,384]{1,0:T(8,128)(2,1)S(1)}, bf16[128,384]{1,0:T(8,128)(2,1)}, u32[]{:S(2)}) copy-start(bf16[128,384]{1,0:T(8,128)(2,1)} %constant.57.clone.spread) | copy-start | bytes 294916
  108.2 9.2 %copy-start.2 = (f32[2,2,1024,256]{3,2,1,0:T(8,128)S(1)}, f32[2,2,1024,256]{3,2,1,0:T(8,128)}, u32[]{:S(2)}) copy-start(f32[2,2,1024,256]{3,2,1,0:T(8,128)} %trail_first.1.partial) | copy-start | bytes 12582916
  117.4 7.6 %copy-start.16 = (bf16[2,2,8,256]{3,2,1,0:T(8,128)(2,1)S(1)}, bf16[2,2,8,256]{3,2,1,0:T(8,128)(2,1)}, u32[]{:S(2)}) copy-start(bf16[2,2,8,256]{3,2,1,0:T(8,128)(2,1)} %get-tuple-element.15) | copy-start | bytes 49156
  117.4 8.2 %copy-start.4 = (bf16[128,384]{1,0:T(8,128)(2,1)S(1)}, bf16[128,384]{1,0:T(8,128)(2,1)}, u32[]{:S(2)}) copy-start(bf16[128,384]{1,0:T(8,128)(2,1)} %constant.58.clone.spread) | copy-start | bytes 294916
  (1 other events, 0.8 us)

commit v4 on v3

v4 whole, which is shorter than its diff:
```python
import jax
import jax.numpy as jnp
import numpy as np
from jax import lax
from jax.experimental import pallas as pl
from jax.experimental.pallas import tpu as pltpu
from jax.sharding import Mesh
from jax.sharding import PartitionSpec as P


ALL = ("x", "core", "col")
F32 = jnp.float32
BF16 = jnp.bfloat16
VMEM_LIMIT = 48 * 1024 * 1024
HEIGHT = 256


def lanes_below(shape, bound):
    return lax.broadcasted_iota(jnp.int32, shape, len(shape) - 1) < bound


def pair_lanes(left, right):
    low = lanes_below(left.shape, 64)
    real = jnp.where(low, left, pltpu.roll(right, 64, 1))
    imag = jnp.where(low, pltpu.roll(left, 64, 1), right)
    return real, imag


def fold_parts(top, low):
    turned = pltpu.roll(low, 64, 1)
    return top + jnp.where(lanes_below(low.shape, 64), -turned, turned)


def prepare_kernel(place, inverse, rhs, below, own_rhs, first, send, own, give):
    system = pl.program_id(0)
    left = jnp.concatenate([inverse[0, 0, 0].astype(F32), inverse[0, 0, 1].astype(F32)]).astype(BF16)
    by_real = jnp.dot(left, rhs[0, 0], preferred_element_type=F32)
    by_imag = jnp.dot(left, rhs[0, 1], preferred_element_type=F32)
    real = (by_real[:8] - by_imag[8:]).astype(BF16)
    imag = (by_imag[:8] + by_real[8:]).astype(BF16)
    first[0, 0] = real
    first[0, 1] = imag
    real = real.astype(F32)
    imag = imag.astype(F32)
    for half in range(2):
        cut = slice(128 * half, 128 * half + 128)
        even, odd = pair_lanes(real[:, cut], imag[:, cut])
        for group, value in ((2 * half, even), (2 * half + 1, odd)):
            value = value.astype(BF16)
            for col in range(16):
                send[group, 0, col, 0] = value
    lane_block = lax.broadcasted_iota(jnp.int32, (8, 128), 1) // 8
    pieces = [
        below[0, part, :, 128 * row : 128 * row + 128].astype(F32)
        for part in range(2)
        for row in range(8)
    ]
    for col in range(16):
        value = pltpu.roll(pieces[0], (128 - 8 * col) % 128, 1)
        for block in range(1, 16):
            turned = pltpu.roll(pieces[block], (8 * block - 8 * col) % 128, 1)
            value = jnp.where(lane_block == block, turned, value)
        value = value.astype(BF16)
        for group in range(4):
            send[group, 0, col, 1] = value

    def fill(target):
        for part in range(2):
            target[part, :, :1024] = inverse[0, 1, part]
            target[part, :, 1024:] = own_rhs[0, part]

    @pl.when(system == place[1])
    def _():
        fill(own)

    @pl.when(system != place[1])
    def _():
        fill(give)


def prepare(place, panel_inverse, first_rhs, panel_below, second_rhs):
    return pl.pallas_call(
        prepare_kernel,
        grid_spec=pltpu.PrefetchScalarGridSpec(
            num_scalar_prefetch=1,
            grid=(2,),
            in_specs=[
                pl.BlockSpec((1, 2, 2, 8, 1024), lambda s, _: (s, 0, 0, 0, 0)),
                pl.BlockSpec((1, 2, 1024, 256), lambda s, _: (s, 0, 0, 0)),
                pl.BlockSpec((1, 2, 8, 1024), lambda s, _: (s, 0, 0, 0)),
                pl.BlockSpec((1, 2, 8, 256), lambda s, _: (s, 0, 0, 0)),
            ],
            out_specs=[
                pl.BlockSpec((1, 2, 8, 256), lambda s, _: (s, 0, 0, 0)),
                pl.BlockSpec((4, 1, 16, 2, 8, 128), lambda s, _: (0, s, 0, 0, 0, 0)),
                pl.BlockSpec((2, 8, 1280), lambda s, _: (0, 0, 0)),
                pl.BlockSpec((2, 8, 1280), lambda s, _: (0, 0, 0)),
            ],
        ),
        out_shape=[
            jax.ShapeDtypeStruct((2, 2, 8, 256), BF16),
            jax.ShapeDtypeStruct((4, 2, 16, 2, 8, 128), BF16),
            jax.ShapeDtypeStruct((2, 8, 1280), BF16),
            jax.ShapeDtypeStruct((2, 8, 1280), BF16),
        ],
        name="prepare",
    )(place, panel_inverse, first_rhs, panel_below, second_rhs)


def right_kernel(place, received, rows0, rows1, rows2, rows3, block, send, offset):
    x = place[0]
    half = pl.multiple_of(1024 + 128 * (x // 2), 128)
    odd = x % 2 == 1
    for step, rows in enumerate((rows0, rows1, rows2, rows3)):
        source = lax.rem(x - step + 4, 4)
        for core in range(2):
            real = rows[core, 0, :, pl.ds(half, 128)].astype(F32)
            imag = rows[core, 1, :, pl.ds(half, 128)].astype(F32)
            even_pair, odd_pair = pair_lanes(real, imag)
            value = jnp.where(odd, odd_pair, even_pair)
            offset[pl.ds(pl.multiple_of(16 * source + 8 * core, 8), 8), :] = value
    first = received[:, 0].astype(F32).reshape(1024, 128).astype(BF16)
    below = received[:, 1].astype(F32).reshape(1024, 128).astype(BF16)
    block[...] = first
    product = lax.dot_general(below, first, (((0,), (0,)), ((), ())), preferred_element_type=F32)
    right = (offset[...] - fold_parts(product[:64], product[64:])).astype(BF16)
    for col in range(16):
        send[col] = right


def right_side(place, received, rows):
    return pl.pallas_call(
        right_kernel,
        grid_spec=pltpu.PrefetchScalarGridSpec(
            num_scalar_prefetch=1,
            grid=(1,),
            in_specs=[pl.BlockSpec((128, 2, 8, 128), lambda i, _: (0, 0, 0, 0))]
            + [pl.BlockSpec((2, 2, 8, 1280), lambda i, _: (0, 0, 0, 0))] * 4,
            out_specs=[
                pl.BlockSpec((1024, 128), lambda i, _: (0, 0)),
                pl.BlockSpec((16, 64, 128), lambda i, _: (0, 0, 0)),
            ],
            scratch_shapes=[pltpu.VMEM((64, 128), F32)],
        ),
        out_shape=[
            jax.ShapeDtypeStruct((1024, 128), BF16),
            jax.ShapeDtypeStruct((16, 64, 128), BF16),
        ],
        name="right_side",
    )(place, received, *rows)


def second_kernel(place, received, rows0, rows1, rows2, rows3, tile, send):
    x = place[0]
    right = received[...].astype(F32).reshape(16, 8, 8, 128)
    right = right.transpose(1, 0, 2, 3).reshape(1024, 128).astype(BF16)
    pieces = [
        rows[core, part, :, :1024].astype(F32)
        for part in range(2)
        for rows in (rows0, rows1, rows2, rows3)
        for core in range(2)
    ]
    left = jnp.concatenate(pieces).astype(BF16)
    product = jnp.dot(left, right, preferred_element_type=F32)
    value = fold_parts(product[:64], product[64:]).astype(BF16)
    for step in range(4):
        target = pl.multiple_of(16 * lax.rem(x - step + 4, 4), 16)
        part = value[16 * step : 16 * step + 16]
        for copy in range(64):
            send[copy, pl.ds(target, 16), :] = part
    for copy in range(64):
        send[copy, 64:] = tile[...]


def second_rows(place, received, rows, tile):
    return pl.pallas_call(
        second_kernel,
        grid_spec=pltpu.PrefetchScalarGridSpec(
            num_scalar_prefetch=1,
            grid=(1,),
            in_specs=[pl.BlockSpec((16, 64, 128), lambda i, _: (0, 0, 0))]
            + [pl.BlockSpec((2, 2, 8, 1280), lambda i, _: (0, 0, 0, 0))] * 4
            + [pl.BlockSpec((8, 128), lambda i, _: (0, 0))],
            out_specs=pl.BlockSpec((64, 72, 128), lambda i, _: (0, 0, 0)),
        ),
        out_shape=jax.ShapeDtypeStruct((64, 72, 128), BF16),
        name="second_rows",
    )(place, received, *rows, tile)


def trail_product(factor, blocks):
    height = factor.shape[3]
    stacked = factor[0, 0].reshape(2 * height, 1024)
    product = jnp.dot(stacked, blocks[...], preferred_element_type=F32)
    real, imag = [], []
    for half in range(2):
        lanes = slice(256 * half, 256 * half + 128)
        even, even_turned = product[:height, lanes], product[height:, lanes]
        lanes = slice(256 * half + 128, 256 * half + 256)
        odd, odd_turned = product[:height, lanes], product[height:, lanes]
        low = lanes_below(even.shape, 64)
        turn = lambda value: pltpu.roll(value, 64, 1)
        real.append(jnp.where(low, even - turn(even_turned), turn(odd) - odd_turned))
        imag.append(jnp.where(low, turn(even) + even_turned, odd + turn(odd_turned)))
    return jnp.concatenate(real, axis=1), jnp.concatenate(imag, axis=1)


def trail_first_kernel(place, mine, theirs, factor, rhs, out, blocks):
    x = place[0]
    turn = pl.program_id(0)

    @pl.when((turn == 0) & (pl.program_id(1) == 0))
    def _():
        for q in range(4):
            blocks[:, 128 * q : 128 * q + 128] = mine[lax.rem(x - q + 4, 4)]

    @pl.when((turn == 1) & (pl.program_id(1) == 0))
    def _():
        for q in range(4):
            blocks[:, 128 * q : 128 * q + 128] = theirs[lax.rem(x - q + 4, 4)]

    real, imag = trail_product(factor, blocks)
    out[0, 0] = rhs[0, 0].astype(F32) - real
    out[0, 1] = rhs[0, 1].astype(F32) - imag


def trail_first(place, mine, theirs, trail_factor, trail_rhs):
    rows = trail_rhs.shape[2]
    height = min(HEIGHT, rows)
    system = lambda turn, p: jnp.where(turn == 0, p[1], 1 - p[1])
    return pl.pallas_call(
        trail_first_kernel,
        grid_spec=pltpu.PrefetchScalarGridSpec(
            num_scalar_prefetch=1,
            grid=(2, rows // height),
            in_specs=[pl.BlockSpec((4, 1024, 128), lambda t, i, p: (0, 0, 0))] * 2
            + [
                pl.BlockSpec((1, 1, 2, height, 1024), lambda t, i, p: (system(t, p), 0, 0, i, 0)),
                pl.BlockSpec((1, 2, height, 256), lambda t, i, p: (system(t, p), 0, i, 0)),
            ],
            out_specs=pl.BlockSpec((1, 2, height, 256), lambda t, i, p: (system(t, p), 0, i, 0)),
            scratch_shapes=[pltpu.VMEM((1024, 512), BF16)],
        ),
        out_shape=jax.ShapeDtypeStruct((2, 2, rows, 256), F32),
        compiler_params=pltpu.CompilerParams(vmem_limit_bytes=VMEM_LIMIT),
        name="trail_first",
    )(place, mine, theirs, trail_factor, trail_rhs)


def trail_second_kernel(place, received, factor, partial, *refs):
    out, own, blocks = refs[-3:]

    @pl.when(pl.program_id(0) == 0)
    def _():
        for q in range(4):
            for row in range(8):
                value = received[q, :, 8 * row : 8 * row + 8, :].astype(F32).reshape(128, 128)
                blocks[128 * row : 128 * row + 128, 128 * q : 128 * q + 128] = value.astype(BF16)
        near = pl.multiple_of(8 * place[3], 8)
        parts = [received[q, place[4], pl.ds(near, 8), :].astype(F32) for q in range(4)]
        for half in range(2):
            real, imag = pair_lanes(parts[2 * half], parts[2 * half + 1])
            own[0, :, 128 * half : 128 * half + 128] = real.astype(BF16)
            own[1, :, 128 * half : 128 * half + 128] = imag.astype(BF16)

    real, imag = trail_product(factor, blocks)
    out[0, 0] = (partial[0, 0] - real).astype(BF16)
    out[0, 1] = (partial[0, 1] - imag).astype(BF16)


def trail_second(place, which, received, trail_factor, partial, previous=None):
    rows = partial.shape[2]
    height = min(HEIGHT, rows)
    place = jnp.concatenate([place[:2], which[None], place[2:]])
    extra = () if previous is None else (previous,)
    return pl.pallas_call(
        trail_second_kernel,
        grid_spec=pltpu.PrefetchScalarGridSpec(
            num_scalar_prefetch=1,
            grid=(rows // height,),
            in_specs=[
                pl.BlockSpec((4, 16, 72, 128), lambda i, p: (0, 0, 0, 0)),
                pl.BlockSpec((1, 1, 2, height, 1024), lambda i, p: (p[2], 1, 0, i, 0)),
                pl.BlockSpec((1, 2, height, 256), lambda i, p: (p[2], 0, i, 0)),
            ]
            + [pl.BlockSpec(memory_space=pl.ANY)] * len(extra),
            out_specs=[
                pl.BlockSpec((1, 2, height, 256), lambda i, p: (p[2], 0, i, 0)),
                pl.BlockSpec((2, 8, 256), lambda i, p: (0, 0, 0)),
            ],
            scratch_shapes=[pltpu.VMEM((1024, 512), BF16)],
        ),
        out_shape=[
            jax.ShapeDtypeStruct((2, 2, rows, 256), BF16),
            jax.ShapeDtypeStruct((2, 8, 256), BF16),
        ],
        input_output_aliases={4: 0} if extra else {},
        compiler_params=pltpu.CompilerParams(vmem_limit_bytes=VMEM_LIMIT),
        name="trail_second",
    )(place, received, trail_factor, partial, *extra)


def spread_matrix():
    spread = np.zeros((128, 2, 3, 128), np.float32)
    for panel in range(2):
        for corner in range(3):
            for coordinate in range(3):
                lanes = slice(24 * corner + 8 * coordinate, 24 * corner + 8 * coordinate + 8)
                for part in range(2):
                    source = 18 * part + 9 * panel + 3 * corner + coordinate
                    for term in range(3):
                        spread[36 * term + source, panel, part, lanes] = 1.0
                spread[108 + 3 * panel + corner, panel, 2, lanes] = 32.0
                spread[114 + 3 * panel + corner, panel, 2, lanes] = 1.0
    return jnp.asarray(spread.reshape(128, 768), BF16)


def couple(pairs):
    same = jnp.zeros((128, 128), F32)
    crossed = jnp.zeros((128, 128), F32)
    for mine, theirs in pairs:
        mine = mine.astype(F32).reshape(128, 128)
        theirs = theirs.astype(F32).reshape(128, 128)
        same = same + mine * theirs
        crossed = crossed + mine * pltpu.roll(theirs, 64, 1)
    low = lanes_below((128, 128), 64)
    real = jnp.sum(jnp.where(low, same, -same), axis=1, keepdims=True)
    imag = jnp.sum(crossed, axis=1, keepdims=True)
    return real, imag


def couple_first_kernel(mine, theirs, out):
    low = lanes_below((128, 128), 64)
    for row in range(8):
        cut = slice(128 * row, 128 * row + 128)
        real, imag = couple((mine[q, cut, :], theirs[q, cut, :]) for q in range(4))
        out[cut, :] = jnp.where(low, real, imag)


def couple_first(mine, theirs):
    return pl.pallas_call(
        couple_first_kernel,
        out_shape=jax.ShapeDtypeStruct((1024, 128), F32),
        compiler_params=pltpu.CompilerParams(vmem_limit_bytes=VMEM_LIMIT),
        name="couple_first",
    )(mine, theirs)


def gradient_kernel(place, mine, theirs, before, spread, out):
    base = 8 * (16 * place[2] + place[3])
    target = (base + lax.rem(lax.broadcasted_iota(jnp.int32, (128, 128), 1), 8)).astype(F32)
    total = jnp.zeros((8, 128), F32)
    for source in range(4):
        for side in range(2):
            near, _ = (mine, theirs) if side == 0 else (theirs, mine)
            row = 2 * source + (place[1] if side == 0 else 1 - place[1])
            cut = pl.ds(pl.multiple_of(8 * row, 8), 8)
            real, imag = couple((mine[q, :, cut, :], theirs[q, :, cut, :]) for q in range(4))
            first = before[pl.ds(pl.multiple_of(128 * row, 128), 128), :]
            tile = near[source, :, 64:, :].astype(F32).reshape(128, 128).astype(BF16)
            table = jnp.dot(tile, spread[...], preferred_element_type=F32)
            for at, real, imag in ((0, first[:, :1], first[:, 64:65]), (384, real, imag)):
                value = table[:, at + 128 : at + 256] * imag - table[:, at : at + 128] * real
                value = jnp.where(table[:, at + 256 : at + 384] == target, value, 0.0)
                total = total + jnp.sum(value.reshape(16, 8, 128), axis=0)
    total = jnp.sum(total, axis=0, keepdims=True)
    total = total + pltpu.roll(total, 104, 1) + pltpu.roll(total, 80, 1)
    for coordinate in range(3):
        out[coordinate : coordinate + 1, :] = total[:, 8 * coordinate : 8 * coordinate + 8]


def gradient_of(place, mine, theirs, before, spread):
    return pl.pallas_call(
        gradient_kernel,
        grid_spec=pltpu.PrefetchScalarGridSpec(
            num_scalar_prefetch=1,
            grid=(1,),
            in_specs=[pl.BlockSpec((4, 16, 72, 128), lambda i, p: (0, 0, 0, 0))] * 2
            + [
                pl.BlockSpec((1024, 128), lambda i, p: (0, 0)),
                pl.BlockSpec((128, 768), lambda i, p: (0, 0)),
            ],
            out_specs=pl.BlockSpec((3, 8), lambda i, p: (0, 0)),
        ),
        out_shape=jax.ShapeDtypeStruct((3, 8), F32),
        compiler_params=pltpu.CompilerParams(vmem_limit_bytes=VMEM_LIMIT),
        name="gradient",
    )(place, mine, theirs, before, spread)


def rounds_x(value):
    sent = [lax.ppermute(value, "x", [(i, (i + step) % 4) for i in range(4)]) for step in (1, 2, 3)]
    return [value, *sent]


def swap_core(value):
    return lax.ppermute(value, "core", [(0, 1), (1, 0)])


def element_tile(shape_tiles, element_vertices, vertex_slot):
    values = shape_tiles.transpose(3, 0, 2, 1).reshape(8, 36)
    high = lax.reduce_precision(values, 8, 7)
    rest = values - high
    mid = lax.reduce_precision(rest, 8, 7)
    low = rest - mid
    slots = vertex_slot[element_vertices].transpose(1, 0, 2).reshape(8, 6)
    parts = [high, mid, low, (slots // 32).astype(F32), (slots % 32).astype(F32), jnp.zeros((8, 8), F32)]
    return jnp.concatenate(parts, axis=1).astype(BF16)


def steps(
    panel_inverse,
    panel_below,
    trail_factor,
    first_rhs,
    second_rhs,
    trail_rhs,
    shape_tiles,
    element_vertices,
    vertex_slot,
):
    x = lax.axis_index("x")
    core = lax.axis_index("core")
    col = lax.axis_index("col")
    place = jnp.stack([x, core, 2 * x + core, col]).astype(jnp.int32)

    first, send, own, give = prepare(place, panel_inverse, first_rhs, panel_below, second_rhs)
    received = lax.all_to_all(send.reshape(128, 2, 8, 128), ALL, 0, 0, tiled=True)

    other = swap_core(give)
    chip = jnp.where(core == 0, jnp.stack([own, other]), jnp.stack([other, own]))
    rows = rounds_x(chip)
    tile = element_tile(shape_tiles, element_vertices, vertex_slot)

    first_block, send = right_side(place, received, rows)
    received = lax.all_to_all(send, "col", 0, 0, tiled=True)
    first_mine = rounds_x(first_block)
    first_mine = jnp.stack(first_mine)
    first_theirs = swap_core(first_mine)

    send = second_rows(place, received, rows, tile)
    second_mine = lax.all_to_all(send, ("x", "col"), 0, 0, tiled=True)

    partial = trail_first(place, first_mine, first_theirs, trail_factor, trail_rhs)
    partial = pltpu.with_memory_space_constraint(partial, pltpu.HBM)
    before = couple_first(first_mine, first_theirs)

    second_theirs = swap_core(second_mine)
    mine = second_mine.reshape(4, 16, 72, 128)
    theirs = second_theirs.reshape(4, 16, 72, 128)
    update, own_mine = trail_second(place, core, mine, trail_factor, partial)
    update, own_theirs = trail_second(place, 1 - core, theirs, trail_factor, partial, update)
    gradient = gradient_of(place, mine, theirs, before, spread_matrix())

    second = jnp.where(
        core == 0, jnp.stack([own_mine, own_theirs]), jnp.stack([own_theirs, own_mine])
    )
    return (jnp.stack([first, second], axis=1), update, gradient)


def solution(mesh):
    fine = Mesh(mesh.devices.reshape(4, 2, 16), ALL)
    return jax.shard_map(
        steps,
        mesh=fine,
        in_specs=(
            P(None, None, None, ALL, None),
            P(None, None, ALL, None),
            P(None, None, None, ALL, None),
            P(),
            P(None, None, ALL, None),
            P(None, None, ALL, None),
            P(None, None, None, ALL),
            P(None, ALL, None),
            P(),
        ),
        out_specs=(
            P(None, None, None, ALL, None),
            P(None, None, ALL, None),
            P(None, ALL),
        ),
        check_vma=False,
    )
```

time: 130 us -> 122 us (0.938)
  blocking collectives: 14.3 us -> 0 us
  starting transfers between devices: 29.5 us -> 40 us
  waiting for transfers between devices: 34 us -> 30.8 us
  local copies, waits for them, and re-layouts: 6.64 us -> 4.38 us
  other arithmetic: 1.42 us -> 3.44 us
    ppermute x9 -> x6, waiting for transfers between devices: 32.1 us -> 5.14 us  [rounds_x(): lax.ppermute(value, 'x', [(i, (i + step) % 4) for i in range(4)])]
    all_to_all x1 -> x0, blocking collectives: 14.3 us -> none  [steps(): received = lax.all_to_all(send, 'col', 0, 0, tiled=True)]
    all_to_all x1, waiting for transfers between devices: 0.01 us -> 14 us  [steps(): second_mine = lax.all_to_all(send, ('x', 'col'), 0, 0, tiled=True)]
    ppermute x4 -> x3, starting transfers between devices: 4.23 us -> 11.3 us  [swap_core(): return lax.ppermute(value, 'core', [(0, 1), (1, 0)])]
    all_to_all x0 -> x1, waiting for transfers between devices: none -> 6.77 us  [steps(): received = lax.all_to_all(send, 'col', 0, 0, tiled=True)]
    all_to_all x0 -> x1, starting transfers between devices: none -> 5.93 us  [steps(): received = lax.all_to_all(send, 'col', 0, 0, tiled=True)]
    ppermute x4 -> x3, waiting for transfers between devices: 0.01 us -> 3.14 us  [swap_core(): return lax.ppermute(value, 'core', [(0, 1), (1, 0)])]
    ppermute x9 -> x6, starting transfers between devices: 9.03 us -> 6.66 us  [rounds_x(): lax.ppermute(value, 'x', [(i, (i + step) % 4) for i in range(4)])]
  transfers between devices with their start and end apart: 15 -> 12, of which waited for: 10 -> 8; matrix products, arithmetic and copies ran while one was open for 2% -> 3% of each run, Pallas kernels for 17% -> 18%
where the time goes in v4:
time: 122 us; the launch traced here: 121 us
  Pallas kernels  41.4 us (34%)
  starting transfers between devices  40 us (33%)
  waiting for transfers between devices  30.8 us (25%)
  local copies, waits for them, and re-layouts  4.38 us (4%)
  other arithmetic  3.44 us (3%)
    pallas_call x2, Pallas kernels, trail_second(): pl.pallas_call(trail_second_kernel, grid_spec=pltpu.PrefetchScalarGridSpe...  14.4 us
    all_to_all x1, waiting for transfers between devices, steps(): second_mine = lax.all_to_all(send, ('x', 'col'), 0, 0, tiled=True)  14 us
    pallas_call x1, Pallas kernels, trail_first(): pl.pallas_call(trail_first_kernel, grid_spec=pltpu.PrefetchScalarGridSpec...  12.4 us
    all_to_all x1, starting transfers between devices, steps(): lax.all_to_all(send.reshape(128, 2, 8, 128), ALL, 0, 0, tiled=True)  11.5 us
    ppermute x3, starting transfers between devices, swap_core(): return lax.ppermute(value, 'core', [(0, 1), (1, 0)])  11.3 us
    all_to_all x1, waiting for transfers between devices, steps(): received = lax.all_to_all(send, 'col', 0, 0, tiled=True)  6.77 us
    ppermute x6, starting transfers between devices, rounds_x(): lax.ppermute(value, 'x', [(i, (i + step) % 4) for i in range(4)])  6.66 us
    all_to_all x1, starting transfers between devices, steps(): received = lax.all_to_all(send, 'col', 0, 0, tiled=True)  5.93 us
  transfers between devices with their start and end apart: 12, of which 8 were waited for; matrix products, arithmetic and copies ran while one was open for 3% of the time, Pallas kernels for 18%

profile of v4, /device:TPU:1, one launch (start us, length us, event | category | flops | bytes accessed | tf_op | source)
XLA Modules:
  0.0 120.9 jit_solution(10812302351006953825)
XLA Ops:
  1.3 3.4 %prepare.1 = (bf16[2,2,8,256]{3,2,1,0:T(8,128)(2,1)}, bf16[4,2,16,2,8,128]{5,4,3,2,1,0:T(8,128)(2,1)}, bf16[2,8,1280]{2,1,0:T(8,128)(2,1)}, bf16[2,8,1280]{2,1,0:T(8,128)(2,1)}) custom-call(s32[4]{0:T(128)} %pad_add_fusion.place, bf16[2,2,2,8,1024]{4,3,2,1,0:T(8,128)(2,1)} %inverse.1, bf16[2,2,1024,256]{3,2,1,0:T(8,128)(2,1)} %rhs.2, ...), custom_call_target="tpu_custom_call" | custom-call | tf_op jit(solution)/shard_map/prepare/pallas_call | solution.py:82
  4.6 11.5 %all-to-all-start = ((bf16[128,2,8,128]{3,2,1,0:T(8,128)(2,1)}), bf16[128,2,8,128]{3,2,1,0:T(8,128)(2,1)S(1)}, u32[]{:S(2)}, u32[]{:S(2)}) async-start(bf16[128,2,8,128]{3,2,1,0:T(8,128)(2,1)} %bitcast.25), calls=%async_computation | async-start | bytes 1048576 | tf_op jit(solution)/shard_map/all_to_all | solution.py:428
  16.1 1.1 collective-permute-start
  17.5 0.9 collective-permute-done
  18.4 0.9 maximum_select_fusion.rows0
  19.2 2.0 %collective-permute-start.3 = (bf16[2,2,8,1280]{3,2,1,0:T(8,128)(2,1)S(1)}, bf16[2,2,8,1280]{3,2,1,0:T(8,128)(2,1)S(1)}, u32[]{:S(2)}, u32[]{:S(2)}) collective-permute-start(bf16[2,2,8,1280]{3,2,1,0:T(8,128)(2,1)S(1)} %maximum_select_fusion.rows0), channel_id=1, source_target_pairs={{0,96},{32,0},{64,32},{96,64},{1,97},{33,1},{65,33},{97,65},{2,98}... | collective-permute-start | bytes 245768 | tf_op jit(solution)/shard_map/ppermute | solution.py:392
  22.4 0.7 gather_fusion
  23.3 1.6 %collective-permute-done.3.rows3 = bf16[2,2,8,1280]{3,2,1,0:T(8,128)(2,1)S(1)} collective-permute-done((bf16[2,2,8,1280]{3,2,1,0:T(8,128)(2,1)S(1)}, bf16[2,2,8,1280]{3,2,1,0:T(8,128)(2,1)S(1)}, u32[]{:S(2)}, u32[]{:S(2)}) %collective-permute-start.3) | collective-permute-done | bytes 81952 | tf_op jit(solution)/shard_map/ppermute | solution.py:392
  24.9 1.4 %collective-permute-done.2.rows2 = bf16[2,2,8,1280]{3,2,1,0:T(8,128)(2,1)S(1)} collective-permute-done((bf16[2,2,8,1280]{3,2,1,0:T(8,128)(2,1)S(1)}, bf16[2,2,8,1280]{3,2,1,0:T(8,128)(2,1)S(1)}, u32[]{:S(2)}, u32[]{:S(2)}) %collective-permute-start.2) | collective-permute-done | bytes 81952 | tf_op jit(solution)/shard_map/ppermute | solution.py:392
  26.3 2.1 %collective-permute-done.1.rows1 = bf16[2,2,8,1280]{3,2,1,0:T(8,128)(2,1)S(1)} collective-permute-done((bf16[2,2,8,1280]{3,2,1,0:T(8,128)(2,1)S(1)}, bf16[2,2,8,1280]{3,2,1,0:T(8,128)(2,1)S(1)}, u32[]{:S(2)}, u32[]{:S(2)}) %collective-permute-start.1) | collective-permute-done | bytes 81952 | tf_op jit(solution)/shard_map/ppermute | solution.py:392
  28.4 1.7 %all-to-all-done.received = bf16[128,2,8,128]{3,2,1,0:T(8,128)(2,1)S(1)} async-done(((bf16[128,2,8,128]{3,2,1,0:T(8,128)(2,1)}), bf16[128,2,8,128]{3,2,1,0:T(8,128)(2,1)S(1)}, u32[]{:S(2)}, u32[]{:S(2)}) %all-to-all-start) | async-done | bytes 524320 | tf_op jit(solution)/shard_map/all_to_all | solution.py:428
  30.2 0.8 copy-done.4
  31.0 2.9 %right_side.1 = (bf16[1024,128]{1,0:T(8,128)(2,1)}, bf16[16,64,128]{2,1,0:T(8,128)(2,1)}) custom-call(s32[4]{0:T(128)} %pad_add_fusion.place, bf16[128,2,8,128]{3,2,1,0:T(8,128)(2,1)} %copy-done.4, bf16[2,2,8,1280]{3,2,1,0:T(8,128)(2,1)} %copy-done.6, bf16[2,2,8,1280]{3,2,1,0:T(8,128)(2,1)} %copy-done.9, bf16[2,2,8,1280]{3,2,1,0:T(8,128)(2,1)} %copy-done.8, ...), custom_call_target="tpu_custom_call" | custom-call | tf_op jit(solution)/shard_map/right_side/pallas_call | solution.py:132
  33.9 5.9 %all-to-all-start.1 = ((bf16[16,64,128]{2,1,0:T(8,128)(2,1)}), bf16[16,64,128]{2,1,0:T(8,128)(2,1)S(1)}, u32[]{:S(2)}, u32[]{:S(2)}) async-start(bf16[16,64,128]{2,1,0:T(8,128)(2,1)} %get-tuple-element.17), calls=%async_computation.1 | async-start | bytes 524288 | tf_op jit(solution)/shard_map/all_to_all | solution.py:436
  40.0 0.7 concatenate.29.tile
  40.6 6.8 %all-to-all-done.1.received = bf16[16,64,128]{2,1,0:T(8,128)(2,1)S(1)} async-done(((bf16[16,64,128]{2,1,0:T(8,128)(2,1)}), bf16[16,64,128]{2,1,0:T(8,128)(2,1)S(1)}, u32[]{:S(2)}, u32[]{:S(2)}) %all-to-all-start.1) | async-done | bytes 262176 | tf_op jit(solution)/shard_map/all_to_all | solution.py:436
  47.4 0.7 copy-done.5
  48.1 3.2 %second_rows.1 = bf16[64,72,128]{2,1,0:T(8,128)(2,1)} custom-call(s32[4]{0:T(128)} %pad_add_fusion.place, bf16[16,64,128]{2,1,0:T(8,128)(2,1)} %copy-done.5, bf16[2,2,8,1280]{3,2,1,0:T(8,128)(2,1)} %copy-done.6, bf16[2,2,8,1280]{3,2,1,0:T(8,128)(2,1)} %copy-done.9, bf16[2,2,8,1280]{3,2,1,0:T(8,128)(2,1)} %copy-done.8, bf16[2,2,8,1280]{3,2,1,0:T(8,128)(2,1)} %copy-done.7, ...), custom_call_target="tpu_custom_call" | custom-call | tf_op jit(solution)/shard_map/second_rows/pallas_call | solution.py:176
  51.3 4.7 %all-to-all-start.2 = ((bf16[64,72,128]{2,1,0:T(8,128)(2,1)}), bf16[64,72,128]{2,1,0:T(8,128)(2,1)S(1)}, u32[]{:S(2)}, u32[]{:S(2)}) async-start(bf16[64,72,128]{2,1,0:T(8,128)(2,1)} %second_rows.1), calls=%async_computation.2 | async-start | bytes 2359296 | tf_op jit(solution)/shard_map/all_to_all | solution.py:442
  56.0 2.5 %collective-permute-start.6 = (bf16[1024,128]{1,0:T(8,128)(2,1)S(1)}, bf16[1024,128]{1,0:T(8,128)(2,1)S(1)}, u32[]{:S(2)}, u32[]{:S(2)}) collective-permute-start(bf16[1024,128]{1,0:T(8,128)(2,1)S(1)} %copy-done.10), channel_id=1, source_target_pairs={{0,96},{32,0},{64,32},{96,64},{1,97},{33,1},{65,33},{97,65},{2,98}... | collective-permute-start | bytes 786440 | tf_op jit(solution)/shard_map/ppermute | solution.py:392
  58.8 0.7 collective-permute-start.4
  59.5 14.0 %all-to-all-done.2 = bf16[64,72,128]{2,1,0:T(8,128)(2,1)S(1)} async-done(((bf16[64,72,128]{2,1,0:T(8,128)(2,1)}), bf16[64,72,128]{2,1,0:T(8,128)(2,1)S(1)}, u32[]{:S(2)}, u32[]{:S(2)}) %all-to-all-start.2) | async-done | bytes 1179680 | tf_op jit(solution)/shard_map/all_to_all | solution.py:442
  73.5 8.9 %collective-permute-start.8 = (bf16[64,72,128]{2,1,0:T(8,128)(2,1)S(1)}, bf16[64,72,128]{2,1,0:T(8,128)(2,1)S(1)}, u32[]{:S(2)}, u32[]{:S(2)}) collective-permute-start(bf16[64,72,128]{2,1,0:T(8,128)(2,1)S(1)} %all-to-all-done.2), channel_id=1, source_target_pairs={{0,16},{16,0},{1,17},{17,1},{2,18},{18,2},{3,19},{19,3},{4,20},{20... | collective-permute-start | bytes 3538952 | tf_op jit(solution)/shard_map/ppermute | solution.py:397
  82.4 0.7 copy-done.11
  83.2 1.3 %pad_maximum_fusion.mine = bf16[4,1024,128]{2,1,0:T(8,128)(2,1)S(1)} fusion(bf16[1,1024,128]{2,1,0:T(8,128)(2,1)} %bitcast.27, bf16[1,1024,128]{2,1,0:T(8,128)(2,1)} %bitcast.28, bf16[1,1024,128]{2,1,0:T(8,128)(2,1)} %bitcast.29, bf16[1,1024,128]{2,1,0:T(8,128)(2,1)} %bitcast.26), kind=kLoop, calls=%fused_computation.1 | loop fusion | flops 1572864 | bytes 2097152 | tf_op jit(solution)/shard_map/stack | solution.py:438
  84.6 1.3 %collective-permute-start.7 = (bf16[4,1024,128]{2,1,0:T(8,128)(2,1)S(1)}, bf16[4,1024,128]{2,1,0:T(8,128)(2,1)}, u32[]{:S(2)}, u32[]{:S(2)}) collective-permute-start(bf16[4,1024,128]{2,1,0:T(8,128)(2,1)S(1)} %pad_maximum_fusion.mine), channel_id=1, source_target_pairs={{0,16},{16,0},{1,17},{17,1},{2,18},{18,2},{3,19},{19,3},{4,20},{20... | collective-permute-start | bytes 3145736 | tf_op jit(solution)/shard_map/ppermute | solution.py:397
  86.0 2.2 %collective-permute-done.7.theirs = bf16[4,1024,128]{2,1,0:T(8,128)(2,1)} collective-permute-done((bf16[4,1024,128]{2,1,0:T(8,128)(2,1)S(1)}, bf16[4,1024,128]{2,1,0:T(8,128)(2,1)}, u32[]{:S(2)}, u32[]{:S(2)}) %collective-permute-start.7) | collective-permute-done | bytes 1048608 | tf_op jit(solution)/shard_map/ppermute | solution.py:397
  88.3 2.3 %couple_first.1.before = f32[1024,128]{1,0:T(8,128)S(1)} custom-call(bf16[4,1024,128]{2,1,0:T(8,128)(2,1)S(1)} %pad_maximum_fusion.mine, bf16[4,1024,128]{2,1,0:T(8,128)(2,1)} %collective-permute-done.7.theirs), custom_call_target="tpu_custom_call" | custom-call | tf_op jit(solution)/shard_map/couple_first/pallas_call | solution.py:341
  90.6 12.4 %trail_first.1.partial = f32[2,2,1024,256]{3,2,1,0:T(8,128)} custom-call(s32[4]{0:T(128)S(1)} %copy-done.3, bf16[4,1024,128]{2,1,0:T(8,128)(2,1)S(1)} %pad_maximum_fusion.mine, bf16[4,1024,128]{2,1,0:T(8,128)(2,1)} %collective-permute-done.7.theirs, bf16[2,2,2,1024,1024]{4,3,2,1,0:T(8,128)(2,1)} %factor.5, bf16[2,2,1024,256]{3,2,1,0:T(8,128)(2,1)S(1)} %copy-done.1), custom_call_target="tpu_custom_call" | custom-call | tf_op jit(solution)/shard_map/trail_first/pallas_call | solution.py:231
  103.0 7.2 %trail_second.2 = (bf16[2,2,1024,256]{3,2,1,0:T(8,128)(2,1)}, bf16[2,8,256]{2,1,0:T(8,128)(2,1)S(1)}) custom-call(s32[5]{0:T(128)S(1)} %concatenate.28.place, bf16[4,16,72,128]{3,2,1,0:T(8,128)(2,1)S(1)} %bitcast.19, bf16[2,2,2,1024,1024]{4,3,2,1,0:T(8,128)(2,1)} %factor.5, f32[2,2,1024,256]{3,2,1,0:T(8,128)} %trail_first.1.partial), custom_call_target="tpu_custom_call" | custom-call | tf_op jit(solution)/shard_map/trail_second/pallas_call | solution.py:276
  110.2 2.9 %gradient.1 = f32[3,8]{1,0:T(4,128)} custom-call(s32[4]{0:T(128)S(1)} %copy-done.3, bf16[4,16,72,128]{3,2,1,0:T(8,128)(2,1)S(1)} %bitcast.20, bf16[4,16,72,128]{3,2,1,0:T(8,128)(2,1)S(1)} %bitcast.21, f32[1024,128]{1,0:T(8,128)S(1)} %couple_first.1.before, bf16[128,768]{1,0:T(8,128)(2,1)S(1)} %copy-done.2), custom_call_target="tpu_custom_call" | custom-call | tf_op jit(solution)/shard_map/gradient/pallas_call | solution.py:373
  113.1 7.2 %trail_second.3 = (bf16[2,2,1024,256]{3,2,1,0:T(8,128)(2,1)}, bf16[2,8,256]{2,1,0:T(8,128)(2,1)S(1)}) custom-call(s32[5]{0:T(128)S(1)} %concatenate.30.place, bf16[4,16,72,128]{3,2,1,0:T(8,128)(2,1)S(1)} %bitcast.22, bf16[2,2,2,1024,1024]{4,3,2,1,0:T(8,128)(2,1)} %factor.5, f32[2,2,1024,256]{3,2,1,0:T(8,128)} %trail_first.1.partial, ...), custom_call_target="tpu_custom_call", output_to_operand_aliasing={{0}: (4, {})} | custom-call | tf_op jit(solution)/shard_map/trail_second/pallas_call | solution.py:276
  (55 shorter events, 3.6 us)
Async XLA Ops:
  0.6 21.7 %copy-start = (s32[1024]{0:T(1024)S(1)}, s32[1024]{0:T(1024)}, u32[]{:S(2)}) copy-start(s32[1024]{0:T(1024)} %param.18) | copy-start | bytes 12292
  0.6 16.6 %copy-start.16 = (s32[2,8,3]{1,0,2:T(2,128)S(1)}, s32[2,8,3]{1,0,2:T(2,128)}, u32[]{:S(2)}) copy-start(s32[2,8,3]{1,0,2:T(2,128)} %param.17) | copy-start | bytes 580
  4.6 25.6 %all-to-all-start = ((bf16[128,2,8,128]{3,2,1,0:T(8,128)(2,1)}), bf16[128,2,8,128]{3,2,1,0:T(8,128)(2,1)S(1)}, u32[]{:S(2)}, u32[]{:S(2)}) async-start(bf16[128,2,8,128]{3,2,1,0:T(8,128)(2,1)} %bitcast.25), calls=%async_computation | async-start | bytes 1048576 | tf_op jit(solution)/shard_map/all_to_all | solution.py:428
  16.1 2.2 %collective-permute-start = (bf16[2,8,1280]{2,1,0:T(8,128)(2,1)}, bf16[2,8,1280]{2,1,0:T(8,128)(2,1)S(1)}, u32[]{:S(2)}, u32[]{:S(2)}) collective-permute-start(bf16[2,8,1280]{2,1,0:T(8,128)(2,1)} %get-tuple-element.16), channel_id=1, source_target_pairs={{0,16},{16,0},{1,17},{17,1},{2,18},{18,2},{3,19},{19,3},{4,20},{20... | collective-permute-start | bytes 122888 | tf_op jit(solution)/shard_map/ppermute | solution.py:397
  19.2 3.9 %copy-start.6 = (bf16[2,2,8,1280]{3,2,1,0:T(8,128)(2,1)}, bf16[2,2,8,1280]{3,2,1,0:T(8,128)(2,1)S(1)}, u32[]{:S(2)}) copy-start(bf16[2,2,8,1280]{3,2,1,0:T(8,128)(2,1)S(1)} %maximum_select_fusion.rows0) | copy-start | bytes 245764
  19.2 5.6 %collective-permute-start.3 = (bf16[2,2,8,1280]{3,2,1,0:T(8,128)(2,1)S(1)}, bf16[2,2,8,1280]{3,2,1,0:T(8,128)(2,1)S(1)}, u32[]{:S(2)}, u32[]{:S(2)}) collective-permute-start(bf16[2,2,8,1280]{3,2,1,0:T(8,128)(2,1)S(1)} %maximum_select_fusion.rows0), channel_id=1, source_target_pairs={{0,96},{32,0},{64,32},{96,64},{1,97},{33,1},{65,33},{97,65},{2,98}... | collective-permute-start | bytes 245768 | tf_op jit(solution)/shard_map/ppermute | solution.py:392
  21.2 5.1 %collective-permute-start.2 = (bf16[2,2,8,1280]{3,2,1,0:T(8,128)(2,1)S(1)}, bf16[2,2,8,1280]{3,2,1,0:T(8,128)(2,1)S(1)}, u32[]{:S(2)}, u32[]{:S(2)}) collective-permute-start(bf16[2,2,8,1280]{3,2,1,0:T(8,128)(2,1)S(1)} %maximum_select_fusion.rows0), channel_id=1, source_target_pairs={{0,64},{32,96},{64,0},{96,32},{1,65},{33,97},{65,1},{97,33},{2,66}... | collective-permute-start | bytes 245768 | tf_op jit(solution)/shard_map/ppermute | solution.py:392
  21.8 6.7 %collective-permute-start.1 = (bf16[2,2,8,1280]{3,2,1,0:T(8,128)(2,1)S(1)}, bf16[2,2,8,1280]{3,2,1,0:T(8,128)(2,1)S(1)}, u32[]{:S(2)}, u32[]{:S(2)}) collective-permute-start(bf16[2,2,8,1280]{3,2,1,0:T(8,128)(2,1)S(1)} %maximum_select_fusion.rows0), channel_id=1, source_target_pairs={{0,32},{32,64},{64,96},{96,0},{1,33},{33,65},{65,97},{97,1},{2,34}... | collective-permute-start | bytes 245768 | tf_op jit(solution)/shard_map/ppermute | solution.py:392
  22.4 17.5 %copy-start.14 = (f32[2,9,2,8]{1,3,2,0:T(8,128)S(1)}, f32[2,9,2,8]{1,3,2,0:T(8,128)}, u32[]{:S(2)}) copy-start(f32[2,9,2,8]{1,3,2,0:T(8,128)} %param.16) | copy-start | bytes 3460
  24.9 5.3 %copy-start.7 = (bf16[2,2,8,1280]{3,2,1,0:T(8,128)(2,1)}, bf16[2,2,8,1280]{3,2,1,0:T(8,128)(2,1)S(1)}, u32[]{:S(2)}) copy-start(bf16[2,2,8,1280]{3,2,1,0:T(8,128)(2,1)S(1)} %collective-permute-done.3.rows3) | copy-start | bytes 245764
  26.3 3.9 %copy-start.8 = (bf16[2,2,8,1280]{3,2,1,0:T(8,128)(2,1)}, bf16[2,2,8,1280]{3,2,1,0:T(8,128)(2,1)S(1)}, u32[]{:S(2)}) copy-start(bf16[2,2,8,1280]{3,2,1,0:T(8,128)(2,1)S(1)} %collective-permute-done.2.rows2) | copy-start | bytes 245764
  28.4 1.8 %copy-start.9 = (bf16[2,2,8,1280]{3,2,1,0:T(8,128)(2,1)}, bf16[2,2,8,1280]{3,2,1,0:T(8,128)(2,1)S(1)}, u32[]{:S(2)}) copy-start(bf16[2,2,8,1280]{3,2,1,0:T(8,128)(2,1)S(1)} %collective-permute-done.1.rows1) | copy-start | bytes 245764
  30.2 0.8 copy-start.4
  33.9 13.5 %all-to-all-start.1 = ((bf16[16,64,128]{2,1,0:T(8,128)(2,1)}), bf16[16,64,128]{2,1,0:T(8,128)(2,1)S(1)}, u32[]{:S(2)}, u32[]{:S(2)}) async-start(bf16[16,64,128]{2,1,0:T(8,128)(2,1)} %get-tuple-element.17), calls=%async_computation.1 | async-start | bytes 524288 | tf_op jit(solution)/shard_map/all_to_all | solution.py:436
  39.9 16.1 %copy-start.10 = (bf16[1024,128]{1,0:T(8,128)(2,1)S(1)}, bf16[1024,128]{1,0:T(8,128)(2,1)}, u32[]{:S(2)}) copy-start(bf16[1024,128]{1,0:T(8,128)(2,1)} %get-tuple-element.18) | copy-start | bytes 786436
  47.4 0.7 copy-start.5
  51.3 22.2 %all-to-all-start.2 = ((bf16[64,72,128]{2,1,0:T(8,128)(2,1)}), bf16[64,72,128]{2,1,0:T(8,128)(2,1)S(1)}, u32[]{:S(2)}, u32[]{:S(2)}) async-start(bf16[64,72,128]{2,1,0:T(8,128)(2,1)} %second_rows.1), calls=%async_computation.2 | async-start | bytes 2359296 | tf_op jit(solution)/shard_map/all_to_all | solution.py:442
  56.0 26.4 %collective-permute-start.6 = (bf16[1024,128]{1,0:T(8,128)(2,1)S(1)}, bf16[1024,128]{1,0:T(8,128)(2,1)S(1)}, u32[]{:S(2)}, u32[]{:S(2)}) collective-permute-start(bf16[1024,128]{1,0:T(8,128)(2,1)S(1)} %copy-done.10), channel_id=1, source_target_pairs={{0,96},{32,0},{64,32},{96,64},{1,97},{33,1},{65,33},{97,65},{2,98}... | collective-permute-start | bytes 786440 | tf_op jit(solution)/shard_map/ppermute | solution.py:392
  58.5 23.9 %collective-permute-start.5 = (bf16[1024,128]{1,0:T(8,128)(2,1)S(1)}, bf16[1024,128]{1,0:T(8,128)(2,1)S(1)}, u32[]{:S(2)}, u32[]{:S(2)}) collective-permute-start(bf16[1024,128]{1,0:T(8,128)(2,1)S(1)} %copy-done.10), channel_id=1, source_target_pairs={{0,64},{32,96},{64,0},{96,32},{1,65},{33,97},{65,1},{97,33},{2,66}... | collective-permute-start | bytes 786440 | tf_op jit(solution)/shard_map/ppermute | solution.py:392
  58.8 23.6 %collective-permute-start.4 = (bf16[1024,128]{1,0:T(8,128)(2,1)S(1)}, bf16[1024,128]{1,0:T(8,128)(2,1)S(1)}, u32[]{:S(2)}, u32[]{:S(2)}) collective-permute-start(bf16[1024,128]{1,0:T(8,128)(2,1)S(1)} %copy-done.10), channel_id=1, source_target_pairs={{0,32},{32,64},{64,96},{96,0},{1,33},{33,65},{65,97},{97,1},{2,34}... | collective-permute-start | bytes 786440 | tf_op jit(solution)/shard_map/ppermute | solution.py:392
  73.5 36.7 %collective-permute-start.8 = (bf16[64,72,128]{2,1,0:T(8,128)(2,1)S(1)}, bf16[64,72,128]{2,1,0:T(8,128)(2,1)S(1)}, u32[]{:S(2)}, u32[]{:S(2)}) collective-permute-start(bf16[64,72,128]{2,1,0:T(8,128)(2,1)S(1)} %all-to-all-done.2), channel_id=1, source_target_pairs={{0,16},{16,0},{1,17},{17,1},{2,18},{18,2},{3,19},{19,3},{4,20},{20... | collective-permute-start | bytes 3538952 | tf_op jit(solution)/shard_map/ppermute | solution.py:397
  82.4 0.7 copy-start.11
  82.4 0.8 copy-start.12
  82.4 0.8 copy-start.13
  83.2 7.3 %copy-start.3 = (s32[4]{0:T(128)S(1)}, s32[4]{0:T(128)}, u32[]{:S(2)}) copy-start(s32[4]{0:T(128)} %pad_add_fusion.place) | copy-start | bytes 52
  84.6 3.7 %collective-permute-start.7 = (bf16[4,1024,128]{2,1,0:T(8,128)(2,1)S(1)}, bf16[4,1024,128]{2,1,0:T(8,128)(2,1)}, u32[]{:S(2)}, u32[]{:S(2)}) collective-permute-start(bf16[4,1024,128]{2,1,0:T(8,128)(2,1)S(1)} %pad_maximum_fusion.mine), channel_id=1, source_target_pairs={{0,16},{16,0},{1,17},{17,1},{2,18},{18,2},{3,19},{19,3},{4,20},{20... | collective-permute-start | bytes 3145736 | tf_op jit(solution)/shard_map/ppermute | solution.py:397
  86.0 4.5 %copy-start.1 = (bf16[2,2,1024,256]{3,2,1,0:T(8,128)(2,1)S(1)}, bf16[2,2,1024,256]{3,2,1,0:T(8,128)(2,1)}, u32[]{:S(2)}) copy-start(bf16[2,2,1024,256]{3,2,1,0:T(8,128)(2,1)} %rhs.3) | copy-start | bytes 6291460
  103.0 7.2 %copy-start.2 = (bf16[128,768]{1,0:T(8,128)(2,1)S(1)}, bf16[128,768]{1,0:T(8,128)(2,1)}, u32[]{:S(2)}) copy-start(bf16[128,768]{1,0:T(8,128)(2,1)} %constant.55.clone.spread) | copy-start | bytes 589828
  113.1 7.2 %copy-start.15 = (bf16[2,2,8,256]{3,2,1,0:T(8,128)(2,1)S(1)}, bf16[2,2,8,256]{3,2,1,0:T(8,128)(2,1)}, u32[]{:S(2)}) copy-start(bf16[2,2,8,256]{3,2,1,0:T(8,128)(2,1)} %get-tuple-element.13) | copy-start | bytes 49156

commit v5 on v4

v5 whole, which is shorter than its diff:
```python
import jax
import jax.numpy as jnp
import numpy as np
from jax import lax
from jax.experimental import pallas as pl
from jax.experimental.pallas import tpu as pltpu
from jax.sharding import Mesh
from jax.sharding import PartitionSpec as P


ALL = ("x", "core", "col")
F32 = jnp.float32
BF16 = jnp.bfloat16
TRAIL_VMEM = 24 * 1024 * 1024
SMALL_VMEM = 12 * 1024 * 1024
SPACE = pltpu.VMEM


def lanes_below(shape, bound):
    return lax.broadcasted_iota(jnp.int32, shape, len(shape) - 1) < bound


def pair_lanes(left, right):
    low = lanes_below(left.shape, 64)
    real = jnp.where(low, left, pltpu.roll(right, 64, 1))
    imag = jnp.where(low, pltpu.roll(left, 64, 1), right)
    return real, imag


def fold_parts(top, low):
    turned = pltpu.roll(low, 64, 1)
    return top + jnp.where(lanes_below(low.shape, 64), -turned, turned)


def prepare_kernel(inverse, rhs, below, own_rhs, first, send, own, give):
    system = pl.program_id(0)
    core = lax.axis_index("core")
    left = jnp.concatenate([inverse[0, 0, 0].astype(F32), inverse[0, 0, 1].astype(F32)]).astype(BF16)
    by_real = jnp.dot(left, rhs[0, 0], preferred_element_type=F32)
    by_imag = jnp.dot(left, rhs[0, 1], preferred_element_type=F32)
    real = (by_real[:8] - by_imag[8:]).astype(BF16)
    imag = (by_imag[:8] + by_real[8:]).astype(BF16)
    first[0, 0] = real
    first[0, 1] = imag
    real = real.astype(F32)
    imag = imag.astype(F32)
    for half in range(2):
        cut = slice(128 * half, 128 * half + 128)
        even, odd = pair_lanes(real[:, cut], imag[:, cut])
        for group, value in ((2 * half, even), (2 * half + 1, odd)):
            value = value.astype(BF16)
            for col in range(16):
                send[group, 0, col, 0] = value
    lane_block = lax.broadcasted_iota(jnp.int32, (8, 128), 1) // 8
    pieces = [
        below[0, part, :, 128 * row : 128 * row + 128].astype(F32)
        for part in range(2)
        for row in range(8)
    ]
    for col in range(16):
        value = pltpu.roll(pieces[0], (128 - 8 * col) % 128, 1)
        for block in range(1, 16):
            turned = pltpu.roll(pieces[block], (8 * block - 8 * col) % 128, 1)
            value = jnp.where(lane_block == block, turned, value)
        value = value.astype(BF16)
        for group in range(4):
            send[group, 0, col, 1] = value

    def fill(target):
        for part in range(2):
            target[part, :, :1024] = inverse[0, 1, part]
            target[part, :, 1024:] = own_rhs[0, part]

    @pl.when(system == core)
    def _():
        fill(own)

    @pl.when(system != core)
    def _():
        fill(give)


def prepare(panel_inverse, first_rhs, panel_below, second_rhs):
    return pl.pallas_call(
        prepare_kernel,
        grid=(2,),
        in_specs=[
            pl.BlockSpec((1, 2, 2, 8, 1024), lambda s: (s, 0, 0, 0, 0)),
            pl.BlockSpec((1, 2, 1024, 256), lambda s: (s, 0, 0, 0)),
            pl.BlockSpec((1, 2, 8, 1024), lambda s: (s, 0, 0, 0)),
            pl.BlockSpec((1, 2, 8, 256), lambda s: (s, 0, 0, 0)),
        ],
        out_specs=[
            pl.BlockSpec((1, 2, 8, 256), lambda s: (s, 0, 0, 0)),
            pl.BlockSpec((4, 1, 16, 2, 8, 128), lambda s: (0, s, 0, 0, 0, 0)),
            pl.BlockSpec((2, 8, 1280), lambda s: (0, 0, 0)),
            pl.BlockSpec((2, 8, 1280), lambda s: (0, 0, 0)),
        ],
        out_shape=[
            jax.ShapeDtypeStruct((2, 2, 8, 256), BF16),
            jax.ShapeDtypeStruct((4, 2, 16, 2, 8, 128), BF16),
            jax.ShapeDtypeStruct((2, 8, 1280), BF16),
            jax.ShapeDtypeStruct((2, 8, 1280), BF16),
        ],
        compiler_params=pltpu.CompilerParams(vmem_limit_bytes=SMALL_VMEM),
        name="prepare",
    )(panel_inverse, first_rhs, panel_below, second_rhs)


def right_kernel(place, received, rows0, rows1, rows2, rows3, block, send, offset):
    x = place[0]
    half = pl.multiple_of(1024 + 128 * (x // 2), 128)
    odd = x % 2 == 1
    for step, rows in enumerate((rows0, rows1, rows2, rows3)):
        source = lax.rem(x - step + 4, 4)
        for core in range(2):
            real = rows[core, 0, :, pl.ds(half, 128)].astype(F32)
            imag = rows[core, 1, :, pl.ds(half, 128)].astype(F32)
            even_pair, odd_pair = pair_lanes(real, imag)
            value = jnp.where(odd, odd_pair, even_pair)
            offset[pl.ds(pl.multiple_of(16 * source + 8 * core, 8), 8), :] = value
    first = received[:, 0].astype(F32).reshape(1024, 128).astype(BF16)
    below = received[:, 1].astype(F32).reshape(1024, 128).astype(BF16)
    block[...] = first
    product = lax.dot_general(below, first, (((0,), (0,)), ((), ())), preferred_element_type=F32)
    right = (offset[...] - fold_parts(product[:64], product[64:])).astype(BF16)
    for col in range(16):
        send[col] = right


def right_side(place, received, rows):
    inside = pl.BlockSpec(memory_space=pltpu.VMEM)
    return pl.pallas_call(
        right_kernel,
        in_specs=[pl.BlockSpec(memory_space=pltpu.SMEM)] + [inside] * 5,
        out_specs=[inside] * 2,
        out_shape=[SPACE((1024, 128), BF16), SPACE((16, 64, 128), BF16)],
        scratch_shapes=[pltpu.VMEM((64, 128), F32)],
        compiler_params=pltpu.CompilerParams(vmem_limit_bytes=SMALL_VMEM),
        name="right_side",
    )(place, received, *rows)


def second_kernel(place, received, rows0, rows1, rows2, rows3, tile, send):
    x = place[0]
    right = received[...].astype(F32).reshape(16, 8, 8, 128)
    right = right.transpose(1, 0, 2, 3).reshape(1024, 128).astype(BF16)
    pieces = [
        rows[core, part, :, :1024].astype(F32)
        for part in range(2)
        for rows in (rows0, rows1, rows2, rows3)
        for core in range(2)
    ]
    left = jnp.concatenate(pieces).astype(BF16)
    product = jnp.dot(left, right, preferred_element_type=F32)
    value = fold_parts(product[:64], product[64:]).astype(BF16)
    for step in range(4):
        target = pl.multiple_of(16 * lax.rem(x - step + 4, 4), 16)
        part = value[16 * step : 16 * step + 16]
        for copy in range(64):
            send[copy, pl.ds(target, 16), :] = part
    for copy in range(64):
        send[copy, 64:] = tile[...]


def second_rows(place, received, rows, tile):
    inside = pl.BlockSpec(memory_space=pltpu.VMEM)
    return pl.pallas_call(
        second_kernel,
        in_specs=[pl.BlockSpec(memory_space=pltpu.SMEM)] + [inside] * 6,
        out_specs=inside,
        out_shape=SPACE((64, 72, 128), BF16),
        compiler_params=pltpu.CompilerParams(vmem_limit_bytes=SMALL_VMEM),
        name="second_rows",
    )(place, received, *rows, tile)


def trail_product(stacked, blocks):
    height = stacked.shape[0] // 2
    product = jnp.dot(stacked, blocks[...], preferred_element_type=F32)
    real, imag = [], []
    for half in range(2):
        lanes = slice(256 * half, 256 * half + 128)
        even, even_turned = product[:height, lanes], product[height:, lanes]
        lanes = slice(256 * half + 128, 256 * half + 256)
        odd, odd_turned = product[:height, lanes], product[height:, lanes]
        low = lanes_below(even.shape, 64)
        turn = lambda value: pltpu.roll(value, 64, 1)
        real.append(jnp.where(low, even - turn(even_turned), turn(odd) - odd_turned))
        imag.append(jnp.where(low, turn(even) + even_turned, odd + turn(odd_turned)))
    return jnp.concatenate(real, axis=1), jnp.concatenate(imag, axis=1)


def trail_first_kernel(place, mine, theirs, factor, rhs, near, far, blocks):
    x = place[0]
    turn = pl.program_id(0)
    step = pl.program_id(1)
    system = jnp.where(turn == 0, place[1], 1 - place[1])

    @pl.when((turn == 0) & (step == 0))
    def _():
        for q in range(4):
            blocks[:, 128 * q : 128 * q + 128] = mine[lax.rem(x - q + 4, 4)]

    @pl.when((turn == 1) & (step == 0))
    def _():
        for q in range(4):
            blocks[:, 128 * q : 128 * q + 128] = theirs[lax.rem(x - q + 4, 4)]

    height = factor.shape[3]
    real, imag = trail_product(factor[0, 0].reshape(2 * height, 1024), blocks)
    real = rhs[0, 0].astype(F32) - real
    imag = rhs[0, 1].astype(F32) - imag

    @pl.when(step < 3)
    def _():
        rows = pl.ds(pl.multiple_of(height * step, height), height)
        near[system, 0, rows, :] = real
        near[system, 1, rows, :] = imag

    @pl.when(step == 3)
    def _():
        far[0, 0] = real
        far[0, 1] = imag


def trail_first(place, mine, theirs, trail_factor, trail_rhs):
    rows = trail_rhs.shape[2]
    height = rows // 4
    system = lambda turn, p: jnp.where(turn == 0, p[1], 1 - p[1])
    return pl.pallas_call(
        trail_first_kernel,
        grid_spec=pltpu.PrefetchScalarGridSpec(
            num_scalar_prefetch=1,
            grid=(2, 4),
            in_specs=[pl.BlockSpec((4, 1024, 128), lambda t, i, p: (0, 0, 0))] * 2
            + [
                pl.BlockSpec((1, 1, 2, height, 1024), lambda t, i, p: (system(t, p), 0, 0, i, 0)),
                pl.BlockSpec((1, 2, height, 256), lambda t, i, p: (system(t, p), 0, i, 0)),
            ],
            out_specs=[
                pl.BlockSpec(memory_space=pltpu.VMEM),
                pl.BlockSpec((1, 2, height, 256), lambda t, i, p: (system(t, p), 0, 0, 0)),
            ],
            scratch_shapes=[pltpu.VMEM((1024, 512), BF16)],
        ),
        out_shape=[
            pltpu.VMEM((2, 2, 3 * height, 256), F32),
            pltpu.HBM((2, 2, height, 256), F32),
        ],
        compiler_params=pltpu.CompilerParams(vmem_limit_bytes=TRAIL_VMEM),
        name="trail_first",
    )(place, mine, theirs, trail_factor, trail_rhs)


def take_blocks(place, received, blocks, tiles):
    for q in range(4):
        for row in range(8):
            value = received[q, :, 8 * row : 8 * row + 8, :].astype(F32).reshape(128, 128)
            blocks[128 * row : 128 * row + 128, 128 * q : 128 * q + 128] = value.astype(BF16)
        tiles[q] = received[q, :, 64:, :].astype(F32).reshape(128, 128).astype(BF16)
    near = pl.multiple_of(8 * place[2], 8)
    parts = [received[q, place[3], pl.ds(near, 8), :].astype(F32) for q in range(4)]
    pairs = [pair_lanes(parts[0], parts[1]), pair_lanes(parts[2], parts[3])]
    return [
        jnp.concatenate([pairs[0][part], pairs[1][part]], axis=1).astype(BF16) for part in range(2)
    ]


class Trail:
    scratch = staticmethod(
        lambda height: [
            pltpu.VMEM((4, 16, 72, 128), BF16),
            pltpu.VMEM((4, 2, height, 1024), BF16),
            pltpu.VMEM((2, height, 256), F32),
            pltpu.VMEM((4, 2, height, 256), BF16),
            pltpu.SemaphoreType.DMA((10,)),
        ]
    )

    def __init__(self, system, received, factor, near, far, out, scratch):
        arrived, rows, last, done, sems = scratch
        height = last.shape[1]
        self.system, self.near, self.height = system, near, height
        self.arrived, self.rows, self.last, self.done = arrived, rows, last, done
        copy = pltpu.make_async_copy
        self.take = copy(received, arrived, sems.at[0])
        self.take_last = copy(far.at[system], last, sems.at[1])
        self.take_rows = [
            copy(factor.at[system, 1, :, pl.ds(i * height, height)], rows.at[i], sems.at[2 + i])
            for i in range(4)
        ]
        self.give = [
            copy(done.at[i], out.at[system, :, pl.ds(i * height, height)], sems.at[6 + i])
            for i in range(4)
        ]

    def start(self):
        self.take.start()
        for one in self.take_rows:
            one.start()
        self.take_last.start()

    def run(self, blocks):
        height = self.height
        for i in range(4):
            self.take_rows[i].wait()
            real, imag = trail_product(self.rows[i].reshape(2 * height, 1024), blocks)
            if i < 3:
                cut = slice(i * height, i * height + height)
                before = (self.near[self.system, 0, cut, :], self.near[self.system, 1, cut, :])
            else:
                self.take_last.wait()
                before = (self.last[0], self.last[1])
            self.done[i, 0] = (before[0] - real).astype(BF16)
            self.done[i, 1] = (before[1] - imag).astype(BF16)
            self.give[i].start()

    def finish(self):
        for one in self.give:
            one.wait()


def trail_mine_kernel(place, received, factor, near, far, out, own, blocks, tiles, *scratch):
    trail = Trail(place[1], received, factor, near, far, out, scratch)
    trail.start()
    trail.take.wait()
    own[0], own[1] = take_blocks(place, trail.arrived, blocks, tiles)
    trail.run(blocks)
    trail.finish()


def trail_mine(place, received, trail_factor, near, far):
    height = far.shape[2]
    inside = pl.BlockSpec(memory_space=pltpu.VMEM)
    outside = pl.BlockSpec(memory_space=pltpu.HBM)
    return pl.pallas_call(
        trail_mine_kernel,
        in_specs=[pl.BlockSpec(memory_space=pltpu.SMEM), outside, outside, inside, outside],
        out_specs=[outside, inside, inside, inside],
        out_shape=[
            pltpu.HBM((2, 2, 4 * height, 256), BF16),
            pltpu.VMEM((2, 8, 256), BF16),
            pltpu.VMEM((1024, 512), BF16),
            pltpu.VMEM((4, 128, 128), BF16),
        ],
        scratch_shapes=Trail.scratch(height),
        compiler_params=pltpu.CompilerParams(vmem_limit_bytes=TRAIL_VMEM),
        name="trail_mine",
    )(place, received, trail_factor, near, far)


def trail_theirs_kernel(
    place, received, factor, near, far, mine, mine_tiles, own, first, before, spread, _, out, panel, gradient, blocks, tiles, *scratch
):
    core = place[1]
    trail = Trail(1 - core, received, factor, near, far, out, scratch)
    trail.start()
    panel[:, 0] = first[...]
    panel[core, 1] = own[...]
    trail.take.wait()
    real, imag = take_blocks(place, trail.arrived, blocks, tiles)
    panel[1 - core, 1, 0] = real
    panel[1 - core, 1, 1] = imag
    trail.run(blocks)
    slot_gradient(place, mine, blocks, (mine_tiles, tiles), before, spread, gradient)
    trail.finish()


def trail_theirs(place, received, trail_factor, near, far, mine, mine_tiles, own, first, before, spread, update):
    height = far.shape[2]
    inside = pl.BlockSpec(memory_space=pltpu.VMEM)
    outside = pl.BlockSpec(memory_space=pltpu.HBM)
    return pl.pallas_call(
        trail_theirs_kernel,
        in_specs=[pl.BlockSpec(memory_space=pltpu.SMEM), outside, outside, inside, outside]
        + [inside] * 6
        + [outside],
        out_specs=[outside, inside, inside],
        out_shape=[
            pltpu.HBM((2, 2, 4 * height, 256), BF16),
            jax.ShapeDtypeStruct((2, 2, 2, 8, 256), BF16),
            jax.ShapeDtypeStruct((3, 8), F32),
        ],
        scratch_shapes=[pltpu.VMEM((1024, 512), BF16), pltpu.VMEM((4, 128, 128), BF16)]
        + Trail.scratch(height),
        input_output_aliases={11: 0},
        compiler_params=pltpu.CompilerParams(vmem_limit_bytes=TRAIL_VMEM),
        name="trail_theirs",
    )(place, received, trail_factor, near, far, mine, mine_tiles, own, first, before, spread, update)


def spread_matrix():
    spread = np.zeros((128, 2, 3, 128), np.float32)
    for panel in range(2):
        for corner in range(3):
            for coordinate in range(3):
                lanes = slice(24 * corner + 8 * coordinate, 24 * corner + 8 * coordinate + 8)
                for part in range(2):
                    source = 18 * part + 9 * panel + 3 * corner + coordinate
                    for term in range(3):
                        spread[36 * term + source, panel, part, lanes] = 1.0
                spread[108 + 3 * panel + corner, panel, 2, lanes] = 32.0
                spread[114 + 3 * panel + corner, panel, 2, lanes] = 1.0
    return jnp.asarray(spread.reshape(128, 768), BF16)


def couple(mine, theirs):
    same = jnp.zeros((128, 128), F32)
    crossed = jnp.zeros((128, 128), F32)
    for near, far in zip(mine, theirs):
        near = near.astype(F32)
        far = far.astype(F32)
        same = same + near * far
        crossed = crossed + near * pltpu.roll(far, 64, 1)
    low = lanes_below((128, 128), 64)
    real = jnp.sum(jnp.where(low, same, -same), axis=1, keepdims=True)
    imag = jnp.sum(crossed, axis=1, keepdims=True)
    return real, imag


def couple_first_kernel(mine, theirs, out):
    low = lanes_below((128, 128), 64)
    for row in range(8):
        cut = slice(128 * row, 128 * row + 128)
        real, imag = couple([mine[q, cut, :] for q in range(4)], [theirs[q, cut, :] for q in range(4)])
        out[cut, :] = jnp.where(low, real, imag)


def couple_first(mine, theirs):
    return pl.pallas_call(
        couple_first_kernel,
        out_shape=pltpu.HBM((1024, 128), F32),
        compiler_params=pltpu.CompilerParams(vmem_limit_bytes=TRAIL_VMEM),
        name="couple_first",
    )(mine, theirs)


def slot_gradient(place, mine, theirs, tiles, before, spread, out):
    base = 8 * (16 * place[2] + place[3])
    target = (base + lax.rem(lax.broadcasted_iota(jnp.int32, (128, 128), 1), 8)).astype(F32)
    total = jnp.zeros((8, 128), F32)
    for source in range(4):
        for side in range(2):
            row = 2 * source + (place[1] if side == 0 else 1 - place[1])
            cut = pl.ds(pl.multiple_of(128 * row, 128), 128)
            lanes = [slice(128 * q, 128 * q + 128) for q in range(4)]
            real, imag = couple([mine[cut, q] for q in lanes], [theirs[cut, q] for q in lanes])
            first = before[cut, :]
            table = jnp.dot(tiles[side][source], spread[...], preferred_element_type=F32)
            for at, real, imag in ((0, first[:, :1], first[:, 64:65]), (384, real, imag)):
                value = table[:, at + 128 : at + 256] * imag - table[:, at : at + 128] * real
                value = jnp.where(table[:, at + 256 : at + 384] == target, value, 0.0)
                total = total + jnp.sum(value.reshape(16, 8, 128), axis=0)
    total = jnp.sum(total, axis=0, keepdims=True)
    total = total + pltpu.roll(total, 104, 1) + pltpu.roll(total, 80, 1)
    for coordinate in range(3):
        out[coordinate : coordinate + 1, :] = total[:, 8 * coordinate : 8 * coordinate + 8]


def rounds_x(value):
    sent = [lax.ppermute(value, "x", [(i, (i + step) % 4) for i in range(4)]) for step in (1, 2, 3)]
    return [value, *sent]


def swap_core(value):
    return lax.ppermute(value, "core", [(0, 1), (1, 0)])


def element_tile(shape_tiles, element_vertices, vertex_slot):
    values = shape_tiles.transpose(3, 0, 2, 1).reshape(8, 36)
    high = lax.reduce_precision(values, 8, 7)
    rest = values - high
    mid = lax.reduce_precision(rest, 8, 7)
    low = rest - mid
    slots = vertex_slot[element_vertices].transpose(1, 0, 2).reshape(8, 6)
    parts = [high, mid, low, (slots // 32).astype(F32), (slots % 32).astype(F32), jnp.zeros((8, 8), F32)]
    return jnp.concatenate(parts, axis=1).astype(BF16)


def steps(
    panel_inverse,
    panel_below,
    trail_factor,
    first_rhs,
    second_rhs,
    trail_rhs,
    shape_tiles,
    element_vertices,
    vertex_slot,
):
    x = lax.axis_index("x")
    core = lax.axis_index("core")
    col = lax.axis_index("col")
    outside = lambda value: pltpu.with_memory_space_constraint(value, pltpu.HBM)
    trail_factor, panel_inverse, first_rhs = map(outside, (trail_factor, panel_inverse, first_rhs))
    panel_below, second_rhs = map(outside, (panel_below, second_rhs))
    place = jnp.stack([x, core, 2 * x + core, col]).astype(jnp.int32)

    first, send, own, give = prepare(panel_inverse, first_rhs, panel_below, second_rhs)
    received = lax.all_to_all(send.reshape(128, 2, 8, 128), ALL, 0, 0, tiled=True)

    other = swap_core(give)
    chip = jnp.where(core == 0, jnp.stack([own, other]), jnp.stack([other, own]))
    rows = rounds_x(chip)
    tile = element_tile(shape_tiles, element_vertices, vertex_slot)

    first_block, send = right_side(place, received, rows)
    received = lax.all_to_all(send, "col", 0, 0, tiled=True)
    first_mine = rounds_x(first_block)
    first_mine = jnp.stack(first_mine)
    first_theirs = swap_core(first_mine)

    send = second_rows(place, received, rows, tile)
    second_mine = lax.all_to_all(send, ("x", "col"), 0, 0, tiled=True)

    near, far = trail_first(place, first_mine, first_theirs, trail_factor, outside(trail_rhs))
    far = outside(far)
    before = couple_first(first_mine, first_theirs)

    second_theirs = swap_core(second_mine)
    mine = second_mine.reshape(4, 16, 72, 128)
    theirs = second_theirs.reshape(4, 16, 72, 128)
    update, own, mine, mine_tiles = trail_mine(place, mine, trail_factor, near, far)
    update, panel_solution, gradient = trail_theirs(
        place,
        theirs,
        trail_factor,
        near,
        far,
        mine,
        mine_tiles,
        own,
        first,
        before,
        spread_matrix(),
        update,
    )
    return (panel_solution, update, gradient)


def solution(mesh):
    fine = Mesh(mesh.devices.reshape(4, 2, 16), ALL)
    return jax.shard_map(
        steps,
        mesh=fine,
        in_specs=(
            P(None, None, None, ALL, None),
            P(None, None, ALL, None),
            P(None, None, None, ALL, None),
            P(),
            P(None, None, ALL, None),
            P(None, None, ALL, None),
            P(None, None, None, ALL),
            P(None, ALL, None),
            P(),
        ),
        out_specs=(
            P(None, None, None, ALL, None),
            P(None, None, ALL, None),
            P(None, ALL),
        ),
        check_vma=False,
    )
```

time: 122 us -> 111 us (0.910)
  Pallas kernels: 41.4 us -> 35.6 us
  other arithmetic: 3.44 us -> 0.26 us
  local copies, waits for them, and re-layouts: 4.38 us -> 1.3 us
  waiting for transfers between devices: 30.8 us -> 32.6 us
    pallas_call x7 -> x6, Pallas kernels: 29.1 us -> 23.6 us  [the longest x1 8.88 us: trail_theirs(): pl.pallas_call(trail_theirs_kernel, in_specs=[pl.BlockSpec(memory_space=p...]
    unnamed x34 -> x10, local copies, waits for them, and re-layouts: 2.38 us -> 0.03 us
    ppermute x6, waiting for transfers between devices: 5.14 us -> 6.72 us  [rounds_x(): lax.ppermute(value, 'x', [(i, (i + step) % 4) for i in range(4)])]
  transfers between devices with their start and end apart: 12 -> 12, of which waited for: 8 -> 7; matrix products, arithmetic and copies ran while one was open for 3% -> 1% of each run, Pallas kernels for 18% -> 18%
where the time goes in v5:
time: 111 us; the launch traced here: 110 us
  starting transfers between devices  39.7 us (36%)
  Pallas kernels  35.6 us (32%)
  waiting for transfers between devices  32.6 us (29%)
  local copies, waits for them, and re-layouts  1.3 us (1%)
    all_to_all x1, waiting for transfers between devices, steps(): second_mine = lax.all_to_all(send, ('x', 'col'), 0, 0, tiled=True)  13.8 us
    pallas_call x1, Pallas kernels, trail_first(): pl.pallas_call(trail_first_kernel, grid_spec=pltpu.PrefetchScalarGridSpec...  11.9 us
    ppermute x3, starting transfers between devices, swap_core(): return lax.ppermute(value, 'core', [(0, 1), (1, 0)])  11.9 us
    all_to_all x1, starting transfers between devices, steps(): lax.all_to_all(send.reshape(128, 2, 8, 128), ALL, 0, 0, tiled=True)  11.5 us
    pallas_call x1, Pallas kernels, trail_theirs(): pl.pallas_call(trail_theirs_kernel, in_specs=[pl.BlockSpec(memory_space=p...  8.88 us
    all_to_all x1, waiting for transfers between devices, steps(): received = lax.all_to_all(send, 'col', 0, 0, tiled=True)  7.69 us
    ppermute x6, waiting for transfers between devices, rounds_x(): lax.ppermute(value, 'x', [(i, (i + step) % 4) for i in range(4)])  6.72 us
    ppermute x6, starting transfers between devices, rounds_x(): lax.ppermute(value, 'x', [(i, (i + step) % 4) for i in range(4)])  6.66 us
  transfers between devices with their start and end apart: 12, of which 7 were waited for; matrix products, arithmetic and copies ran while one was open for 1% of the time, Pallas kernels for 18%

profile of v5, /device:TPU:1, one launch (start us, length us, event | category | flops | bytes accessed | tf_op | source)
XLA Modules:
  0.0 110.3 jit_solution(947670428839519770)
XLA Ops:
  0.7 2.7 %prepare.1 = (bf16[2,2,8,256]{3,2,1,0:T(8,128)(2,1)S(1)}, bf16[4,2,16,2,8,128]{5,4,3,2,1,0:T(8,128)(2,1)}, bf16[2,8,1280]{2,1,0:T(8,128)(2,1)S(1)}, bf16[2,8,1280]{2,1,0:T(8,128)(2,1)S(1)}) custom-call(bf16[2,2,2,8,1024]{4,3,2,1,0:T(8,128)(2,1)} %inverse.1, bf16[2,2,1024,256]{3,2,1,0:T(8,128)(2,1)} %rhs.2, bf16[2,2,8,1024]{3,2,1,0:T(8,128)(2,1)} %below.1, ...), custom_call_target="tpu_custom_call" | custom-call | tf_op jit(solution)/shard_map/prepare/pallas_call | solution.py:84
  3.3 11.5 %all-to-all-start = ((bf16[128,2,8,128]{3,2,1,0:T(8,128)(2,1)}), bf16[128,2,8,128]{3,2,1,0:T(8,128)(2,1)S(1)}, u32[]{:S(2)}, u32[]{:S(2)}) async-start(bf16[128,2,8,128]{3,2,1,0:T(8,128)(2,1)} %bitcast.4), calls=%async_computation | async-start | bytes 1048576 | tf_op jit(solution)/shard_map/all_to_all | solution.py:501
  14.8 1.1 %collective-permute-start = (bf16[2,8,1280]{2,1,0:T(8,128)(2,1)S(1)}, bf16[2,8,1280]{2,1,0:T(8,128)(2,1)S(1)}, u32[]{:S(2)}, u32[]{:S(2)}) collective-permute-start(bf16[2,8,1280]{2,1,0:T(8,128)(2,1)S(1)} %get-tuple-element.20), channel_id=1, source_target_pairs={{0,16},{16,0},{1,17},{17,1},{2,18},{18,2},{3,19},{19,3},{4,20},{20... | collective-permute-start | bytes 122888 | tf_op jit(solution)/shard_map/ppermute | solution.py:467
  16.0 0.1 copy.22
  16.1 0.1 reshape.28
  16.2 0.7 gather_fusion
  17.1 2.0 %collective-permute-start.3 = (bf16[2,2,8,1280]{3,2,1,0:T(8,128)(2,1)S(1)}, bf16[2,2,8,1280]{3,2,1,0:T(8,128)(2,1)S(1)}, u32[]{:S(2)}, u32[]{:S(2)}) collective-permute-start(bf16[2,2,8,1280]{3,2,1,0:T(8,128)(2,1)S(1)} %maximum_select_fusion.rows0), channel_id=1, source_target_pairs={{0,96},{32,0},{64,32},{96,64},{1,97},{33,1},{65,33},{97,65},{2,98}... | collective-permute-start | bytes 245768 | tf_op jit(solution)/shard_map/ppermute | solution.py:462
  19.1 0.6 collective-permute-start.2
  19.7 0.6 collective-permute-start.1
  20.3 3.2 %collective-permute-done.3.rows3 = bf16[2,2,8,1280]{3,2,1,0:T(8,128)(2,1)S(1)} collective-permute-done((bf16[2,2,8,1280]{3,2,1,0:T(8,128)(2,1)S(1)}, bf16[2,2,8,1280]{3,2,1,0:T(8,128)(2,1)S(1)}, u32[]{:S(2)}, u32[]{:S(2)}) %collective-permute-start.3) | collective-permute-done | bytes 81952 | tf_op jit(solution)/shard_map/ppermute | solution.py:462
  23.6 1.5 %collective-permute-done.2.rows2 = bf16[2,2,8,1280]{3,2,1,0:T(8,128)(2,1)S(1)} collective-permute-done((bf16[2,2,8,1280]{3,2,1,0:T(8,128)(2,1)S(1)}, bf16[2,2,8,1280]{3,2,1,0:T(8,128)(2,1)S(1)}, u32[]{:S(2)}, u32[]{:S(2)}) %collective-permute-start.2) | collective-permute-done | bytes 81952 | tf_op jit(solution)/shard_map/ppermute | solution.py:462
  25.1 2.0 %collective-permute-done.1.rows1 = bf16[2,2,8,1280]{3,2,1,0:T(8,128)(2,1)S(1)} collective-permute-done((bf16[2,2,8,1280]{3,2,1,0:T(8,128)(2,1)S(1)}, bf16[2,2,8,1280]{3,2,1,0:T(8,128)(2,1)S(1)}, u32[]{:S(2)}, u32[]{:S(2)}) %collective-permute-start.1) | collective-permute-done | bytes 81952 | tf_op jit(solution)/shard_map/ppermute | solution.py:462
  27.1 2.0 %all-to-all-done.received = bf16[128,2,8,128]{3,2,1,0:T(8,128)(2,1)S(1)} async-done(((bf16[128,2,8,128]{3,2,1,0:T(8,128)(2,1)}), bf16[128,2,8,128]{3,2,1,0:T(8,128)(2,1)S(1)}, u32[]{:S(2)}, u32[]{:S(2)}) %all-to-all-start) | async-done | bytes 524320 | tf_op jit(solution)/shard_map/all_to_all | solution.py:501
  29.1 1.6 %right_side.1 = (bf16[1024,128]{1,0:T(8,128)(2,1)S(1)}, bf16[16,64,128]{2,1,0:T(8,128)(2,1)}) custom-call(s32[4]{0:T(128)S(1)} %pad_add_fusion.place, bf16[128,2,8,128]{3,2,1,0:T(8,128)(2,1)S(1)} %all-to-all-done.received, bf16[2,2,8,1280]{3,2,1,0:T(8,128)(2,1)S(1)} %maximum_select_fusion.rows0, bf16[2,2,8,1280]{3,2,1,0:T(8,128)(2,1)S(1)} %collective-permute-done.1.rows1, ...), custom_call_target="tpu_custom_call" | custom-call | tf_op jit(solution)/shard_map/right_side/pallas_call | solution.py:133
  30.7 5.0 %all-to-all-start.1 = ((bf16[16,64,128]{2,1,0:T(8,128)(2,1)}), bf16[16,64,128]{2,1,0:T(8,128)(2,1)S(1)}, u32[]{:S(2)}, u32[]{:S(2)}) async-start(bf16[16,64,128]{2,1,0:T(8,128)(2,1)} %get-tuple-element.21), calls=%async_computation.1 | async-start | bytes 524288 | tf_op jit(solution)/shard_map/all_to_all | solution.py:509
  35.7 0.1 reshape.22
  35.8 0.1 concatenate.4.tile
  35.9 7.7 %all-to-all-done.1.received = bf16[16,64,128]{2,1,0:T(8,128)(2,1)S(1)} async-done(((bf16[16,64,128]{2,1,0:T(8,128)(2,1)}), bf16[16,64,128]{2,1,0:T(8,128)(2,1)S(1)}, u32[]{:S(2)}, u32[]{:S(2)}) %all-to-all-start.1) | async-done | bytes 262176 | tf_op jit(solution)/shard_map/all_to_all | solution.py:509
  43.6 2.0 %second_rows.1 = bf16[64,72,128]{2,1,0:T(8,128)(2,1)} custom-call(s32[4]{0:T(128)S(1)} %pad_add_fusion.place, bf16[16,64,128]{2,1,0:T(8,128)(2,1)S(1)} %all-to-all-done.1.received, bf16[2,2,8,1280]{3,2,1,0:T(8,128)(2,1)S(1)} %maximum_select_fusion.rows0, bf16[2,2,8,1280]{3,2,1,0:T(8,128)(2,1)S(1)} %collective-permute-done.1.rows1, ...), custom_call_target="tpu_custom_call" | custom-call | tf_op jit(solution)/shard_map/second_rows/pallas_call | solution.py:168
  45.6 4.7 %all-to-all-start.2 = ((bf16[64,72,128]{2,1,0:T(8,128)(2,1)}), bf16[64,72,128]{2,1,0:T(8,128)(2,1)S(1)}, u32[]{:S(2)}, u32[]{:S(2)}) async-start(bf16[64,72,128]{2,1,0:T(8,128)(2,1)} %second_rows.1), calls=%async_computation.2 | async-start | bytes 2359296 | tf_op jit(solution)/shard_map/all_to_all | solution.py:515
  50.3 2.5 %collective-permute-start.7 = (bf16[1024,128]{1,0:T(8,128)(2,1)S(1)}, bf16[1024,128]{1,0:T(8,128)(2,1)S(1)}, u32[]{:S(2)}, u32[]{:S(2)}) collective-permute-start(bf16[1024,128]{1,0:T(8,128)(2,1)S(1)} %get-tuple-element.22), channel_id=1, source_target_pairs={{0,96},{32,0},{64,32},{96,64},{1,97},{33,1},{65,33},{97,65},{2,98}... | collective-permute-start | bytes 786440 | tf_op jit(solution)/shard_map/ppermute | solution.py:462
  52.8 0.4 collective-permute-start.6
  53.1 0.7 collective-permute-start.5
  53.8 13.8 %all-to-all-done.2 = bf16[64,72,128]{2,1,0:T(8,128)(2,1)S(1)} async-done(((bf16[64,72,128]{2,1,0:T(8,128)(2,1)}), bf16[64,72,128]{2,1,0:T(8,128)(2,1)S(1)}, u32[]{:S(2)}, u32[]{:S(2)}) %all-to-all-start.2) | async-done | bytes 1179680 | tf_op jit(solution)/shard_map/all_to_all | solution.py:515
  67.6 9.3 %collective-permute-start.4 = (bf16[64,72,128]{2,1,0:T(8,128)(2,1)S(1)}, bf16[64,72,128]{2,1,0:T(8,128)(2,1)S(1)}, u32[]{:S(2)}, u32[]{:S(2)}) collective-permute-start(bf16[64,72,128]{2,1,0:T(8,128)(2,1)S(1)} %all-to-all-done.2), channel_id=1, source_target_pairs={{0,16},{16,0},{1,17},{17,1},{2,18},{18,2},{3,19},{19,3},{4,20},{20... | collective-permute-start | bytes 3538952 | tf_op jit(solution)/shard_map/ppermute | solution.py:467
  76.9 0.1 pad_maximum_fusion.mine
  77.0 1.4 %collective-permute-start.8 = (bf16[4,1024,128]{2,1,0:T(8,128)(2,1)S(1)}, bf16[4,1024,128]{2,1,0:T(8,128)(2,1)S(1)}, u32[]{:S(2)}, u32[]{:S(2)}) collective-permute-start(bf16[4,1024,128]{2,1,0:T(8,128)(2,1)S(1)} %pad_maximum_fusion.mine), channel_id=1, source_target_pairs={{0,16},{16,0},{1,17},{17,1},{2,18},{18,2},{3,19},{19,3},{4,20},{20... | collective-permute-start | bytes 3145736 | tf_op jit(solution)/shard_map/ppermute | solution.py:467
  78.5 2.4 %collective-permute-done.8.theirs = bf16[4,1024,128]{2,1,0:T(8,128)(2,1)S(1)} collective-permute-done((bf16[4,1024,128]{2,1,0:T(8,128)(2,1)S(1)}, bf16[4,1024,128]{2,1,0:T(8,128)(2,1)S(1)}, u32[]{:S(2)}, u32[]{:S(2)}) %collective-permute-start.8) | collective-permute-done | bytes 1048608 | tf_op jit(solution)/shard_map/ppermute | solution.py:467
  80.8 1.9 %couple_first.1.before = f32[1024,128]{1,0:T(8,128)} custom-call(bf16[4,1024,128]{2,1,0:T(8,128)(2,1)S(1)} %pad_maximum_fusion.mine, bf16[4,1024,128]{2,1,0:T(8,128)(2,1)S(1)} %collective-permute-done.8.theirs), custom_call_target="tpu_custom_call" | custom-call | tf_op jit(solution)/shard_map/couple_first/pallas_call | solution.py:431
  82.7 11.9 %trail_first.1 = (f32[2,2,768,256]{3,2,1,0:T(8,128)S(1)}, f32[2,2,256,256]{3,2,1,0:T(8,128)}) custom-call(s32[4]{0:T(128)S(1)} %pad_add_fusion.place, bf16[4,1024,128]{2,1,0:T(8,128)(2,1)S(1)} %pad_maximum_fusion.mine, bf16[4,1024,128]{2,1,0:T(8,128)(2,1)S(1)} %collective-permute-done.8.theirs, bf16[2,2,2,1024,1024]{4,3,2,1,0:T(8,128)(2,1)} %factor.5, ...), custom_call_target="tpu_custom_call" | custom-call | tf_op jit(solution)/shard_map/trail_first/pallas_call | solution.py:231
  94.6 6.6 %trail_mine.1 = (bf16[2,2,1024,256]{3,2,1,0:T(8,128)(2,1)}, bf16[2,8,256]{2,1,0:T(8,128)(2,1)S(1)}, bf16[1024,512]{1,0:T(8,128)(2,1)S(1)}, bf16[4,128,128]{2,1,0:T(8,128)(2,1)S(1)}) custom-call(s32[4]{0:T(128)S(1)} %pad_add_fusion.place, bf16[4,16,72,128]{3,2,1,0:T(8,128)(2,1)S(1)} %bitcast.15, bf16[2,2,2,1024,1024]{4,3,2,1,0:T(8,128)(2,1)} %factor.5, ...), custom_call_target="tpu_custom_call" | custom-call | tf_op jit(solution)/shard_map/trail_mine/pallas_call | solution.py:337
  101.3 8.9 %trail_theirs.1 = (bf16[2,2,1024,256]{3,2,1,0:T(8,128)(2,1)}, bf16[2,2,2,8,256]{4,3,2,1,0:T(8,128)(2,1)}, f32[3,8]{1,0:T(4,128)}) custom-call(s32[4]{0:T(128)S(1)} %pad_add_fusion.place, bf16[4,16,72,128]{3,2,1,0:T(8,128)(2,1)S(1)} %bitcast.16, bf16[2,2,2,1024,1024]{4,3,2,1,0:T(8,128)(2,1)} %factor.5, ...), custom_call_target="tpu_custom_call", output_to_operand_aliasing={{0}: (11, {})} | custom-call | tf_op jit(solution)/shard_map/trail_theirs/pallas_call | solution.py:374
  (26 shorter events, 0.3 us)
Async XLA Ops:
  0.6 15.6 %copy-start = (s32[1024]{0:T(1024)S(1)}, s32[1024]{0:T(1024)}, u32[]{:S(2)}) copy-start(s32[1024]{0:T(1024)} %param.18) | copy-start | bytes 12292
  0.6 15.3 %copy-start.4 = (s32[2,8,3]{1,0,2:T(2,128)S(1)}, s32[2,8,3]{1,0,2:T(2,128)}, u32[]{:S(2)}) copy-start(s32[2,8,3]{1,0,2:T(2,128)} %param.17) | copy-start | bytes 580
  3.3 25.8 %all-to-all-start = ((bf16[128,2,8,128]{3,2,1,0:T(8,128)(2,1)}), bf16[128,2,8,128]{3,2,1,0:T(8,128)(2,1)S(1)}, u32[]{:S(2)}, u32[]{:S(2)}) async-start(bf16[128,2,8,128]{3,2,1,0:T(8,128)(2,1)} %bitcast.4), calls=%async_computation | async-start | bytes 1048576 | tf_op jit(solution)/shard_map/all_to_all | solution.py:501
  14.8 2.3 %collective-permute-start = (bf16[2,8,1280]{2,1,0:T(8,128)(2,1)S(1)}, bf16[2,8,1280]{2,1,0:T(8,128)(2,1)S(1)}, u32[]{:S(2)}, u32[]{:S(2)}) collective-permute-start(bf16[2,8,1280]{2,1,0:T(8,128)(2,1)S(1)} %get-tuple-element.20), channel_id=1, source_target_pairs={{0,16},{16,0},{1,17},{17,1},{2,18},{18,2},{3,19},{19,3},{4,20},{20... | collective-permute-start | bytes 122888 | tf_op jit(solution)/shard_map/ppermute | solution.py:467
  16.2 19.5 %copy-start.3 = (f32[2,9,2,8]{1,3,2,0:T(8,128)S(1)}, f32[2,9,2,8]{1,3,2,0:T(8,128)}, u32[]{:S(2)}) copy-start(f32[2,9,2,8]{1,3,2,0:T(8,128)} %param.16) | copy-start | bytes 3460
  17.1 6.4 %collective-permute-start.3 = (bf16[2,2,8,1280]{3,2,1,0:T(8,128)(2,1)S(1)}, bf16[2,2,8,1280]{3,2,1,0:T(8,128)(2,1)S(1)}, u32[]{:S(2)}, u32[]{:S(2)}) collective-permute-start(bf16[2,2,8,1280]{3,2,1,0:T(8,128)(2,1)S(1)} %maximum_select_fusion.rows0), channel_id=1, source_target_pairs={{0,96},{32,0},{64,32},{96,64},{1,97},{33,1},{65,33},{97,65},{2,98}... | collective-permute-start | bytes 245768 | tf_op jit(solution)/shard_map/ppermute | solution.py:462
  19.1 6.0 %collective-permute-start.2 = (bf16[2,2,8,1280]{3,2,1,0:T(8,128)(2,1)S(1)}, bf16[2,2,8,1280]{3,2,1,0:T(8,128)(2,1)S(1)}, u32[]{:S(2)}, u32[]{:S(2)}) collective-permute-start(bf16[2,2,8,1280]{3,2,1,0:T(8,128)(2,1)S(1)} %maximum_select_fusion.rows0), channel_id=1, source_target_pairs={{0,64},{32,96},{64,0},{96,32},{1,65},{33,97},{65,1},{97,33},{2,66}... | collective-permute-start | bytes 245768 | tf_op jit(solution)/shard_map/ppermute | solution.py:462
  19.7 7.4 %collective-permute-start.1 = (bf16[2,2,8,1280]{3,2,1,0:T(8,128)(2,1)S(1)}, bf16[2,2,8,1280]{3,2,1,0:T(8,128)(2,1)S(1)}, u32[]{:S(2)}, u32[]{:S(2)}) collective-permute-start(bf16[2,2,8,1280]{3,2,1,0:T(8,128)(2,1)S(1)} %maximum_select_fusion.rows0), channel_id=1, source_target_pairs={{0,32},{32,64},{64,96},{96,0},{1,33},{33,65},{65,97},{97,1},{2,34}... | collective-permute-start | bytes 245768 | tf_op jit(solution)/shard_map/ppermute | solution.py:462
  30.7 12.9 %all-to-all-start.1 = ((bf16[16,64,128]{2,1,0:T(8,128)(2,1)}), bf16[16,64,128]{2,1,0:T(8,128)(2,1)S(1)}, u32[]{:S(2)}, u32[]{:S(2)}) async-start(bf16[16,64,128]{2,1,0:T(8,128)(2,1)} %get-tuple-element.21), calls=%async_computation.1 | async-start | bytes 524288 | tf_op jit(solution)/shard_map/all_to_all | solution.py:509
  45.6 22.0 %all-to-all-start.2 = ((bf16[64,72,128]{2,1,0:T(8,128)(2,1)}), bf16[64,72,128]{2,1,0:T(8,128)(2,1)S(1)}, u32[]{:S(2)}, u32[]{:S(2)}) async-start(bf16[64,72,128]{2,1,0:T(8,128)(2,1)} %second_rows.1), calls=%async_computation.2 | async-start | bytes 2359296 | tf_op jit(solution)/shard_map/all_to_all | solution.py:515
  50.3 26.6 %collective-permute-start.7 = (bf16[1024,128]{1,0:T(8,128)(2,1)S(1)}, bf16[1024,128]{1,0:T(8,128)(2,1)S(1)}, u32[]{:S(2)}, u32[]{:S(2)}) collective-permute-start(bf16[1024,128]{1,0:T(8,128)(2,1)S(1)} %get-tuple-element.22), channel_id=1, source_target_pairs={{0,96},{32,0},{64,32},{96,64},{1,97},{33,1},{65,33},{97,65},{2,98}... | collective-permute-start | bytes 786440 | tf_op jit(solution)/shard_map/ppermute | solution.py:462
  52.8 24.1 %collective-permute-start.6 = (bf16[1024,128]{1,0:T(8,128)(2,1)S(1)}, bf16[1024,128]{1,0:T(8,128)(2,1)S(1)}, u32[]{:S(2)}, u32[]{:S(2)}) collective-permute-start(bf16[1024,128]{1,0:T(8,128)(2,1)S(1)} %get-tuple-element.22), channel_id=1, source_target_pairs={{0,64},{32,96},{64,0},{96,32},{1,65},{33,97},{65,1},{97,33},{2,66}... | collective-permute-start | bytes 786440 | tf_op jit(solution)/shard_map/ppermute | solution.py:462
  53.1 23.7 %collective-permute-start.5 = (bf16[1024,128]{1,0:T(8,128)(2,1)S(1)}, bf16[1024,128]{1,0:T(8,128)(2,1)S(1)}, u32[]{:S(2)}, u32[]{:S(2)}) collective-permute-start(bf16[1024,128]{1,0:T(8,128)(2,1)S(1)} %get-tuple-element.22), channel_id=1, source_target_pairs={{0,32},{32,64},{64,96},{96,0},{1,33},{33,65},{65,97},{97,1},{2,34}... | collective-permute-start | bytes 786440 | tf_op jit(solution)/shard_map/ppermute | solution.py:462
  67.6 33.7 %collective-permute-start.4 = (bf16[64,72,128]{2,1,0:T(8,128)(2,1)S(1)}, bf16[64,72,128]{2,1,0:T(8,128)(2,1)S(1)}, u32[]{:S(2)}, u32[]{:S(2)}) collective-permute-start(bf16[64,72,128]{2,1,0:T(8,128)(2,1)S(1)} %all-to-all-done.2), channel_id=1, source_target_pairs={{0,16},{16,0},{1,17},{17,1},{2,18},{18,2},{3,19},{19,3},{4,20},{20... | collective-permute-start | bytes 3538952 | tf_op jit(solution)/shard_map/ppermute | solution.py:467
  77.0 3.8 %collective-permute-start.8 = (bf16[4,1024,128]{2,1,0:T(8,128)(2,1)S(1)}, bf16[4,1024,128]{2,1,0:T(8,128)(2,1)S(1)}, u32[]{:S(2)}, u32[]{:S(2)}) collective-permute-start(bf16[4,1024,128]{2,1,0:T(8,128)(2,1)S(1)} %pad_maximum_fusion.mine), channel_id=1, source_target_pairs={{0,16},{16,0},{1,17},{17,1},{2,18},{18,2},{3,19},{19,3},{4,20},{20... | collective-permute-start | bytes 3145736 | tf_op jit(solution)/shard_map/ppermute | solution.py:467
  94.6 6.6 %copy-start.1 = (f32[1024,128]{1,0:T(8,128)S(1)}, f32[1024,128]{1,0:T(8,128)}, u32[]{:S(2)}) copy-start(f32[1024,128]{1,0:T(8,128)} %couple_first.1.before) | copy-start | bytes 1572868
  94.6 6.6 %copy-start.2 = (bf16[128,768]{1,0:T(8,128)(2,1)S(1)}, bf16[128,768]{1,0:T(8,128)(2,1)}, u32[]{:S(2)}) copy-start(bf16[128,768]{1,0:T(8,128)(2,1)} %constant.54.clone.spread) | copy-start | bytes 589828

commit v6 on v5

--- a/solution.py
+++ b/solution.py
@@ -11,7 +11,6 @@
 ALL = ("x", "core", "col")
 F32 = jnp.float32
 BF16 = jnp.bfloat16
-TRAIL_VMEM = 24 * 1024 * 1024
 SMALL_VMEM = 12 * 1024 * 1024
 SPACE = pltpu.VMEM
 
@@ -175,89 +174,93 @@
     )(place, received, *rows, tile)
 
 
+def set_blocks(blocks, at, parts):
+    for half in range(2):
+        real, imag = pair_lanes(parts[2 * half], parts[2 * half + 1])
+        blocks[at : at + 128, 128 * half : 128 * half + 128] = real.astype(BF16)
+        blocks[at : at + 128, 256 + 128 * half : 384 + 128 * half] = imag.astype(BF16)
+
+
 def trail_product(stacked, blocks):
     height = stacked.shape[0] // 2
     product = jnp.dot(stacked, blocks[...], preferred_element_type=F32)
-    real, imag = [], []
-    for half in range(2):
-        lanes = slice(256 * half, 256 * half + 128)
-        even, even_turned = product[:height, lanes], product[height:, lanes]
-        lanes = slice(256 * half + 128, 256 * half + 256)
-        odd, odd_turned = product[:height, lanes], product[height:, lanes]
-        low = lanes_below(even.shape, 64)
-        turn = lambda value: pltpu.roll(value, 64, 1)
-        real.append(jnp.where(low, even - turn(even_turned), turn(odd) - odd_turned))
-        imag.append(jnp.where(low, turn(even) + even_turned, odd + turn(odd_turned)))
-    return jnp.concatenate(real, axis=1), jnp.concatenate(imag, axis=1)
-
-
-def trail_first_kernel(place, mine, theirs, factor, rhs, near, far, blocks):
-    x = place[0]
-    turn = pl.program_id(0)
-    step = pl.program_id(1)
-    system = jnp.where(turn == 0, place[1], 1 - place[1])
-
-    @pl.when((turn == 0) & (step == 0))
-    def _():
-        for q in range(4):
-            blocks[:, 128 * q : 128 * q + 128] = mine[lax.rem(x - q + 4, 4)]
-
-    @pl.when((turn == 1) & (step == 0))
-    def _():
-        for q in range(4):
-            blocks[:, 128 * q : 128 * q + 128] = theirs[lax.rem(x - q + 4, 4)]
-
-    height = factor.shape[3]
-    real, imag = trail_product(factor[0, 0].reshape(2 * height, 1024), blocks)
-    real = rhs[0, 0].astype(F32) - real
-    imag = rhs[0, 1].astype(F32) - imag
-
-    @pl.when(step < 3)
-    def _():
-        rows = pl.ds(pl.multiple_of(height * step, height), height)
-        near[system, 0, rows, :] = real
-        near[system, 1, rows, :] = imag
-
-    @pl.when(step == 3)
-    def _():
-        far[0, 0] = real
-        far[0, 1] = imag
+    top, low = product[:height], product[height:]
+    return top[:, :256] - low[:, 256:], top[:, 256:] + low[:, :256]
+
+
+def trail_first_kernel(place, mine, theirs, factor, rhs, total, before, early, blocks, rows, start, done, sems):
+    x, core = place[0], place[1]
+    height = rows.shape[3]
+    copy = pltpu.make_async_copy
+    cuts = [pl.ds(i * height, height) for i in range(4)]
+    systems = (core, 1 - core)
+    take = [
+        [
+            *(copy(factor.at[systems[t], 0, :, cuts[i]], rows.at[t, i], sems.at[t, i]) for i in range(4)),
+            copy(rhs.at[systems[t]], start.at[t], sems.at[t, 4]),
+        ]
+        for t in range(2)
+    ]
+    give = [copy(done.at[t], total.at[systems[t]], sems.at[t, 5]) for t in range(2)]
+    take_early = [copy(factor.at[core, 1, :, cuts[i]], early.at[i], sems.at[2, i]) for i in range(2)]
+    for one in (*take[0], *take[1], *take_early):
+        one.start()
+    for t, source in enumerate((mine, theirs)):
+        for row in range(8):
+            cut = slice(128 * row, 128 * row + 128)
+            parts = [source[lax.rem(x - q + 4, 4), cut, :].astype(F32) for q in range(4)]
+            set_blocks(blocks.at[t], 128 * row, parts)
+    for t in range(2):
+        for one in take[t]:
+            one.wait()
+        for i in range(4):
+            real, imag = trail_product(rows[t, i].reshape(2 * height, 1024), blocks.at[t])
+            cut = slice(i * height, i * height + height)
+            done[t, 0, cut, :] = start[t, 0, cut, :].astype(F32) - real
+            done[t, 1, cut, :] = start[t, 1, cut, :].astype(F32) - imag
+        give[t].start()
+    low = lanes_below((128, 128), 64)
+    for row in range(8):
+        cut = slice(128 * row, 128 * row + 128)
+        real, imag = couple(blocks[0, cut, :], blocks[1, cut, :])
+        before[cut, :] = jnp.where(low, real, imag)
+    for one in (*take_early, *give):
+        one.wait()
 
 
 def trail_first(place, mine, theirs, trail_factor, trail_rhs):
     rows = trail_rhs.shape[2]
     height = rows // 4
-    system = lambda turn, p: jnp.where(turn == 0, p[1], 1 - p[1])
+    inside = pl.BlockSpec(memory_space=pltpu.VMEM)
+    outside = pl.BlockSpec(memory_space=pltpu.HBM)
     return pl.pallas_call(
         trail_first_kernel,
-        grid_spec=pltpu.PrefetchScalarGridSpec(
-            num_scalar_prefetch=1,
-            grid=(2, 4),
-            in_specs=[pl.BlockSpec((4, 1024, 128), lambda t, i, p: (0, 0, 0))] * 2
-            + [
-                pl.BlockSpec((1, 1, 2, height, 1024), lambda t, i, p: (system(t, p), 0, 0, i, 0)),
-                pl.BlockSpec((1, 2, height, 256), lambda t, i, p: (system(t, p), 0, i, 0)),
-            ],
-            out_specs=[
-                pl.BlockSpec(memory_space=pltpu.VMEM),
-                pl.BlockSpec((1, 2, height, 256), lambda t, i, p: (system(t, p), 0, 0, 0)),
-            ],
-            scratch_shapes=[pltpu.VMEM((1024, 512), BF16)],
-        ),
+        in_specs=[pl.BlockSpec(memory_space=pltpu.SMEM), inside, inside, outside, outside],
+        out_specs=[outside, inside, inside],
         out_shape=[
-            pltpu.VMEM((2, 2, 3 * height, 256), F32),
-            pltpu.HBM((2, 2, height, 256), F32),
-        ],
-        compiler_params=pltpu.CompilerParams(vmem_limit_bytes=TRAIL_VMEM),
+            pltpu.HBM((2, 2, rows, 256), F32),
+            pltpu.HBM((1024, 128), F32),
+            pltpu.VMEM((2, 2, height, 1024), BF16),
+        ],
+        scratch_shapes=[
+            pltpu.VMEM((2, 1024, 512), BF16),
+            pltpu.VMEM((2, 4, 2, height, 1024), BF16),
+            pltpu.VMEM((2, 2, rows, 256), BF16),
+            pltpu.VMEM((2, 2, rows, 256), F32),
+            pltpu.SemaphoreType.DMA((3, 6)),
+        ],
+        compiler_params=pltpu.CompilerParams(vmem_limit_bytes=28 * 1024 * 1024),
         name="trail_first",
     )(place, mine, theirs, trail_factor, trail_rhs)
 
 
 def take_blocks(place, received, blocks, tiles):
+    for row in range(8):
+        parts = [
+            received[q, :, 8 * row : 8 * row + 8, :].astype(F32).reshape(128, 128) for q in range(4)
+        ]
+        set_blocks(blocks, 128 * row, parts)
     for q in range(4):
-        for row in range(8):
-            value = received[q, :, 8 * row : 8 * row + 8, :].astype(F32).reshape(128, 128)
-            blocks[128 * row : 128 * row + 128, 128 * q : 128 * q + 128] = value.astype(BF16)
         tiles[q] = received[q, :, 64:, :].astype(F32).reshape(128, 128).astype(BF16)
     near = pl.multiple_of(8 * place[2], 8)
     parts = [received[q, place[3], pl.ds(near, 8), :].astype(F32) for q in range(4)]
@@ -267,127 +270,123 @@
     ]
 
 
-class Trail:
-    scratch = staticmethod(
-        lambda height: [
-            pltpu.VMEM((4, 16, 72, 128), BF16),
-            pltpu.VMEM((4, 2, height, 1024), BF16),
-            pltpu.VMEM((2, height, 256), F32),
-            pltpu.VMEM((4, 2, height, 256), BF16),
-            pltpu.SemaphoreType.DMA((10,)),
-        ]
-    )
-
-    def __init__(self, system, received, factor, near, far, out, scratch):
-        arrived, rows, last, done, sems = scratch
-        height = last.shape[1]
-        self.system, self.near, self.height = system, near, height
-        self.arrived, self.rows, self.last, self.done = arrived, rows, last, done
-        copy = pltpu.make_async_copy
-        self.take = copy(received, arrived, sems.at[0])
-        self.take_last = copy(far.at[system], last, sems.at[1])
-        self.take_rows = [
-            copy(factor.at[system, 1, :, pl.ds(i * height, height)], rows.at[i], sems.at[2 + i])
-            for i in range(4)
-        ]
-        self.give = [
-            copy(done.at[i], out.at[system, :, pl.ds(i * height, height)], sems.at[6 + i])
-            for i in range(4)
-        ]
-
-    def start(self):
-        self.take.start()
-        for one in self.take_rows:
-            one.start()
-        self.take_last.start()
-
-    def run(self, blocks):
-        height = self.height
-        for i in range(4):
-            self.take_rows[i].wait()
-            real, imag = trail_product(self.rows[i].reshape(2 * height, 1024), blocks)
-            if i < 3:
-                cut = slice(i * height, i * height + height)
-                before = (self.near[self.system, 0, cut, :], self.near[self.system, 1, cut, :])
-            else:
-                self.take_last.wait()
-                before = (self.last[0], self.last[1])
-            self.done[i, 0] = (before[0] - real).astype(BF16)
-            self.done[i, 1] = (before[1] - imag).astype(BF16)
-            self.give[i].start()
-
-    def finish(self):
-        for one in self.give:
-            one.wait()
-
-
-def trail_mine_kernel(place, received, factor, near, far, out, own, blocks, tiles, *scratch):
-    trail = Trail(place[1], received, factor, near, far, out, scratch)
-    trail.start()
-    trail.take.wait()
-    own[0], own[1] = take_blocks(place, trail.arrived, blocks, tiles)
-    trail.run(blocks)
-    trail.finish()
-
-
-def trail_mine(place, received, trail_factor, near, far):
-    height = far.shape[2]
+def finish_rows(i, product, before, done):
+    height = done.shape[2]
+    cut = slice(i * height, i * height + height)
+    done[i, 0] = (before[0, cut, :] - product[0]).astype(BF16)
+    done[i, 1] = (before[1, cut, :] - product[1]).astype(BF16)
+
+
+def trail_mine_kernel(
+    place, received, factor, early, total, out, own, blocks, tiles, later, rest, arrived, rows, before, done, sems
+):
+    core = place[1]
+    height = rows.shape[1] // 2
+    copy = pltpu.make_async_copy
+    cuts = [pl.ds(i * height, height) for i in range(4)]
+    take = copy(received, arrived, sems.at[0])
+    take_row = copy(factor.at[core, 1, :, pl.ds(2 * height, 2 * height)], rows, sems.at[1])
+    take_before = copy(total.at[core], before, sems.at[2])
+    take_rest = copy(total.at[1 - core], rest, sems.at[3])
+    give = [copy(done.at[i], out.at[core, :, cuts[i]], sems.at[4 + i]) for i in range(4)]
+    take_later = [
+        copy(factor.at[1 - core, 1, :, cuts[i]], later.at[i], sems.at[8 + i]) for i in range(4)
+    ]
+    take.start()
+    take.wait()
+    for one in (take_row, take_before, *take_later, take_rest):
+        one.start()
+    own[0], own[1] = take_blocks(place, arrived, blocks, tiles)
+    products = [trail_product(early[i].reshape(2 * height, 1024), blocks) for i in range(2)]
+    take_row.wait()
+    take_before.wait()
+    for i in range(2):
+        cut = slice(i * height, i * height + height)
+        products.append(trail_product(rows[:, cut, :].reshape(2 * height, 1024), blocks))
+    for i in range(4):
+        finish_rows(i, products[i], before, done)
+        give[i].start()
+    for one in (*take_later, take_rest, *give):
+        one.wait()
+
+
+def trail_mine(place, received, trail_factor, early, total):
+    rows = total.shape[2]
+    height = rows // 4
     inside = pl.BlockSpec(memory_space=pltpu.VMEM)
     outside = pl.BlockSpec(memory_space=pltpu.HBM)
     return pl.pallas_call(
         trail_mine_kernel,
         in_specs=[pl.BlockSpec(memory_space=pltpu.SMEM), outside, outside, inside, outside],
-        out_specs=[outside, inside, inside, inside],
+        out_specs=[outside] + [inside] * 5,
         out_shape=[
-            pltpu.HBM((2, 2, 4 * height, 256), BF16),
+            pltpu.HBM((2, 2, rows, 256), BF16),
             pltpu.VMEM((2, 8, 256), BF16),
             pltpu.VMEM((1024, 512), BF16),
             pltpu.VMEM((4, 128, 128), BF16),
-        ],
-        scratch_shapes=Trail.scratch(height),
-        compiler_params=pltpu.CompilerParams(vmem_limit_bytes=TRAIL_VMEM),
+            pltpu.VMEM((4, 2, height, 1024), BF16),
+            pltpu.VMEM((2, rows, 256), F32),
+        ],
+        scratch_shapes=[
+            pltpu.VMEM((4, 16, 72, 128), BF16),
+            pltpu.VMEM((2, 2 * height, 1024), BF16),
+            pltpu.VMEM((2, rows, 256), F32),
+            pltpu.VMEM((4, 2, height, 256), BF16),
+            pltpu.SemaphoreType.DMA((12,)),
+        ],
+        compiler_params=pltpu.CompilerParams(vmem_limit_bytes=14 * 1024 * 1024),
         name="trail_mine",
-    )(place, received, trail_factor, near, far)
+    )(place, received, trail_factor, early, total)
 
 
 def trail_theirs_kernel(
-    place, received, factor, near, far, mine, mine_tiles, own, first, before, spread, _, out, panel, gradient, blocks, tiles, *scratch
+    place, received, rows, rest, mine, mine_tiles, own, first, before, spread, _, out, panel, gradient, blocks, tiles, done, sems
 ):
     core = place[1]
-    trail = Trail(1 - core, received, factor, near, far, out, scratch)
-    trail.start()
+    height = rows.shape[2]
+    give = [
+        pltpu.make_async_copy(
+            done.at[i], out.at[1 - core, :, pl.ds(i * height, height)], sems.at[i]
+        )
+        for i in range(4)
+    ]
     panel[:, 0] = first[...]
     panel[core, 1] = own[...]
-    trail.take.wait()
-    real, imag = take_blocks(place, trail.arrived, blocks, tiles)
+    real, imag = take_blocks(place, received, blocks, tiles)
     panel[1 - core, 1, 0] = real
     panel[1 - core, 1, 1] = imag
-    trail.run(blocks)
+    for i in range(4):
+        product = trail_product(rows[i].reshape(2 * height, 1024), blocks)
+        finish_rows(i, product, rest, done)
+        give[i].start()
     slot_gradient(place, mine, blocks, (mine_tiles, tiles), before, spread, gradient)
-    trail.finish()
-
-
-def trail_theirs(place, received, trail_factor, near, far, mine, mine_tiles, own, first, before, spread, update):
-    height = far.shape[2]
+    for one in give:
+        one.wait()
+
+
+def trail_theirs(place, received, later, rest, mine, mine_tiles, own, first, before, spread, update):
+    height = later.shape[2]
     inside = pl.BlockSpec(memory_space=pltpu.VMEM)
     outside = pl.BlockSpec(memory_space=pltpu.HBM)
     return pl.pallas_call(
         trail_theirs_kernel,
-        in_specs=[pl.BlockSpec(memory_space=pltpu.SMEM), outside, outside, inside, outside]
-        + [inside] * 6
-        + [outside],
+        in_specs=[pl.BlockSpec(memory_space=pltpu.SMEM)] + [inside] * 9 + [outside],
         out_specs=[outside, inside, inside],
         out_shape=[
-            pltpu.HBM((2, 2, 4 * height, 256), BF16),
+            pltpu.HBM(update.shape, BF16),
             jax.ShapeDtypeStruct((2, 2, 2, 8, 256), BF16),
             jax.ShapeDtypeStruct((3, 8), F32),
         ],
-        scratch_shapes=[pltpu.VMEM((1024, 512), BF16), pltpu.VMEM((4, 128, 128), BF16)]
-        + Trail.scratch(height),
-        input_output_aliases={11: 0},
-        compiler_params=pltpu.CompilerParams(vmem_limit_bytes=TRAIL_VMEM),
+        scratch_shapes=[
+            pltpu.VMEM((1024, 512), BF16),
+            pltpu.VMEM((4, 128, 128), BF16),
+            pltpu.VMEM((4, 2, height, 256), BF16),
+            pltpu.SemaphoreType.DMA((4,)),
+        ],
+        input_output_aliases={10: 0},
+        compiler_params=pltpu.CompilerParams(vmem_limit_bytes=14 * 1024 * 1024),
         name="trail_theirs",
-    )(place, received, trail_factor, near, far, mine, mine_tiles, own, first, before, spread, update)
+    )(place, received, later, rest, mine, mine_tiles, own, first, before, spread, update)
 
 
 def spread_matrix():
@@ -405,50 +404,33 @@
     return jnp.asarray(spread.reshape(128, 768), BF16)
 
 
-def couple(mine, theirs):
-    same = jnp.zeros((128, 128), F32)
-    crossed = jnp.zeros((128, 128), F32)
-    for near, far in zip(mine, theirs):
-        near = near.astype(F32)
-        far = far.astype(F32)
-        same = same + near * far
-        crossed = crossed + near * pltpu.roll(far, 64, 1)
-    low = lanes_below((128, 128), 64)
-    real = jnp.sum(jnp.where(low, same, -same), axis=1, keepdims=True)
-    imag = jnp.sum(crossed, axis=1, keepdims=True)
-    return real, imag
-
-
-def couple_first_kernel(mine, theirs, out):
-    low = lanes_below((128, 128), 64)
-    for row in range(8):
-        cut = slice(128 * row, 128 * row + 128)
-        real, imag = couple([mine[q, cut, :] for q in range(4)], [theirs[q, cut, :] for q in range(4)])
-        out[cut, :] = jnp.where(low, real, imag)
-
-
-def couple_first(mine, theirs):
-    return pl.pallas_call(
-        couple_first_kernel,
-        out_shape=pltpu.HBM((1024, 128), F32),
-        compiler_params=pltpu.CompilerParams(vmem_limit_bytes=TRAIL_VMEM),
-        name="couple_first",
-    )(mine, theirs)
+def couple(near, far):
+    near = near.astype(F32)
+    far = far.astype(F32)
+    near_real, near_imag, far_real, far_imag = near[:, :256], near[:, 256:], far[:, :256], far[:, 256:]
+    real = near_real * far_real - near_imag * far_imag
+    imag = near_real * far_imag + near_imag * far_real
+    sums = jnp.concatenate([real[:, :128] + real[:, 128:], imag[:, :128] + imag[:, 128:]])
+    sums = jnp.broadcast_to(jnp.sum(sums, axis=1, keepdims=True), (256, 128))
+    return sums[:128], sums[128:]
 
 
 def slot_gradient(place, mine, theirs, tiles, before, spread, out):
     base = 8 * (16 * place[2] + place[3])
     target = (base + lax.rem(lax.broadcasted_iota(jnp.int32, (128, 128), 1), 8)).astype(F32)
+    source_lane = lax.broadcasted_iota(jnp.int32, (128, 256), 0)
+    high = lax.broadcasted_iota(jnp.int32, (128, 256), 1) >= 128
+    pick = (source_lane == jnp.where(high, 64, 0)).astype(F32)
     total = jnp.zeros((8, 128), F32)
     for source in range(4):
         for side in range(2):
             row = 2 * source + (place[1] if side == 0 else 1 - place[1])
             cut = pl.ds(pl.multiple_of(128 * row, 128), 128)
-            lanes = [slice(128 * q, 128 * q + 128) for q in range(4)]
-            real, imag = couple([mine[cut, q] for q in lanes], [theirs[cut, q] for q in lanes])
-            first = before[cut, :]
+            value = before[cut, :]
+            first = jnp.concatenate([jnp.broadcast_to(value[:, :1], (128, 128)), jnp.broadcast_to(value[:, 64:65], (128, 128))], axis=1)
+            second = couple(mine[cut, :], theirs[cut, :])
             table = jnp.dot(tiles[side][source], spread[...], preferred_element_type=F32)
-            for at, real, imag in ((0, first[:, :1], first[:, 64:65]), (384, real, imag)):
+            for at, real, imag in ((0, first[:, :128], first[:, 128:]), (384, *second)):
                 value = table[:, at + 128 : at + 256] * imag - table[:, at : at + 128] * real
                 value = jnp.where(table[:, at + 256 : at + 384] == target, value, 0.0)
                 total = total + jnp.sum(value.reshape(16, 8, 128), axis=0)
@@ -514,20 +496,20 @@
     send = second_rows(place, received, rows, tile)
     second_mine = lax.all_to_all(send, ("x", "col"), 0, 0, tiled=True)
 
-    near, far = trail_first(place, first_mine, first_theirs, trail_factor, outside(trail_rhs))
-    far = outside(far)
-    before = couple_first(first_mine, first_theirs)
+    total, before, early = trail_first(
+        place, first_mine, first_theirs, trail_factor, outside(trail_rhs)
+    )
+    total = outside(total)
 
     second_theirs = swap_core(second_mine)
     mine = second_mine.reshape(4, 16, 72, 128)
     theirs = second_theirs.reshape(4, 16, 72, 128)
-    update, own, mine, mine_tiles = trail_mine(place, mine, trail_factor, near, far)
+    update, own, mine, mine_tiles, later, rest = trail_mine(place, mine, trail_factor, early, total)
     update, panel_solution, gradient = trail_theirs(
         place,
         theirs,
-        trail_factor,
-        near,
-        far,
+        later,
+        rest,
         mine,
         mine_tiles,
         own,

time: 111 us -> 103 us (0.928)
  Pallas kernels: 35.6 us -> 28.4 us
    pallas_call x1, Pallas kernels: 8.88 us -> 4.97 us  [trail_theirs(): pl.pallas_call(trail_theirs_kernel, in_specs=[pl.BlockSpec(memory_space=p...]
    pallas_call x2 -> x1, Pallas kernels: 13.8 us -> 10.6 us  [trail_first(): pl.pallas_call(trail_first_kernel, in_specs=[pl.BlockSpec(memory_space=pl...]
    ppermute x6, starting transfers between devices: 6.66 us -> 9.75 us  [rounds_x(): lax.ppermute(value, 'x', [(i, (i + step) % 4) for i in range(4)])]
    ppermute x3, starting transfers between devices: 11.9 us -> 9.47 us  [swap_core(): return lax.ppermute(value, 'core', [(0, 1), (1, 0)])]
    ppermute x6, waiting for transfers between devices: 6.72 us -> 8.21 us  [rounds_x(): lax.ppermute(value, 'x', [(i, (i + step) % 4) for i in range(4)])]
    all_to_all x1, starting transfers between devices: 11.5 us -> 10.2 us  [steps(): lax.all_to_all(send.reshape(128, 2, 8, 128), ALL, 0, 0, tiled=True)]
  transfers between devices with their start and end apart: 12 -> 12, of which waited for: 7 -> 7; matrix products, arithmetic and copies ran while one was open for 1% -> 1% of each run, Pallas kernels for 18% -> 17%
where the time goes in v6:
time: 103 us
  starting transfers between devices  38.9 us (38%)
  waiting for transfers between devices  33.1 us (32%)
  Pallas kernels  28.4 us (28%)
  local copies, waits for them, and re-layouts  1.3 us (1%)
    all_to_all x1, waiting for transfers between devices, steps(): second_mine = lax.all_to_all(send, ('x', 'col'), 0, 0, tiled=True)  12.9 us
    pallas_call x1, Pallas kernels, trail_first(): pl.pallas_call(trail_first_kernel, in_specs=[pl.BlockSpec(memory_space=pl...  10.6 us
    all_to_all x1, starting transfers between devices, steps(): lax.all_to_all(send.reshape(128, 2, 8, 128), ALL, 0, 0, tiled=True)  10.2 us
    ppermute x6, starting transfers between devices, rounds_x(): lax.ppermute(value, 'x', [(i, (i + step) % 4) for i in range(4)])  9.75 us
    ppermute x3, starting transfers between devices, swap_core(): return lax.ppermute(value, 'core', [(0, 1), (1, 0)])  9.47 us
    ppermute x6, waiting for transfers between devices, rounds_x(): lax.ppermute(value, 'x', [(i, (i + step) % 4) for i in range(4)])  8.21 us
    all_to_all x1, waiting for transfers between devices, steps(): received = lax.all_to_all(send, 'col', 0, 0, tiled=True)  7.44 us
    pallas_call x1, Pallas kernels, trail_mine(): pl.pallas_call(trail_mine_kernel, in_specs=[pl.BlockSpec(memory_space=plt...  6.52 us
  transfers between devices with their start and end apart: 12, of which 7 were waited for; matrix products, arithmetic and copies ran while one was open for 1% of the time, Pallas kernels for 17%

profile of v6, /device:TPU:1, one launch (start us, length us, event | category | flops | bytes accessed | tf_op | source)
XLA Modules:
  0.0 103.0 jit_solution(8285517029526786458)
XLA Ops:
  0.7 2.7 %prepare.1 = (bf16[2,2,8,256]{3,2,1,0:T(8,128)(2,1)S(1)}, bf16[4,2,16,2,8,128]{5,4,3,2,1,0:T(8,128)(2,1)}, bf16[2,8,1280]{2,1,0:T(8,128)(2,1)S(1)}, bf16[2,8,1280]{2,1,0:T(8,128)(2,1)S(1)}) custom-call(bf16[2,2,2,8,1024]{4,3,2,1,0:T(8,128)(2,1)} %inverse.1, bf16[2,2,1024,256]{3,2,1,0:T(8,128)(2,1)} %rhs.2, bf16[2,2,8,1024]{3,2,1,0:T(8,128)(2,1)} %below.1, ...), custom_call_target="tpu_custom_call" | custom-call | tf_op jit(solution)/shard_map/prepare/pallas_call | solution.py:83
  3.3 1.4 %collective-permute-start = (bf16[2,8,1280]{2,1,0:T(8,128)(2,1)S(1)}, bf16[2,8,1280]{2,1,0:T(8,128)(2,1)S(1)}, u32[]{:S(2)}, u32[]{:S(2)}) collective-permute-start(bf16[2,8,1280]{2,1,0:T(8,128)(2,1)S(1)} %get-tuple-element.23), channel_id=1, source_target_pairs={{0,16},{16,0},{1,17},{17,1},{2,18},{18,2},{3,19},{19,3},{4,20},{20... | collective-permute-start | bytes 122888 | tf_op jit(solution)/shard_map/ppermute | solution.py:449
  4.7 10.2 %all-to-all-start = ((bf16[128,2,8,128]{3,2,1,0:T(8,128)(2,1)}), bf16[128,2,8,128]{3,2,1,0:T(8,128)(2,1)S(1)}, u32[]{:S(2)}, u32[]{:S(2)}) async-start(bf16[128,2,8,128]{3,2,1,0:T(8,128)(2,1)} %bitcast.4), calls=%async_computation | async-start | bytes 1048576 | tf_op jit(solution)/shard_map/all_to_all | solution.py:483
  15.0 0.1 copy.22
  15.1 0.1 reshape.28
  15.2 0.7 gather_fusion
  15.9 0.1 reshape.27
  16.1 1.4 %collective-permute-start.1 = (bf16[2,2,8,1280]{3,2,1,0:T(8,128)(2,1)S(1)}, bf16[2,2,8,1280]{3,2,1,0:T(8,128)(2,1)S(1)}, u32[]{:S(2)}, u32[]{:S(2)}) collective-permute-start(bf16[2,2,8,1280]{3,2,1,0:T(8,128)(2,1)S(1)} %maximum_select_fusion.rows0), channel_id=1, source_target_pairs={{0,32},{32,64},{64,96},{96,0},{1,33},{33,65},{65,97},{97,1},{2,34}... | collective-permute-start | bytes 245768 | tf_op jit(solution)/shard_map/ppermute | solution.py:444
  17.6 2.4 %collective-permute-start.2 = (bf16[2,2,8,1280]{3,2,1,0:T(8,128)(2,1)S(1)}, bf16[2,2,8,1280]{3,2,1,0:T(8,128)(2,1)S(1)}, u32[]{:S(2)}, u32[]{:S(2)}) collective-permute-start(bf16[2,2,8,1280]{3,2,1,0:T(8,128)(2,1)S(1)} %maximum_select_fusion.rows0), channel_id=1, source_target_pairs={{0,64},{32,96},{64,0},{96,32},{1,65},{33,97},{65,1},{97,33},{2,66}... | collective-permute-start | bytes 245768 | tf_op jit(solution)/shard_map/ppermute | solution.py:444
  19.9 1.2 %collective-permute-start.3 = (bf16[2,2,8,1280]{3,2,1,0:T(8,128)(2,1)S(1)}, bf16[2,2,8,1280]{3,2,1,0:T(8,128)(2,1)S(1)}, u32[]{:S(2)}, u32[]{:S(2)}) collective-permute-start(bf16[2,2,8,1280]{3,2,1,0:T(8,128)(2,1)S(1)} %maximum_select_fusion.rows0), channel_id=1, source_target_pairs={{0,96},{32,0},{64,32},{96,64},{1,97},{33,1},{65,33},{97,65},{2,98}... | collective-permute-start | bytes 245768 | tf_op jit(solution)/shard_map/ppermute | solution.py:444
  21.2 3.8 %collective-permute-done.1.rows1 = bf16[2,2,8,1280]{3,2,1,0:T(8,128)(2,1)S(1)} collective-permute-done((bf16[2,2,8,1280]{3,2,1,0:T(8,128)(2,1)S(1)}, bf16[2,2,8,1280]{3,2,1,0:T(8,128)(2,1)S(1)}, u32[]{:S(2)}, u32[]{:S(2)}) %collective-permute-start.1) | collective-permute-done | bytes 81952 | tf_op jit(solution)/shard_map/ppermute | solution.py:444
  25.0 1.9 %collective-permute-done.2.rows2 = bf16[2,2,8,1280]{3,2,1,0:T(8,128)(2,1)S(1)} collective-permute-done((bf16[2,2,8,1280]{3,2,1,0:T(8,128)(2,1)S(1)}, bf16[2,2,8,1280]{3,2,1,0:T(8,128)(2,1)S(1)}, u32[]{:S(2)}, u32[]{:S(2)}) %collective-permute-start.2) | collective-permute-done | bytes 81952 | tf_op jit(solution)/shard_map/ppermute | solution.py:444
  26.9 2.3 %all-to-all-done.received = bf16[128,2,8,128]{3,2,1,0:T(8,128)(2,1)S(1)} async-done(((bf16[128,2,8,128]{3,2,1,0:T(8,128)(2,1)}), bf16[128,2,8,128]{3,2,1,0:T(8,128)(2,1)S(1)}, u32[]{:S(2)}, u32[]{:S(2)}) %all-to-all-start) | async-done | bytes 524320 | tf_op jit(solution)/shard_map/all_to_all | solution.py:483
  29.2 1.6 %right_side.1 = (bf16[1024,128]{1,0:T(8,128)(2,1)S(1)}, bf16[16,64,128]{2,1,0:T(8,128)(2,1)}) custom-call(s32[4]{0:T(128)S(1)} %pad_add_fusion.place, bf16[128,2,8,128]{3,2,1,0:T(8,128)(2,1)S(1)} %all-to-all-done.received, bf16[2,2,8,1280]{3,2,1,0:T(8,128)(2,1)S(1)} %maximum_select_fusion.rows0, bf16[2,2,8,1280]{3,2,1,0:T(8,128)(2,1)S(1)} %collective-permute-done.1.rows1, ...), custom_call_target="tpu_custom_call" | custom-call | tf_op jit(solution)/shard_map/right_side/pallas_call | solution.py:132
  30.8 4.8 %all-to-all-start.1 = ((bf16[16,64,128]{2,1,0:T(8,128)(2,1)}), bf16[16,64,128]{2,1,0:T(8,128)(2,1)S(1)}, u32[]{:S(2)}, u32[]{:S(2)}) async-start(bf16[16,64,128]{2,1,0:T(8,128)(2,1)} %get-tuple-element.24), calls=%async_computation.1 | async-start | bytes 524288 | tf_op jit(solution)/shard_map/all_to_all | solution.py:491
  35.6 0.1 reshape.22
  35.7 0.1 concatenate.4.tile
  35.8 7.4 %all-to-all-done.1.received = bf16[16,64,128]{2,1,0:T(8,128)(2,1)S(1)} async-done(((bf16[16,64,128]{2,1,0:T(8,128)(2,1)}), bf16[16,64,128]{2,1,0:T(8,128)(2,1)S(1)}, u32[]{:S(2)}, u32[]{:S(2)}) %all-to-all-start.1) | async-done | bytes 262176 | tf_op jit(solution)/shard_map/all_to_all | solution.py:491
  43.3 2.0 %second_rows.1 = bf16[64,72,128]{2,1,0:T(8,128)(2,1)} custom-call(s32[4]{0:T(128)S(1)} %pad_add_fusion.place, bf16[16,64,128]{2,1,0:T(8,128)(2,1)S(1)} %all-to-all-done.1.received, bf16[2,2,8,1280]{3,2,1,0:T(8,128)(2,1)S(1)} %maximum_select_fusion.rows0, bf16[2,2,8,1280]{3,2,1,0:T(8,128)(2,1)S(1)} %collective-permute-done.1.rows1, ...), custom_call_target="tpu_custom_call" | custom-call | tf_op jit(solution)/shard_map/second_rows/pallas_call | solution.py:167
  45.3 4.7 %all-to-all-start.2 = ((bf16[64,72,128]{2,1,0:T(8,128)(2,1)}), bf16[64,72,128]{2,1,0:T(8,128)(2,1)S(1)}, u32[]{:S(2)}, u32[]{:S(2)}) async-start(bf16[64,72,128]{2,1,0:T(8,128)(2,1)} %second_rows.1), calls=%async_computation.2 | async-start | bytes 2359296 | tf_op jit(solution)/shard_map/all_to_all | solution.py:497
  50.0 1.1 %collective-permute-start.5 = (bf16[1024,128]{1,0:T(8,128)(2,1)S(1)}, bf16[1024,128]{1,0:T(8,128)(2,1)S(1)}, u32[]{:S(2)}, u32[]{:S(2)}) collective-permute-start(bf16[1024,128]{1,0:T(8,128)(2,1)S(1)} %get-tuple-element.25), channel_id=1, source_target_pairs={{0,32},{32,64},{64,96},{96,0},{1,33},{33,65},{65,97},{97,1},{2,34}... | collective-permute-start | bytes 786440 | tf_op jit(solution)/shard_map/ppermute | solution.py:444
  51.1 2.6 %collective-permute-start.6 = (bf16[1024,128]{1,0:T(8,128)(2,1)S(1)}, bf16[1024,128]{1,0:T(8,128)(2,1)S(1)}, u32[]{:S(2)}, u32[]{:S(2)}) collective-permute-start(bf16[1024,128]{1,0:T(8,128)(2,1)S(1)} %get-tuple-element.25), channel_id=1, source_target_pairs={{0,64},{32,96},{64,0},{96,32},{1,65},{33,97},{65,1},{97,33},{2,66}... | collective-permute-start | bytes 786440 | tf_op jit(solution)/shard_map/ppermute | solution.py:444
  53.7 1.1 %collective-permute-start.7 = (bf16[1024,128]{1,0:T(8,128)(2,1)S(1)}, bf16[1024,128]{1,0:T(8,128)(2,1)S(1)}, u32[]{:S(2)}, u32[]{:S(2)}) collective-permute-start(bf16[1024,128]{1,0:T(8,128)(2,1)S(1)} %get-tuple-element.25), channel_id=1, source_target_pairs={{0,96},{32,0},{64,32},{96,64},{1,97},{33,1},{65,33},{97,65},{2,98}... | collective-permute-start | bytes 786440 | tf_op jit(solution)/shard_map/ppermute | solution.py:444
  54.8 12.9 %all-to-all-done.2 = bf16[64,72,128]{2,1,0:T(8,128)(2,1)S(1)} async-done(((bf16[64,72,128]{2,1,0:T(8,128)(2,1)}), bf16[64,72,128]{2,1,0:T(8,128)(2,1)S(1)}, u32[]{:S(2)}, u32[]{:S(2)}) %all-to-all-start.2) | async-done | bytes 1179680 | tf_op jit(solution)/shard_map/all_to_all | solution.py:497
  67.7 4.8 %collective-permute-start.4 = (bf16[64,72,128]{2,1,0:T(8,128)(2,1)S(1)}, bf16[64,72,128]{2,1,0:T(8,128)(2,1)S(1)}, u32[]{:S(2)}, u32[]{:S(2)}) collective-permute-start(bf16[64,72,128]{2,1,0:T(8,128)(2,1)S(1)} %all-to-all-done.2), channel_id=1, source_target_pairs={{0,16},{16,0},{1,17},{17,1},{2,18},{18,2},{3,19},{19,3},{4,20},{20... | collective-permute-start | bytes 3538952 | tf_op jit(solution)/shard_map/ppermute | solution.py:449
  72.4 2.5 %collective-permute-done.6 = bf16[1024,128]{1,0:T(8,128)(2,1)S(1)} collective-permute-done((bf16[1024,128]{1,0:T(8,128)(2,1)S(1)}, bf16[1024,128]{1,0:T(8,128)(2,1)S(1)}, u32[]{:S(2)}, u32[]{:S(2)}) %collective-permute-start.6) | collective-permute-done | bytes 262176 | tf_op jit(solution)/shard_map/ppermute | solution.py:444
  74.9 0.1 pad_maximum_fusion.mine
  75.0 3.3 %collective-permute-start.8 = (bf16[4,1024,128]{2,1,0:T(8,128)(2,1)S(1)}, bf16[4,1024,128]{2,1,0:T(8,128)(2,1)S(1)}, u32[]{:S(2)}, u32[]{:S(2)}) collective-permute-start(bf16[4,1024,128]{2,1,0:T(8,128)(2,1)S(1)} %pad_maximum_fusion.mine), channel_id=1, source_target_pairs={{0,16},{16,0},{1,17},{17,1},{2,18},{18,2},{3,19},{19,3},{4,20},{20... | collective-permute-start | bytes 3145736 | tf_op jit(solution)/shard_map/ppermute | solution.py:449
  78.4 2.3 %collective-permute-done.8.theirs = bf16[4,1024,128]{2,1,0:T(8,128)(2,1)S(1)} collective-permute-done((bf16[4,1024,128]{2,1,0:T(8,128)(2,1)S(1)}, bf16[4,1024,128]{2,1,0:T(8,128)(2,1)S(1)}, u32[]{:S(2)}, u32[]{:S(2)}) %collective-permute-start.8) | collective-permute-done | bytes 1048608 | tf_op jit(solution)/shard_map/ppermute | solution.py:449
  80.7 10.6 %trail_first.1 = (f32[2,2,1024,256]{3,2,1,0:T(8,128)}, f32[1024,128]{1,0:T(8,128)}, bf16[2,2,256,1024]{3,2,1,0:T(8,128)(2,1)S(1)}) custom-call(s32[4]{0:T(128)S(1)} %pad_add_fusion.place, bf16[4,1024,128]{2,1,0:T(8,128)(2,1)S(1)} %pad_maximum_fusion.mine, bf16[4,1024,128]{2,1,0:T(8,128)(2,1)S(1)} %collective-permute-done.8.theirs, ...), custom_call_target="tpu_custom_call" | custom-call | tf_op jit(solution)/shard_map/trail_first/pallas_call | solution.py:236
  91.3 6.5 %trail_mine.1 = (bf16[2,2,1024,256]{3,2,1,0:T(8,128)(2,1)}, bf16[2,8,256]{2,1,0:T(8,128)(2,1)S(1)}, bf16[1024,512]{1,0:T(8,128)(2,1)S(1)}, bf16[4,128,128]{2,1,0...) custom-call(s32[4]{0:T(128)S(1)} %pad_add_fusion.place, ...), custom_call_target="tpu_custom_call" | custom-call | tf_op jit(solution)/shard_map/trail_mine/pallas_call | solution.py:318
  97.9 5.0 %trail_theirs.1 = (bf16[2,2,1024,256]{3,2,1,0:T(8,128)(2,1)}, bf16[2,2,2,8,256]{4,3,2,1,0:T(8,128)(2,1)}, f32[3,8]{1,0:T(4,128)}) custom-call(s32[4]{0:T(128)S(1)} %pad_add_fusion.place, bf16[4,16,72,128]{3,2,1,0:T(8,128)(2,1)S(1)} %bitcast.16, bf16[4,2,256,1024]{3,2,1,0:T(8,128)(2,1)S(1)} %get-tuple-element.28.rows, ...), custom_call_target="tpu_custom_call", output_to_operand_aliasing={{0}: (10, {})} | custom-call | tf_op jit(solution)/shard_map/trail_theirs/pallas_call | solution.py:371
  (25 shorter events, 0.3 us)
Async XLA Ops:
  0.6 14.5 %copy-start = (s32[1024]{0:T(1024)S(1)}, s32[1024]{0:T(1024)}, u32[]{:S(2)}) copy-start(s32[1024]{0:T(1024)} %param.18) | copy-start | bytes 12292
  0.6 14.3 %copy-start.4 = (s32[2,8,3]{1,0,2:T(2,128)S(1)}, s32[2,8,3]{1,0,2:T(2,128)}, u32[]{:S(2)}) copy-start(s32[2,8,3]{1,0,2:T(2,128)} %param.17) | copy-start | bytes 580
  3.3 12.8 %collective-permute-start = (bf16[2,8,1280]{2,1,0:T(8,128)(2,1)S(1)}, bf16[2,8,1280]{2,1,0:T(8,128)(2,1)S(1)}, u32[]{:S(2)}, u32[]{:S(2)}) collective-permute-start(bf16[2,8,1280]{2,1,0:T(8,128)(2,1)S(1)} %get-tuple-element.23), channel_id=1, source_target_pairs={{0,16},{16,0},{1,17},{17,1},{2,18},{18,2},{3,19},{19,3},{4,20},{20... | collective-permute-start | bytes 122888 | tf_op jit(solution)/shard_map/ppermute | solution.py:449
  4.7 24.5 %all-to-all-start = ((bf16[128,2,8,128]{3,2,1,0:T(8,128)(2,1)}), bf16[128,2,8,128]{3,2,1,0:T(8,128)(2,1)S(1)}, u32[]{:S(2)}, u32[]{:S(2)}) async-start(bf16[128,2,8,128]{3,2,1,0:T(8,128)(2,1)} %bitcast.4), calls=%async_computation | async-start | bytes 1048576 | tf_op jit(solution)/shard_map/all_to_all | solution.py:483
  15.2 20.4 %copy-start.3 = (f32[2,9,2,8]{1,3,2,0:T(8,128)S(1)}, f32[2,9,2,8]{1,3,2,0:T(8,128)}, u32[]{:S(2)}) copy-start(f32[2,9,2,8]{1,3,2,0:T(8,128)} %param.16) | copy-start | bytes 3460
  16.1 8.9 %collective-permute-start.1 = (bf16[2,2,8,1280]{3,2,1,0:T(8,128)(2,1)S(1)}, bf16[2,2,8,1280]{3,2,1,0:T(8,128)(2,1)S(1)}, u32[]{:S(2)}, u32[]{:S(2)}) collective-permute-start(bf16[2,2,8,1280]{3,2,1,0:T(8,128)(2,1)S(1)} %maximum_select_fusion.rows0), channel_id=1, source_target_pairs={{0,32},{32,64},{64,96},{96,0},{1,33},{33,65},{65,97},{97,1},{2,34}... | collective-permute-start | bytes 245768 | tf_op jit(solution)/shard_map/ppermute | solution.py:444
  17.6 9.4 %collective-permute-start.2 = (bf16[2,2,8,1280]{3,2,1,0:T(8,128)(2,1)S(1)}, bf16[2,2,8,1280]{3,2,1,0:T(8,128)(2,1)S(1)}, u32[]{:S(2)}, u32[]{:S(2)}) collective-permute-start(bf16[2,2,8,1280]{3,2,1,0:T(8,128)(2,1)S(1)} %maximum_select_fusion.rows0), channel_id=1, source_target_pairs={{0,64},{32,96},{64,0},{96,32},{1,65},{33,97},{65,1},{97,33},{2,66}... | collective-permute-start | bytes 245768 | tf_op jit(solution)/shard_map/ppermute | solution.py:444
  19.9 7.0 %collective-permute-start.3 = (bf16[2,2,8,1280]{3,2,1,0:T(8,128)(2,1)S(1)}, bf16[2,2,8,1280]{3,2,1,0:T(8,128)(2,1)S(1)}, u32[]{:S(2)}, u32[]{:S(2)}) collective-permute-start(bf16[2,2,8,1280]{3,2,1,0:T(8,128)(2,1)S(1)} %maximum_select_fusion.rows0), channel_id=1, source_target_pairs={{0,96},{32,0},{64,32},{96,64},{1,97},{33,1},{65,33},{97,65},{2,98}... | collective-permute-start | bytes 245768 | tf_op jit(solution)/shard_map/ppermute | solution.py:444
  30.8 12.5 %all-to-all-start.1 = ((bf16[16,64,128]{2,1,0:T(8,128)(2,1)}), bf16[16,64,128]{2,1,0:T(8,128)(2,1)S(1)}, u32[]{:S(2)}, u32[]{:S(2)}) async-start(bf16[16,64,128]{2,1,0:T(8,128)(2,1)} %get-tuple-element.24), calls=%async_computation.1 | async-start | bytes 524288 | tf_op jit(solution)/shard_map/all_to_all | solution.py:491
  45.3 22.4 %all-to-all-start.2 = ((bf16[64,72,128]{2,1,0:T(8,128)(2,1)}), bf16[64,72,128]{2,1,0:T(8,128)(2,1)S(1)}, u32[]{:S(2)}, u32[]{:S(2)}) async-start(bf16[64,72,128]{2,1,0:T(8,128)(2,1)} %second_rows.1), calls=%async_computation.2 | async-start | bytes 2359296 | tf_op jit(solution)/shard_map/all_to_all | solution.py:497
  50.0 22.4 %collective-permute-start.5 = (bf16[1024,128]{1,0:T(8,128)(2,1)S(1)}, bf16[1024,128]{1,0:T(8,128)(2,1)S(1)}, u32[]{:S(2)}, u32[]{:S(2)}) collective-permute-start(bf16[1024,128]{1,0:T(8,128)(2,1)S(1)} %get-tuple-element.25), channel_id=1, source_target_pairs={{0,32},{32,64},{64,96},{96,0},{1,33},{33,65},{65,97},{97,1},{2,34}... | collective-permute-start | bytes 786440 | tf_op jit(solution)/shard_map/ppermute | solution.py:444
  51.1 23.8 %collective-permute-start.6 = (bf16[1024,128]{1,0:T(8,128)(2,1)S(1)}, bf16[1024,128]{1,0:T(8,128)(2,1)S(1)}, u32[]{:S(2)}, u32[]{:S(2)}) collective-permute-start(bf16[1024,128]{1,0:T(8,128)(2,1)S(1)} %get-tuple-element.25), channel_id=1, source_target_pairs={{0,64},{32,96},{64,0},{96,32},{1,65},{33,97},{65,1},{97,33},{2,66}... | collective-permute-start | bytes 786440 | tf_op jit(solution)/shard_map/ppermute | solution.py:444
  53.7 21.2 %collective-permute-start.7 = (bf16[1024,128]{1,0:T(8,128)(2,1)S(1)}, bf16[1024,128]{1,0:T(8,128)(2,1)S(1)}, u32[]{:S(2)}, u32[]{:S(2)}) collective-permute-start(bf16[1024,128]{1,0:T(8,128)(2,1)S(1)} %get-tuple-element.25), channel_id=1, source_target_pairs={{0,96},{32,0},{64,32},{96,64},{1,97},{33,1},{65,33},{97,65},{2,98}... | collective-permute-start | bytes 786440 | tf_op jit(solution)/shard_map/ppermute | solution.py:444
  67.7 30.2 %collective-permute-start.4 = (bf16[64,72,128]{2,1,0:T(8,128)(2,1)S(1)}, bf16[64,72,128]{2,1,0:T(8,128)(2,1)S(1)}, u32[]{:S(2)}, u32[]{:S(2)}) collective-permute-start(bf16[64,72,128]{2,1,0:T(8,128)(2,1)S(1)} %all-to-all-done.2), channel_id=1, source_target_pairs={{0,16},{16,0},{1,17},{17,1},{2,18},{18,2},{3,19},{19,3},{4,20},{20... | collective-permute-start | bytes 3538952 | tf_op jit(solution)/shard_map/ppermute | solution.py:449
  75.0 5.6 %collective-permute-start.8 = (bf16[4,1024,128]{2,1,0:T(8,128)(2,1)S(1)}, bf16[4,1024,128]{2,1,0:T(8,128)(2,1)S(1)}, u32[]{:S(2)}, u32[]{:S(2)}) collective-permute-start(bf16[4,1024,128]{2,1,0:T(8,128)(2,1)S(1)} %pad_maximum_fusion.mine), channel_id=1, source_target_pairs={{0,16},{16,0},{1,17},{17,1},{2,18},{18,2},{3,19},{19,3},{4,20},{20... | collective-permute-start | bytes 3145736 | tf_op jit(solution)/shard_map/ppermute | solution.py:449
  91.3 6.6 %copy-start.1 = (f32[1024,128]{1,0:T(8,128)S(1)}, f32[1024,128]{1,0:T(8,128)}, u32[]{:S(2)}) copy-start(f32[1024,128]{1,0:T(8,128)} %get-tuple-element.34.before) | copy-start | bytes 1572868
  91.3 6.6 %copy-start.2 = (bf16[128,768]{1,0:T(8,128)(2,1)S(1)}, bf16[128,768]{1,0:T(8,128)(2,1)}, u32[]{:S(2)}) copy-start(bf16[128,768]{1,0:T(8,128)(2,1)} %constant.54.clone.spread) | copy-start | bytes 589828

commit v7 on v6

--- a/solution.py
+++ b/solution.py
@@ -286,26 +286,33 @@
     cuts = [pl.ds(i * height, height) for i in range(4)]
     take = copy(received, arrived, sems.at[0])
     take_row = copy(factor.at[core, 1, :, pl.ds(2 * height, 2 * height)], rows, sems.at[1])
-    take_before = copy(total.at[core], before, sems.at[2])
+    halves = [pl.ds(0, 2 * height), pl.ds(2 * height, 2 * height)]
+    take_before = [
+        copy(total.at[core, :, halves[i]], before.at[:, halves[i]], sems.at[(2, 12)[i]]) for i in range(2)
+    ]
     take_rest = copy(total.at[1 - core], rest, sems.at[3])
     give = [copy(done.at[i], out.at[core, :, cuts[i]], sems.at[4 + i]) for i in range(4)]
     take_later = [
         copy(factor.at[1 - core, 1, :, cuts[i]], later.at[i], sems.at[8 + i]) for i in range(4)
     ]
     take.start()
+    take_before[0].start()
     take.wait()
-    for one in (take_row, take_before, *take_later, take_rest):
+    for one in (take_row, take_before[1], *take_later, take_rest):
         one.start()
     own[0], own[1] = take_blocks(place, arrived, blocks, tiles)
-    products = [trail_product(early[i].reshape(2 * height, 1024), blocks) for i in range(2)]
+    take_before[0].wait()
+    for i in range(2):
+        product = trail_product(early[i].reshape(2 * height, 1024), blocks)
+        finish_rows(i, product, before, done)
+        give[i].start()
     take_row.wait()
-    take_before.wait()
+    take_before[1].wait()
     for i in range(2):
         cut = slice(i * height, i * height + height)
-        products.append(trail_product(rows[:, cut, :].reshape(2 * height, 1024), blocks))
-    for i in range(4):
-        finish_rows(i, products[i], before, done)
-        give[i].start()
+        product = trail_product(rows[:, cut, :].reshape(2 * height, 1024), blocks)
+        finish_rows(2 + i, product, before, done)
+        give[2 + i].start()
     for one in (*take_later, take_rest, *give):
         one.wait()
 
@@ -332,7 +339,7 @@
             pltpu.VMEM((2, 2 * height, 1024), BF16),
             pltpu.VMEM((2, rows, 256), F32),
             pltpu.VMEM((4, 2, height, 256), BF16),
-            pltpu.SemaphoreType.DMA((12,)),
+            pltpu.SemaphoreType.DMA((13,)),
         ],
         compiler_params=pltpu.CompilerParams(vmem_limit_bytes=14 * 1024 * 1024),
         name="trail_mine",

time: 103 us -> 102 us (level)
  Pallas kernels: 28.4 us -> 27.3 us
    pallas_call x1, Pallas kernels: 6.52 us -> 5.44 us  [trail_mine(): pl.pallas_call(trail_mine_kernel, in_specs=[pl.BlockSpec(memory_space=plt...]
  transfers between devices with their start and end apart: 12 -> 12, of which waited for: 7 -> 7; matrix products, arithmetic and copies ran while one was open for 1% -> 1% of each run, Pallas kernels for 17% -> 16%
where the time goes in v7:
time: 102 us
  starting transfers between devices  38.9 us (38%)
  waiting for transfers between devices  33.1 us (32%)
  Pallas kernels  27.3 us (27%)
  local copies, waits for them, and re-layouts  1.3 us (1%)
    all_to_all x1, waiting for transfers between devices, steps(): second_mine = lax.all_to_all(send, ('x', 'col'), 0, 0, tiled=True)  12.9 us
    pallas_call x1, Pallas kernels, trail_first(): pl.pallas_call(trail_first_kernel, in_specs=[pl.BlockSpec(memory_space=pl...  10.6 us
    all_to_all x1, starting transfers between devices, steps(): lax.all_to_all(send.reshape(128, 2, 8, 128), ALL, 0, 0, tiled=True)  10.2 us
    ppermute x6, starting transfers between devices, rounds_x(): lax.ppermute(value, 'x', [(i, (i + step) % 4) for i in range(4)])  9.75 us
    ppermute x3, starting transfers between devices, swap_core(): return lax.ppermute(value, 'core', [(0, 1), (1, 0)])  9.47 us
    ppermute x6, waiting for transfers between devices, rounds_x(): lax.ppermute(value, 'x', [(i, (i + step) % 4) for i in range(4)])  8.21 us
    all_to_all x1, waiting for transfers between devices, steps(): received = lax.all_to_all(send, 'col', 0, 0, tiled=True)  7.44 us
    pallas_call x1, Pallas kernels, trail_mine(): pl.pallas_call(trail_mine_kernel, in_specs=[pl.BlockSpec(memory_space=plt...  5.44 us
  transfers between devices with their start and end apart: 12, of which 7 were waited for; matrix products, arithmetic and copies ran while one was open for 1% of the time, Pallas kernels for 16%

profile of v7, /device:TPU:1, one launch (start us, length us, event | category | flops | bytes accessed | tf_op | source)
XLA Modules:
  0.0 101.9 jit_solution(12337883823992867490)
XLA Ops:
  0.7 2.7 %prepare.1 = (bf16[2,2,8,256]{3,2,1,0:T(8,128)(2,1)S(1)}, bf16[4,2,16,2,8,128]{5,4,3,2,1,0:T(8,128)(2,1)}, bf16[2,8,1280]{2,1,0:T(8,128)(2,1)S(1)}, bf16[2,8,1280]{2,1,0:T(8,128)(2,1)S(1)}) custom-call(bf16[2,2,2,8,1024]{4,3,2,1,0:T(8,128)(2,1)} %inverse.1, bf16[2,2,1024,256]{3,2,1,0:T(8,128)(2,1)} %rhs.2, bf16[2,2,8,1024]{3,2,1,0:T(8,128)(2,1)} %below.1, ...), custom_call_target="tpu_custom_call" | custom-call | tf_op jit(solution)/shard_map/prepare/pallas_call | solution.py:83
  3.3 1.4 %collective-permute-start = (bf16[2,8,1280]{2,1,0:T(8,128)(2,1)S(1)}, bf16[2,8,1280]{2,1,0:T(8,128)(2,1)S(1)}, u32[]{:S(2)}, u32[]{:S(2)}) collective-permute-start(bf16[2,8,1280]{2,1,0:T(8,128)(2,1)S(1)} %get-tuple-element.23), channel_id=1, source_target_pairs={{0,16},{16,0},{1,17},{17,1},{2,18},{18,2},{3,19},{19,3},{4,20},{20... | collective-permute-start | bytes 122888 | tf_op jit(solution)/shard_map/ppermute | solution.py:456
  4.7 10.2 %all-to-all-start = ((bf16[128,2,8,128]{3,2,1,0:T(8,128)(2,1)}), bf16[128,2,8,128]{3,2,1,0:T(8,128)(2,1)S(1)}, u32[]{:S(2)}, u32[]{:S(2)}) async-start(bf16[128,2,8,128]{3,2,1,0:T(8,128)(2,1)} %bitcast.4), calls=%async_computation | async-start | bytes 1048576 | tf_op jit(solution)/shard_map/all_to_all | solution.py:490
  15.0 0.1 copy.22
  15.1 0.1 reshape.28
  15.2 0.7 gather_fusion
  15.9 0.1 reshape.27
  16.1 1.4 %collective-permute-start.1 = (bf16[2,2,8,1280]{3,2,1,0:T(8,128)(2,1)S(1)}, bf16[2,2,8,1280]{3,2,1,0:T(8,128)(2,1)S(1)}, u32[]{:S(2)}, u32[]{:S(2)}) collective-permute-start(bf16[2,2,8,1280]{3,2,1,0:T(8,128)(2,1)S(1)} %maximum_select_fusion.rows0), channel_id=1, source_target_pairs={{0,32},{32,64},{64,96},{96,0},{1,33},{33,65},{65,97},{97,1},{2,34}... | collective-permute-start | bytes 245768 | tf_op jit(solution)/shard_map/ppermute | solution.py:451
  17.6 2.4 %collective-permute-start.2 = (bf16[2,2,8,1280]{3,2,1,0:T(8,128)(2,1)S(1)}, bf16[2,2,8,1280]{3,2,1,0:T(8,128)(2,1)S(1)}, u32[]{:S(2)}, u32[]{:S(2)}) collective-permute-start(bf16[2,2,8,1280]{3,2,1,0:T(8,128)(2,1)S(1)} %maximum_select_fusion.rows0), channel_id=1, source_target_pairs={{0,64},{32,96},{64,0},{96,32},{1,65},{33,97},{65,1},{97,33},{2,66}... | collective-permute-start | bytes 245768 | tf_op jit(solution)/shard_map/ppermute | solution.py:451
  19.9 1.2 %collective-permute-start.3 = (bf16[2,2,8,1280]{3,2,1,0:T(8,128)(2,1)S(1)}, bf16[2,2,8,1280]{3,2,1,0:T(8,128)(2,1)S(1)}, u32[]{:S(2)}, u32[]{:S(2)}) collective-permute-start(bf16[2,2,8,1280]{3,2,1,0:T(8,128)(2,1)S(1)} %maximum_select_fusion.rows0), channel_id=1, source_target_pairs={{0,96},{32,0},{64,32},{96,64},{1,97},{33,1},{65,33},{97,65},{2,98}... | collective-permute-start | bytes 245768 | tf_op jit(solution)/shard_map/ppermute | solution.py:451
  21.2 3.8 %collective-permute-done.1.rows1 = bf16[2,2,8,1280]{3,2,1,0:T(8,128)(2,1)S(1)} collective-permute-done((bf16[2,2,8,1280]{3,2,1,0:T(8,128)(2,1)S(1)}, bf16[2,2,8,1280]{3,2,1,0:T(8,128)(2,1)S(1)}, u32[]{:S(2)}, u32[]{:S(2)}) %collective-permute-start.1) | collective-permute-done | bytes 81952 | tf_op jit(solution)/shard_map/ppermute | solution.py:451
  25.0 1.9 %collective-permute-done.2.rows2 = bf16[2,2,8,1280]{3,2,1,0:T(8,128)(2,1)S(1)} collective-permute-done((bf16[2,2,8,1280]{3,2,1,0:T(8,128)(2,1)S(1)}, bf16[2,2,8,1280]{3,2,1,0:T(8,128)(2,1)S(1)}, u32[]{:S(2)}, u32[]{:S(2)}) %collective-permute-start.2) | collective-permute-done | bytes 81952 | tf_op jit(solution)/shard_map/ppermute | solution.py:451
  26.9 2.3 %all-to-all-done.received = bf16[128,2,8,128]{3,2,1,0:T(8,128)(2,1)S(1)} async-done(((bf16[128,2,8,128]{3,2,1,0:T(8,128)(2,1)}), bf16[128,2,8,128]{3,2,1,0:T(8,128)(2,1)S(1)}, u32[]{:S(2)}, u32[]{:S(2)}) %all-to-all-start) | async-done | bytes 524320 | tf_op jit(solution)/shard_map/all_to_all | solution.py:490
  29.2 1.6 %right_side.1 = (bf16[1024,128]{1,0:T(8,128)(2,1)S(1)}, bf16[16,64,128]{2,1,0:T(8,128)(2,1)}) custom-call(s32[4]{0:T(128)S(1)} %pad_add_fusion.place, bf16[128,2,8,128]{3,2,1,0:T(8,128)(2,1)S(1)} %all-to-all-done.received, bf16[2,2,8,1280]{3,2,1,0:T(8,128)(2,1)S(1)} %maximum_select_fusion.rows0, bf16[2,2,8,1280]{3,2,1,0:T(8,128)(2,1)S(1)} %collective-permute-done.1.rows1, ...), custom_call_target="tpu_custom_call" | custom-call | tf_op jit(solution)/shard_map/right_side/pallas_call | solution.py:132
  30.8 4.8 %all-to-all-start.1 = ((bf16[16,64,128]{2,1,0:T(8,128)(2,1)}), bf16[16,64,128]{2,1,0:T(8,128)(2,1)S(1)}, u32[]{:S(2)}, u32[]{:S(2)}) async-start(bf16[16,64,128]{2,1,0:T(8,128)(2,1)} %get-tuple-element.24), calls=%async_computation.1 | async-start | bytes 524288 | tf_op jit(solution)/shard_map/all_to_all | solution.py:498
  35.6 0.1 reshape.22
  35.7 0.1 concatenate.4.tile
  35.8 7.4 %all-to-all-done.1.received = bf16[16,64,128]{2,1,0:T(8,128)(2,1)S(1)} async-done(((bf16[16,64,128]{2,1,0:T(8,128)(2,1)}), bf16[16,64,128]{2,1,0:T(8,128)(2,1)S(1)}, u32[]{:S(2)}, u32[]{:S(2)}) %all-to-all-start.1) | async-done | bytes 262176 | tf_op jit(solution)/shard_map/all_to_all | solution.py:498
  43.3 2.0 %second_rows.1 = bf16[64,72,128]{2,1,0:T(8,128)(2,1)} custom-call(s32[4]{0:T(128)S(1)} %pad_add_fusion.place, bf16[16,64,128]{2,1,0:T(8,128)(2,1)S(1)} %all-to-all-done.1.received, bf16[2,2,8,1280]{3,2,1,0:T(8,128)(2,1)S(1)} %maximum_select_fusion.rows0, bf16[2,2,8,1280]{3,2,1,0:T(8,128)(2,1)S(1)} %collective-permute-done.1.rows1, ...), custom_call_target="tpu_custom_call" | custom-call | tf_op jit(solution)/shard_map/second_rows/pallas_call | solution.py:167
  45.3 4.7 %all-to-all-start.2 = ((bf16[64,72,128]{2,1,0:T(8,128)(2,1)}), bf16[64,72,128]{2,1,0:T(8,128)(2,1)S(1)}, u32[]{:S(2)}, u32[]{:S(2)}) async-start(bf16[64,72,128]{2,1,0:T(8,128)(2,1)} %second_rows.1), calls=%async_computation.2 | async-start | bytes 2359296 | tf_op jit(solution)/shard_map/all_to_all | solution.py:504
  50.0 1.1 %collective-permute-start.5 = (bf16[1024,128]{1,0:T(8,128)(2,1)S(1)}, bf16[1024,128]{1,0:T(8,128)(2,1)S(1)}, u32[]{:S(2)}, u32[]{:S(2)}) collective-permute-start(bf16[1024,128]{1,0:T(8,128)(2,1)S(1)} %get-tuple-element.25), channel_id=1, source_target_pairs={{0,32},{32,64},{64,96},{96,0},{1,33},{33,65},{65,97},{97,1},{2,34}... | collective-permute-start | bytes 786440 | tf_op jit(solution)/shard_map/ppermute | solution.py:451
  51.1 2.6 %collective-permute-start.6 = (bf16[1024,128]{1,0:T(8,128)(2,1)S(1)}, bf16[1024,128]{1,0:T(8,128)(2,1)S(1)}, u32[]{:S(2)}, u32[]{:S(2)}) collective-permute-start(bf16[1024,128]{1,0:T(8,128)(2,1)S(1)} %get-tuple-element.25), channel_id=1, source_target_pairs={{0,64},{32,96},{64,0},{96,32},{1,65},{33,97},{65,1},{97,33},{2,66}... | collective-permute-start | bytes 786440 | tf_op jit(solution)/shard_map/ppermute | solution.py:451
  53.7 1.1 %collective-permute-start.7 = (bf16[1024,128]{1,0:T(8,128)(2,1)S(1)}, bf16[1024,128]{1,0:T(8,128)(2,1)S(1)}, u32[]{:S(2)}, u32[]{:S(2)}) collective-permute-start(bf16[1024,128]{1,0:T(8,128)(2,1)S(1)} %get-tuple-element.25), channel_id=1, source_target_pairs={{0,96},{32,0},{64,32},{96,64},{1,97},{33,1},{65,33},{97,65},{2,98}... | collective-permute-start | bytes 786440 | tf_op jit(solution)/shard_map/ppermute | solution.py:451
  54.8 12.9 %all-to-all-done.2 = bf16[64,72,128]{2,1,0:T(8,128)(2,1)S(1)} async-done(((bf16[64,72,128]{2,1,0:T(8,128)(2,1)}), bf16[64,72,128]{2,1,0:T(8,128)(2,1)S(1)}, u32[]{:S(2)}, u32[]{:S(2)}) %all-to-all-start.2) | async-done | bytes 1179680 | tf_op jit(solution)/shard_map/all_to_all | solution.py:504
  67.7 4.8 %collective-permute-start.4 = (bf16[64,72,128]{2,1,0:T(8,128)(2,1)S(1)}, bf16[64,72,128]{2,1,0:T(8,128)(2,1)S(1)}, u32[]{:S(2)}, u32[]{:S(2)}) collective-permute-start(bf16[64,72,128]{2,1,0:T(8,128)(2,1)S(1)} %all-to-all-done.2), channel_id=1, source_target_pairs={{0,16},{16,0},{1,17},{17,1},{2,18},{18,2},{3,19},{19,3},{4,20},{20... | collective-permute-start | bytes 3538952 | tf_op jit(solution)/shard_map/ppermute | solution.py:456
  72.4 2.5 %collective-permute-done.6 = bf16[1024,128]{1,0:T(8,128)(2,1)S(1)} collective-permute-done((bf16[1024,128]{1,0:T(8,128)(2,1)S(1)}, bf16[1024,128]{1,0:T(8,128)(2,1)S(1)}, u32[]{:S(2)}, u32[]{:S(2)}) %collective-permute-start.6) | collective-permute-done | bytes 262176 | tf_op jit(solution)/shard_map/ppermute | solution.py:451
  74.9 0.1 pad_maximum_fusion.mine
  75.0 3.3 %collective-permute-start.8 = (bf16[4,1024,128]{2,1,0:T(8,128)(2,1)S(1)}, bf16[4,1024,128]{2,1,0:T(8,128)(2,1)S(1)}, u32[]{:S(2)}, u32[]{:S(2)}) collective-permute-start(bf16[4,1024,128]{2,1,0:T(8,128)(2,1)S(1)} %pad_maximum_fusion.mine), channel_id=1, source_target_pairs={{0,16},{16,0},{1,17},{17,1},{2,18},{18,2},{3,19},{19,3},{4,20},{20... | collective-permute-start | bytes 3145736 | tf_op jit(solution)/shard_map/ppermute | solution.py:456
  78.4 2.3 %collective-permute-done.8.theirs = bf16[4,1024,128]{2,1,0:T(8,128)(2,1)S(1)} collective-permute-done((bf16[4,1024,128]{2,1,0:T(8,128)(2,1)S(1)}, bf16[4,1024,128]{2,1,0:T(8,128)(2,1)S(1)}, u32[]{:S(2)}, u32[]{:S(2)}) %collective-permute-start.8) | collective-permute-done | bytes 1048608 | tf_op jit(solution)/shard_map/ppermute | solution.py:456
  80.7 10.6 %trail_first.1 = (f32[2,2,1024,256]{3,2,1,0:T(8,128)}, f32[1024,128]{1,0:T(8,128)}, bf16[2,2,256,1024]{3,2,1,0:T(8,128)(2,1)S(1)}) custom-call(s32[4]{0:T(128)S(1)} %pad_add_fusion.place, bf16[4,1024,128]{2,1,0:T(8,128)(2,1)S(1)} %pad_maximum_fusion.mine, bf16[4,1024,128]{2,1,0:T(8,128)(2,1)S(1)} %collective-permute-done.8.theirs, ...), custom_call_target="tpu_custom_call" | custom-call | tf_op jit(solution)/shard_map/trail_first/pallas_call | solution.py:236
  91.3 5.4 %trail_mine.1 = (bf16[2,2,1024,256]{3,2,1,0:T(8,128)(2,1)}, bf16[2,8,256]{2,1,0:T(8,128)(2,1)S(1)}, bf16[1024,512]{1,0:T(8,128)(2,1)S(1)}, bf16[4,128,128]{2,1,0...) custom-call(s32[4]{0:T(128)S(1)} %pad_add_fusion.place, ...), custom_call_target="tpu_custom_call" | custom-call | tf_op jit(solution)/shard_map/trail_mine/pallas_call | solution.py:325
  96.8 5.0 %trail_theirs.1 = (bf16[2,2,1024,256]{3,2,1,0:T(8,128)(2,1)}, bf16[2,2,2,8,256]{4,3,2,1,0:T(8,128)(2,1)}, f32[3,8]{1,0:T(4,128)}) custom-call(s32[4]{0:T(128)S(1)} %pad_add_fusion.place, bf16[4,16,72,128]{3,2,1,0:T(8,128)(2,1)S(1)} %bitcast.16, bf16[4,2,256,1024]{3,2,1,0:T(8,128)(2,1)S(1)} %get-tuple-element.28.rows, ...), custom_call_target="tpu_custom_call", output_to_operand_aliasing={{0}: (10, {})} | custom-call | tf_op jit(solution)/shard_map/trail_theirs/pallas_call | solution.py:378
  (25 shorter events, 0.3 us)
Async XLA Ops:
  0.6 14.5 %copy-start = (s32[1024]{0:T(1024)S(1)}, s32[1024]{0:T(1024)}, u32[]{:S(2)}) copy-start(s32[1024]{0:T(1024)} %param.18) | copy-start | bytes 12292
  0.6 14.3 %copy-start.4 = (s32[2,8,3]{1,0,2:T(2,128)S(1)}, s32[2,8,3]{1,0,2:T(2,128)}, u32[]{:S(2)}) copy-start(s32[2,8,3]{1,0,2:T(2,128)} %param.17) | copy-start | bytes 580
  3.3 12.8 %collective-permute-start = (bf16[2,8,1280]{2,1,0:T(8,128)(2,1)S(1)}, bf16[2,8,1280]{2,1,0:T(8,128)(2,1)S(1)}, u32[]{:S(2)}, u32[]{:S(2)}) collective-permute-start(bf16[2,8,1280]{2,1,0:T(8,128)(2,1)S(1)} %get-tuple-element.23), channel_id=1, source_target_pairs={{0,16},{16,0},{1,17},{17,1},{2,18},{18,2},{3,19},{19,3},{4,20},{20... | collective-permute-start | bytes 122888 | tf_op jit(solution)/shard_map/ppermute | solution.py:456
  4.7 24.5 %all-to-all-start = ((bf16[128,2,8,128]{3,2,1,0:T(8,128)(2,1)}), bf16[128,2,8,128]{3,2,1,0:T(8,128)(2,1)S(1)}, u32[]{:S(2)}, u32[]{:S(2)}) async-start(bf16[128,2,8,128]{3,2,1,0:T(8,128)(2,1)} %bitcast.4), calls=%async_computation | async-start | bytes 1048576 | tf_op jit(solution)/shard_map/all_to_all | solution.py:490
  15.2 20.4 %copy-start.3 = (f32[2,9,2,8]{1,3,2,0:T(8,128)S(1)}, f32[2,9,2,8]{1,3,2,0:T(8,128)}, u32[]{:S(2)}) copy-start(f32[2,9,2,8]{1,3,2,0:T(8,128)} %param.16) | copy-start | bytes 3460
  16.1 8.9 %collective-permute-start.1 = (bf16[2,2,8,1280]{3,2,1,0:T(8,128)(2,1)S(1)}, bf16[2,2,8,1280]{3,2,1,0:T(8,128)(2,1)S(1)}, u32[]{:S(2)}, u32[]{:S(2)}) collective-permute-start(bf16[2,2,8,1280]{3,2,1,0:T(8,128)(2,1)S(1)} %maximum_select_fusion.rows0), channel_id=1, source_target_pairs={{0,32},{32,64},{64,96},{96,0},{1,33},{33,65},{65,97},{97,1},{2,34}... | collective-permute-start | bytes 245768 | tf_op jit(solution)/shard_map/ppermute | solution.py:451
  17.6 9.4 %collective-permute-start.2 = (bf16[2,2,8,1280]{3,2,1,0:T(8,128)(2,1)S(1)}, bf16[2,2,8,1280]{3,2,1,0:T(8,128)(2,1)S(1)}, u32[]{:S(2)}, u32[]{:S(2)}) collective-permute-start(bf16[2,2,8,1280]{3,2,1,0:T(8,128)(2,1)S(1)} %maximum_select_fusion.rows0), channel_id=1, source_target_pairs={{0,64},{32,96},{64,0},{96,32},{1,65},{33,97},{65,1},{97,33},{2,66}... | collective-permute-start | bytes 245768 | tf_op jit(solution)/shard_map/ppermute | solution.py:451
  19.9 7.0 %collective-permute-start.3 = (bf16[2,2,8,1280]{3,2,1,0:T(8,128)(2,1)S(1)}, bf16[2,2,8,1280]{3,2,1,0:T(8,128)(2,1)S(1)}, u32[]{:S(2)}, u32[]{:S(2)}) collective-permute-start(bf16[2,2,8,1280]{3,2,1,0:T(8,128)(2,1)S(1)} %maximum_select_fusion.rows0), channel_id=1, source_target_pairs={{0,96},{32,0},{64,32},{96,64},{1,97},{33,1},{65,33},{97,65},{2,98}... | collective-permute-start | bytes 245768 | tf_op jit(solution)/shard_map/ppermute | solution.py:451
  30.8 12.5 %all-to-all-start.1 = ((bf16[16,64,128]{2,1,0:T(8,128)(2,1)}), bf16[16,64,128]{2,1,0:T(8,128)(2,1)S(1)}, u32[]{:S(2)}, u32[]{:S(2)}) async-start(bf16[16,64,128]{2,1,0:T(8,128)(2,1)} %get-tuple-element.24), calls=%async_computation.1 | async-start | bytes 524288 | tf_op jit(solution)/shard_map/all_to_all | solution.py:498
  45.3 22.4 %all-to-all-start.2 = ((bf16[64,72,128]{2,1,0:T(8,128)(2,1)}), bf16[64,72,128]{2,1,0:T(8,128)(2,1)S(1)}, u32[]{:S(2)}, u32[]{:S(2)}) async-start(bf16[64,72,128]{2,1,0:T(8,128)(2,1)} %second_rows.1), calls=%async_computation.2 | async-start | bytes 2359296 | tf_op jit(solution)/shard_map/all_to_all | solution.py:504
  50.0 22.4 %collective-permute-start.5 = (bf16[1024,128]{1,0:T(8,128)(2,1)S(1)}, bf16[1024,128]{1,0:T(8,128)(2,1)S(1)}, u32[]{:S(2)}, u32[]{:S(2)}) collective-permute-start(bf16[1024,128]{1,0:T(8,128)(2,1)S(1)} %get-tuple-element.25), channel_id=1, source_target_pairs={{0,32},{32,64},{64,96},{96,0},{1,33},{33,65},{65,97},{97,1},{2,34}... | collective-permute-start | bytes 786440 | tf_op jit(solution)/shard_map/ppermute | solution.py:451
  51.1 23.8 %collective-permute-start.6 = (bf16[1024,128]{1,0:T(8,128)(2,1)S(1)}, bf16[1024,128]{1,0:T(8,128)(2,1)S(1)}, u32[]{:S(2)}, u32[]{:S(2)}) collective-permute-start(bf16[1024,128]{1,0:T(8,128)(2,1)S(1)} %get-tuple-element.25), channel_id=1, source_target_pairs={{0,64},{32,96},{64,0},{96,32},{1,65},{33,97},{65,1},{97,33},{2,66}... | collective-permute-start | bytes 786440 | tf_op jit(solution)/shard_map/ppermute | solution.py:451
  53.7 21.2 %collective-permute-start.7 = (bf16[1024,128]{1,0:T(8,128)(2,1)S(1)}, bf16[1024,128]{1,0:T(8,128)(2,1)S(1)}, u32[]{:S(2)}, u32[]{:S(2)}) collective-permute-start(bf16[1024,128]{1,0:T(8,128)(2,1)S(1)} %get-tuple-element.25), channel_id=1, source_target_pairs={{0,96},{32,0},{64,32},{96,64},{1,97},{33,1},{65,33},{97,65},{2,98}... | collective-permute-start | bytes 786440 | tf_op jit(solution)/shard_map/ppermute | solution.py:451
  67.7 29.1 %collective-permute-start.4 = (bf16[64,72,128]{2,1,0:T(8,128)(2,1)S(1)}, bf16[64,72,128]{2,1,0:T(8,128)(2,1)S(1)}, u32[]{:S(2)}, u32[]{:S(2)}) collective-permute-start(bf16[64,72,128]{2,1,0:T(8,128)(2,1)S(1)} %all-to-all-done.2), channel_id=1, source_target_pairs={{0,16},{16,0},{1,17},{17,1},{2,18},{18,2},{3,19},{19,3},{4,20},{20... | collective-permute-start | bytes 3538952 | tf_op jit(solution)/shard_map/ppermute | solution.py:456
  75.0 5.6 %collective-permute-start.8 = (bf16[4,1024,128]{2,1,0:T(8,128)(2,1)S(1)}, bf16[4,1024,128]{2,1,0:T(8,128)(2,1)S(1)}, u32[]{:S(2)}, u32[]{:S(2)}) collective-permute-start(bf16[4,1024,128]{2,1,0:T(8,128)(2,1)S(1)} %pad_maximum_fusion.mine), channel_id=1, source_target_pairs={{0,16},{16,0},{1,17},{17,1},{2,18},{18,2},{3,19},{19,3},{4,20},{20... | collective-permute-start | bytes 3145736 | tf_op jit(solution)/shard_map/ppermute | solution.py:456
  91.3 5.5 %copy-start.1 = (f32[1024,128]{1,0:T(8,128)S(1)}, f32[1024,128]{1,0:T(8,128)}, u32[]{:S(2)}) copy-start(f32[1024,128]{1,0:T(8,128)} %get-tuple-element.34.before) | copy-start | bytes 1572868
  91.3 5.5 %copy-start.2 = (bf16[128,768]{1,0:T(8,128)(2,1)S(1)}, bf16[128,768]{1,0:T(8,128)(2,1)}, u32[]{:S(2)}) copy-start(bf16[128,768]{1,0:T(8,128)(2,1)} %constant.54.clone.spread) | copy-start | bytes 589828

commit v8 on v7

--- a/solution.py
+++ b/solution.py
@@ -278,13 +278,12 @@
 
 
 def trail_mine_kernel(
-    place, received, factor, early, total, out, own, blocks, tiles, later, rest, arrived, rows, before, done, sems
+    place, received, factor, early, total, out, own, blocks, tiles, later, rest, rows, before, done, sems
 ):
     core = place[1]
     height = rows.shape[1] // 2
     copy = pltpu.make_async_copy
     cuts = [pl.ds(i * height, height) for i in range(4)]
-    take = copy(received, arrived, sems.at[0])
     take_row = copy(factor.at[core, 1, :, pl.ds(2 * height, 2 * height)], rows, sems.at[1])
     halves = [pl.ds(0, 2 * height), pl.ds(2 * height, 2 * height)]
     take_before = [
@@ -295,12 +294,10 @@
     take_later = [
         copy(factor.at[1 - core, 1, :, cuts[i]], later.at[i], sems.at[8 + i]) for i in range(4)
     ]
-    take.start()
     take_before[0].start()
-    take.wait()
     for one in (take_row, take_before[1], *take_later, take_rest):
         one.start()
-    own[0], own[1] = take_blocks(place, arrived, blocks, tiles)
+    own[0], own[1] = take_blocks(place, received, blocks, tiles)
     take_before[0].wait()
     for i in range(2):
         product = trail_product(early[i].reshape(2 * height, 1024), blocks)
@@ -324,7 +321,7 @@
     outside = pl.BlockSpec(memory_space=pltpu.HBM)
     return pl.pallas_call(
         trail_mine_kernel,
-        in_specs=[pl.BlockSpec(memory_space=pltpu.SMEM), outside, outside, inside, outside],
+        in_specs=[pl.BlockSpec(memory_space=pltpu.SMEM), inside, outside, inside, outside],
         out_specs=[outside] + [inside] * 5,
         out_shape=[
             pltpu.HBM((2, 2, rows, 256), BF16),
@@ -335,7 +332,6 @@
             pltpu.VMEM((2, rows, 256), F32),
         ],
         scratch_shapes=[
-            pltpu.VMEM((4, 16, 72, 128), BF16),
             pltpu.VMEM((2, 2 * height, 1024), BF16),
             pltpu.VMEM((2, rows, 256), F32),
             pltpu.VMEM((4, 2, height, 256), BF16),

time: 102 us -> 102 us (level)
  no operation moved by 1% of the time
where the time goes in v8:
time: 102 us
  starting transfers between devices  38.9 us (38%)
  waiting for transfers between devices  33.1 us (32%)
  Pallas kernels  27.4 us (27%)
  local copies, waits for them, and re-layouts  1.3 us (1%)
    all_to_all x1, waiting for transfers between devices, steps(): second_mine = lax.all_to_all(send, ('x', 'col'), 0, 0, tiled=True)  12.9 us
    pallas_call x1, Pallas kernels, trail_first(): pl.pallas_call(trail_first_kernel, in_specs=[pl.BlockSpec(memory_space=pl...  10.6 us
    all_to_all x1, starting transfers between devices, steps(): lax.all_to_all(send.reshape(128, 2, 8, 128), ALL, 0, 0, tiled=True)  10.2 us
    ppermute x6, starting transfers between devices, rounds_x(): lax.ppermute(value, 'x', [(i, (i + step) % 4) for i in range(4)])  9.75 us
    ppermute x3, starting transfers between devices, swap_core(): return lax.ppermute(value, 'core', [(0, 1), (1, 0)])  9.47 us
    ppermute x6, waiting for transfers between devices, rounds_x(): lax.ppermute(value, 'x', [(i, (i + step) % 4) for i in range(4)])  8.21 us
    all_to_all x1, waiting for transfers between devices, steps(): received = lax.all_to_all(send, 'col', 0, 0, tiled=True)  7.44 us
    pallas_call x1, Pallas kernels, trail_mine(): pl.pallas_call(trail_mine_kernel, in_specs=[pl.BlockSpec(memory_space=plt...  5.57 us
  transfers between devices with their start and end apart: 12, of which 7 were waited for; matrix products, arithmetic and copies ran while one was open for 1% of the time, Pallas kernels for 16%

profile of v8, /device:TPU:1, one launch (start us, length us, event | category | flops | bytes accessed | tf_op | source)
XLA Modules:
  0.0 102.0 jit_solution(16870186845686769153)
XLA Ops:
  0.7 2.7 %prepare.1 = (bf16[2,2,8,256]{3,2,1,0:T(8,128)(2,1)S(1)}, bf16[4,2,16,2,8,128]{5,4,3,2,1,0:T(8,128)(2,1)}, bf16[2,8,1280]{2,1,0:T(8,128)(2,1)S(1)}, bf16[2,8,1280]{2,1,0:T(8,128)(2,1)S(1)}) custom-call(bf16[2,2,2,8,1024]{4,3,2,1,0:T(8,128)(2,1)} %inverse.1, bf16[2,2,1024,256]{3,2,1,0:T(8,128)(2,1)} %rhs.2, bf16[2,2,8,1024]{3,2,1,0:T(8,128)(2,1)} %below.1, ...), custom_call_target="tpu_custom_call" | custom-call | tf_op jit(solution)/shard_map/prepare/pallas_call | solution.py:83
  3.3 1.4 %collective-permute-start = (bf16[2,8,1280]{2,1,0:T(8,128)(2,1)S(1)}, bf16[2,8,1280]{2,1,0:T(8,128)(2,1)S(1)}, u32[]{:S(2)}, u32[]{:S(2)}) collective-permute-start(bf16[2,8,1280]{2,1,0:T(8,128)(2,1)S(1)} %get-tuple-element.23), channel_id=1, source_target_pairs={{0,16},{16,0},{1,17},{17,1},{2,18},{18,2},{3,19},{19,3},{4,20},{20... | collective-permute-start | bytes 122888 | tf_op jit(solution)/shard_map/ppermute | solution.py:452
  4.7 10.2 %all-to-all-start = ((bf16[128,2,8,128]{3,2,1,0:T(8,128)(2,1)}), bf16[128,2,8,128]{3,2,1,0:T(8,128)(2,1)S(1)}, u32[]{:S(2)}, u32[]{:S(2)}) async-start(bf16[128,2,8,128]{3,2,1,0:T(8,128)(2,1)} %bitcast.4), calls=%async_computation | async-start | bytes 1048576 | tf_op jit(solution)/shard_map/all_to_all | solution.py:486
  15.0 0.1 copy.22
  15.1 0.1 reshape.28
  15.2 0.7 gather_fusion
  15.9 0.1 reshape.27
  16.1 1.4 %collective-permute-start.1 = (bf16[2,2,8,1280]{3,2,1,0:T(8,128)(2,1)S(1)}, bf16[2,2,8,1280]{3,2,1,0:T(8,128)(2,1)S(1)}, u32[]{:S(2)}, u32[]{:S(2)}) collective-permute-start(bf16[2,2,8,1280]{3,2,1,0:T(8,128)(2,1)S(1)} %maximum_select_fusion.rows0), channel_id=1, source_target_pairs={{0,32},{32,64},{64,96},{96,0},{1,33},{33,65},{65,97},{97,1},{2,34}... | collective-permute-start | bytes 245768 | tf_op jit(solution)/shard_map/ppermute | solution.py:447
  17.6 2.4 %collective-permute-start.2 = (bf16[2,2,8,1280]{3,2,1,0:T(8,128)(2,1)S(1)}, bf16[2,2,8,1280]{3,2,1,0:T(8,128)(2,1)S(1)}, u32[]{:S(2)}, u32[]{:S(2)}) collective-permute-start(bf16[2,2,8,1280]{3,2,1,0:T(8,128)(2,1)S(1)} %maximum_select_fusion.rows0), channel_id=1, source_target_pairs={{0,64},{32,96},{64,0},{96,32},{1,65},{33,97},{65,1},{97,33},{2,66}... | collective-permute-start | bytes 245768 | tf_op jit(solution)/shard_map/ppermute | solution.py:447
  19.9 1.2 %collective-permute-start.3 = (bf16[2,2,8,1280]{3,2,1,0:T(8,128)(2,1)S(1)}, bf16[2,2,8,1280]{3,2,1,0:T(8,128)(2,1)S(1)}, u32[]{:S(2)}, u32[]{:S(2)}) collective-permute-start(bf16[2,2,8,1280]{3,2,1,0:T(8,128)(2,1)S(1)} %maximum_select_fusion.rows0), channel_id=1, source_target_pairs={{0,96},{32,0},{64,32},{96,64},{1,97},{33,1},{65,33},{97,65},{2,98}... | collective-permute-start | bytes 245768 | tf_op jit(solution)/shard_map/ppermute | solution.py:447
  21.2 3.8 %collective-permute-done.1.rows1 = bf16[2,2,8,1280]{3,2,1,0:T(8,128)(2,1)S(1)} collective-permute-done((bf16[2,2,8,1280]{3,2,1,0:T(8,128)(2,1)S(1)}, bf16[2,2,8,1280]{3,2,1,0:T(8,128)(2,1)S(1)}, u32[]{:S(2)}, u32[]{:S(2)}) %collective-permute-start.1) | collective-permute-done | bytes 81952 | tf_op jit(solution)/shard_map/ppermute | solution.py:447
  25.0 1.9 %collective-permute-done.2.rows2 = bf16[2,2,8,1280]{3,2,1,0:T(8,128)(2,1)S(1)} collective-permute-done((bf16[2,2,8,1280]{3,2,1,0:T(8,128)(2,1)S(1)}, bf16[2,2,8,1280]{3,2,1,0:T(8,128)(2,1)S(1)}, u32[]{:S(2)}, u32[]{:S(2)}) %collective-permute-start.2) | collective-permute-done | bytes 81952 | tf_op jit(solution)/shard_map/ppermute | solution.py:447
  26.9 2.3 %all-to-all-done.received = bf16[128,2,8,128]{3,2,1,0:T(8,128)(2,1)S(1)} async-done(((bf16[128,2,8,128]{3,2,1,0:T(8,128)(2,1)}), bf16[128,2,8,128]{3,2,1,0:T(8,128)(2,1)S(1)}, u32[]{:S(2)}, u32[]{:S(2)}) %all-to-all-start) | async-done | bytes 524320 | tf_op jit(solution)/shard_map/all_to_all | solution.py:486
  29.2 1.6 %right_side.1 = (bf16[1024,128]{1,0:T(8,128)(2,1)S(1)}, bf16[16,64,128]{2,1,0:T(8,128)(2,1)}) custom-call(s32[4]{0:T(128)S(1)} %pad_add_fusion.place, bf16[128,2,8,128]{3,2,1,0:T(8,128)(2,1)S(1)} %all-to-all-done.received, bf16[2,2,8,1280]{3,2,1,0:T(8,128)(2,1)S(1)} %maximum_select_fusion.rows0, bf16[2,2,8,1280]{3,2,1,0:T(8,128)(2,1)S(1)} %collective-permute-done.1.rows1, ...), custom_call_target="tpu_custom_call" | custom-call | tf_op jit(solution)/shard_map/right_side/pallas_call | solution.py:132
  30.8 4.8 %all-to-all-start.1 = ((bf16[16,64,128]{2,1,0:T(8,128)(2,1)}), bf16[16,64,128]{2,1,0:T(8,128)(2,1)S(1)}, u32[]{:S(2)}, u32[]{:S(2)}) async-start(bf16[16,64,128]{2,1,0:T(8,128)(2,1)} %get-tuple-element.24), calls=%async_computation.1 | async-start | bytes 524288 | tf_op jit(solution)/shard_map/all_to_all | solution.py:494
  35.6 0.1 reshape.22
  35.7 0.1 concatenate.4.tile
  35.8 7.4 %all-to-all-done.1.received = bf16[16,64,128]{2,1,0:T(8,128)(2,1)S(1)} async-done(((bf16[16,64,128]{2,1,0:T(8,128)(2,1)}), bf16[16,64,128]{2,1,0:T(8,128)(2,1)S(1)}, u32[]{:S(2)}, u32[]{:S(2)}) %all-to-all-start.1) | async-done | bytes 262176 | tf_op jit(solution)/shard_map/all_to_all | solution.py:494
  43.3 2.0 %second_rows.1 = bf16[64,72,128]{2,1,0:T(8,128)(2,1)} custom-call(s32[4]{0:T(128)S(1)} %pad_add_fusion.place, bf16[16,64,128]{2,1,0:T(8,128)(2,1)S(1)} %all-to-all-done.1.received, bf16[2,2,8,1280]{3,2,1,0:T(8,128)(2,1)S(1)} %maximum_select_fusion.rows0, bf16[2,2,8,1280]{3,2,1,0:T(8,128)(2,1)S(1)} %collective-permute-done.1.rows1, ...), custom_call_target="tpu_custom_call" | custom-call | tf_op jit(solution)/shard_map/second_rows/pallas_call | solution.py:167
  45.3 4.7 %all-to-all-start.2 = ((bf16[64,72,128]{2,1,0:T(8,128)(2,1)}), bf16[64,72,128]{2,1,0:T(8,128)(2,1)S(1)}, u32[]{:S(2)}, u32[]{:S(2)}) async-start(bf16[64,72,128]{2,1,0:T(8,128)(2,1)} %second_rows.1), calls=%async_computation.2 | async-start | bytes 2359296 | tf_op jit(solution)/shard_map/all_to_all | solution.py:500
  50.0 1.1 %collective-permute-start.5 = (bf16[1024,128]{1,0:T(8,128)(2,1)S(1)}, bf16[1024,128]{1,0:T(8,128)(2,1)S(1)}, u32[]{:S(2)}, u32[]{:S(2)}) collective-permute-start(bf16[1024,128]{1,0:T(8,128)(2,1)S(1)} %get-tuple-element.25), channel_id=1, source_target_pairs={{0,32},{32,64},{64,96},{96,0},{1,33},{33,65},{65,97},{97,1},{2,34}... | collective-permute-start | bytes 786440 | tf_op jit(solution)/shard_map/ppermute | solution.py:447
  51.1 2.6 %collective-permute-start.6 = (bf16[1024,128]{1,0:T(8,128)(2,1)S(1)}, bf16[1024,128]{1,0:T(8,128)(2,1)S(1)}, u32[]{:S(2)}, u32[]{:S(2)}) collective-permute-start(bf16[1024,128]{1,0:T(8,128)(2,1)S(1)} %get-tuple-element.25), channel_id=1, source_target_pairs={{0,64},{32,96},{64,0},{96,32},{1,65},{33,97},{65,1},{97,33},{2,66}... | collective-permute-start | bytes 786440 | tf_op jit(solution)/shard_map/ppermute | solution.py:447
  53.7 1.1 %collective-permute-start.7 = (bf16[1024,128]{1,0:T(8,128)(2,1)S(1)}, bf16[1024,128]{1,0:T(8,128)(2,1)S(1)}, u32[]{:S(2)}, u32[]{:S(2)}) collective-permute-start(bf16[1024,128]{1,0:T(8,128)(2,1)S(1)} %get-tuple-element.25), channel_id=1, source_target_pairs={{0,96},{32,0},{64,32},{96,64},{1,97},{33,1},{65,33},{97,65},{2,98}... | collective-permute-start | bytes 786440 | tf_op jit(solution)/shard_map/ppermute | solution.py:447
  54.8 12.9 %all-to-all-done.2 = bf16[64,72,128]{2,1,0:T(8,128)(2,1)S(1)} async-done(((bf16[64,72,128]{2,1,0:T(8,128)(2,1)}), bf16[64,72,128]{2,1,0:T(8,128)(2,1)S(1)}, u32[]{:S(2)}, u32[]{:S(2)}) %all-to-all-start.2) | async-done | bytes 1179680 | tf_op jit(solution)/shard_map/all_to_all | solution.py:500
  67.7 4.8 %collective-permute-start.4 = (bf16[64,72,128]{2,1,0:T(8,128)(2,1)S(1)}, bf16[64,72,128]{2,1,0:T(8,128)(2,1)S(1)}, u32[]{:S(2)}, u32[]{:S(2)}) collective-permute-start(bf16[64,72,128]{2,1,0:T(8,128)(2,1)S(1)} %all-to-all-done.2), channel_id=1, source_target_pairs={{0,16},{16,0},{1,17},{17,1},{2,18},{18,2},{3,19},{19,3},{4,20},{20... | collective-permute-start | bytes 3538952 | tf_op jit(solution)/shard_map/ppermute | solution.py:452
  72.4 2.5 %collective-permute-done.6 = bf16[1024,128]{1,0:T(8,128)(2,1)S(1)} collective-permute-done((bf16[1024,128]{1,0:T(8,128)(2,1)S(1)}, bf16[1024,128]{1,0:T(8,128)(2,1)S(1)}, u32[]{:S(2)}, u32[]{:S(2)}) %collective-permute-start.6) | collective-permute-done | bytes 262176 | tf_op jit(solution)/shard_map/ppermute | solution.py:447
  74.9 0.1 pad_maximum_fusion.mine
  75.0 3.3 %collective-permute-start.8 = (bf16[4,1024,128]{2,1,0:T(8,128)(2,1)S(1)}, bf16[4,1024,128]{2,1,0:T(8,128)(2,1)S(1)}, u32[]{:S(2)}, u32[]{:S(2)}) collective-permute-start(bf16[4,1024,128]{2,1,0:T(8,128)(2,1)S(1)} %pad_maximum_fusion.mine), channel_id=1, source_target_pairs={{0,16},{16,0},{1,17},{17,1},{2,18},{18,2},{3,19},{19,3},{4,20},{20... | collective-permute-start | bytes 3145736 | tf_op jit(solution)/shard_map/ppermute | solution.py:452
  78.4 2.3 %collective-permute-done.8.theirs = bf16[4,1024,128]{2,1,0:T(8,128)(2,1)S(1)} collective-permute-done((bf16[4,1024,128]{2,1,0:T(8,128)(2,1)S(1)}, bf16[4,1024,128]{2,1,0:T(8,128)(2,1)S(1)}, u32[]{:S(2)}, u32[]{:S(2)}) %collective-permute-start.8) | collective-permute-done | bytes 1048608 | tf_op jit(solution)/shard_map/ppermute | solution.py:452
  80.7 10.6 %trail_first.1 = (f32[2,2,1024,256]{3,2,1,0:T(8,128)}, f32[1024,128]{1,0:T(8,128)}, bf16[2,2,256,1024]{3,2,1,0:T(8,128)(2,1)S(1)}) custom-call(s32[4]{0:T(128)S(1)} %pad_add_fusion.place, bf16[4,1024,128]{2,1,0:T(8,128)(2,1)S(1)} %pad_maximum_fusion.mine, bf16[4,1024,128]{2,1,0:T(8,128)(2,1)S(1)} %collective-permute-done.8.theirs, ...), custom_call_target="tpu_custom_call" | custom-call | tf_op jit(solution)/shard_map/trail_first/pallas_call | solution.py:236
  91.3 5.6 %trail_mine.1 = (bf16[2,2,1024,256]{3,2,1,0:T(8,128)(2,1)}, bf16[2,8,256]{2,1,0:T(8,128)(2,1)S(1)}, bf16[1024,512]{1,0:T(8,128)(2,1)S(1)}, bf16[4,128,128]{2,1,0...) custom-call(s32[4]{0:T(128)S(1)} %pad_add_fusion.place, ...), custom_call_target="tpu_custom_call" | custom-call | tf_op jit(solution)/shard_map/trail_mine/pallas_call | solution.py:322
  96.9 5.0 %trail_theirs.1 = (bf16[2,2,1024,256]{3,2,1,0:T(8,128)(2,1)}, bf16[2,2,2,8,256]{4,3,2,1,0:T(8,128)(2,1)}, f32[3,8]{1,0:T(4,128)}) custom-call(s32[4]{0:T(128)S(1)} %pad_add_fusion.place, bf16[4,16,72,128]{3,2,1,0:T(8,128)(2,1)S(1)} %bitcast.16, bf16[4,2,256,1024]{3,2,1,0:T(8,128)(2,1)S(1)} %get-tuple-element.28.rows, ...), custom_call_target="tpu_custom_call", output_to_operand_aliasing={{0}: (10, {})} | custom-call | tf_op jit(solution)/shard_map/trail_theirs/pallas_call | solution.py:374
  (25 shorter events, 0.3 us)
Async XLA Ops:
  0.6 14.5 %copy-start = (s32[1024]{0:T(1024)S(1)}, s32[1024]{0:T(1024)}, u32[]{:S(2)}) copy-start(s32[1024]{0:T(1024)} %param.18) | copy-start | bytes 12292
  0.6 14.3 %copy-start.4 = (s32[2,8,3]{1,0,2:T(2,128)S(1)}, s32[2,8,3]{1,0,2:T(2,128)}, u32[]{:S(2)}) copy-start(s32[2,8,3]{1,0,2:T(2,128)} %param.17) | copy-start | bytes 580
  3.3 12.8 %collective-permute-start = (bf16[2,8,1280]{2,1,0:T(8,128)(2,1)S(1)}, bf16[2,8,1280]{2,1,0:T(8,128)(2,1)S(1)}, u32[]{:S(2)}, u32[]{:S(2)}) collective-permute-start(bf16[2,8,1280]{2,1,0:T(8,128)(2,1)S(1)} %get-tuple-element.23), channel_id=1, source_target_pairs={{0,16},{16,0},{1,17},{17,1},{2,18},{18,2},{3,19},{19,3},{4,20},{20... | collective-permute-start | bytes 122888 | tf_op jit(solution)/shard_map/ppermute | solution.py:452
  4.7 24.5 %all-to-all-start = ((bf16[128,2,8,128]{3,2,1,0:T(8,128)(2,1)}), bf16[128,2,8,128]{3,2,1,0:T(8,128)(2,1)S(1)}, u32[]{:S(2)}, u32[]{:S(2)}) async-start(bf16[128,2,8,128]{3,2,1,0:T(8,128)(2,1)} %bitcast.4), calls=%async_computation | async-start | bytes 1048576 | tf_op jit(solution)/shard_map/all_to_all | solution.py:486
  15.2 20.4 %copy-start.3 = (f32[2,9,2,8]{1,3,2,0:T(8,128)S(1)}, f32[2,9,2,8]{1,3,2,0:T(8,128)}, u32[]{:S(2)}) copy-start(f32[2,9,2,8]{1,3,2,0:T(8,128)} %param.16) | copy-start | bytes 3460
  16.1 8.9 %collective-permute-start.1 = (bf16[2,2,8,1280]{3,2,1,0:T(8,128)(2,1)S(1)}, bf16[2,2,8,1280]{3,2,1,0:T(8,128)(2,1)S(1)}, u32[]{:S(2)}, u32[]{:S(2)}) collective-permute-start(bf16[2,2,8,1280]{3,2,1,0:T(8,128)(2,1)S(1)} %maximum_select_fusion.rows0), channel_id=1, source_target_pairs={{0,32},{32,64},{64,96},{96,0},{1,33},{33,65},{65,97},{97,1},{2,34}... | collective-permute-start | bytes 245768 | tf_op jit(solution)/shard_map/ppermute | solution.py:447
  17.6 9.4 %collective-permute-start.2 = (bf16[2,2,8,1280]{3,2,1,0:T(8,128)(2,1)S(1)}, bf16[2,2,8,1280]{3,2,1,0:T(8,128)(2,1)S(1)}, u32[]{:S(2)}, u32[]{:S(2)}) collective-permute-start(bf16[2,2,8,1280]{3,2,1,0:T(8,128)(2,1)S(1)} %maximum_select_fusion.rows0), channel_id=1, source_target_pairs={{0,64},{32,96},{64,0},{96,32},{1,65},{33,97},{65,1},{97,33},{2,66}... | collective-permute-start | bytes 245768 | tf_op jit(solution)/shard_map/ppermute | solution.py:447
  19.9 7.0 %collective-permute-start.3 = (bf16[2,2,8,1280]{3,2,1,0:T(8,128)(2,1)S(1)}, bf16[2,2,8,1280]{3,2,1,0:T(8,128)(2,1)S(1)}, u32[]{:S(2)}, u32[]{:S(2)}) collective-permute-start(bf16[2,2,8,1280]{3,2,1,0:T(8,128)(2,1)S(1)} %maximum_select_fusion.rows0), channel_id=1, source_target_pairs={{0,96},{32,0},{64,32},{96,64},{1,97},{33,1},{65,33},{97,65},{2,98}... | collective-permute-start | bytes 245768 | tf_op jit(solution)/shard_map/ppermute | solution.py:447
  30.8 12.5 %all-to-all-start.1 = ((bf16[16,64,128]{2,1,0:T(8,128)(2,1)}), bf16[16,64,128]{2,1,0:T(8,128)(2,1)S(1)}, u32[]{:S(2)}, u32[]{:S(2)}) async-start(bf16[16,64,128]{2,1,0:T(8,128)(2,1)} %get-tuple-element.24), calls=%async_computation.1 | async-start | bytes 524288 | tf_op jit(solution)/shard_map/all_to_all | solution.py:494
  45.3 22.4 %all-to-all-start.2 = ((bf16[64,72,128]{2,1,0:T(8,128)(2,1)}), bf16[64,72,128]{2,1,0:T(8,128)(2,1)S(1)}, u32[]{:S(2)}, u32[]{:S(2)}) async-start(bf16[64,72,128]{2,1,0:T(8,128)(2,1)} %second_rows.1), calls=%async_computation.2 | async-start | bytes 2359296 | tf_op jit(solution)/shard_map/all_to_all | solution.py:500
  50.0 22.4 %collective-permute-start.5 = (bf16[1024,128]{1,0:T(8,128)(2,1)S(1)}, bf16[1024,128]{1,0:T(8,128)(2,1)S(1)}, u32[]{:S(2)}, u32[]{:S(2)}) collective-permute-start(bf16[1024,128]{1,0:T(8,128)(2,1)S(1)} %get-tuple-element.25), channel_id=1, source_target_pairs={{0,32},{32,64},{64,96},{96,0},{1,33},{33,65},{65,97},{97,1},{2,34}... | collective-permute-start | bytes 786440 | tf_op jit(solution)/shard_map/ppermute | solution.py:447
  51.1 23.8 %collective-permute-start.6 = (bf16[1024,128]{1,0:T(8,128)(2,1)S(1)}, bf16[1024,128]{1,0:T(8,128)(2,1)S(1)}, u32[]{:S(2)}, u32[]{:S(2)}) collective-permute-start(bf16[1024,128]{1,0:T(8,128)(2,1)S(1)} %get-tuple-element.25), channel_id=1, source_target_pairs={{0,64},{32,96},{64,0},{96,32},{1,65},{33,97},{65,1},{97,33},{2,66}... | collective-permute-start | bytes 786440 | tf_op jit(solution)/shard_map/ppermute | solution.py:447
  53.7 21.2 %collective-permute-start.7 = (bf16[1024,128]{1,0:T(8,128)(2,1)S(1)}, bf16[1024,128]{1,0:T(8,128)(2,1)S(1)}, u32[]{:S(2)}, u32[]{:S(2)}) collective-permute-start(bf16[1024,128]{1,0:T(8,128)(2,1)S(1)} %get-tuple-element.25), channel_id=1, source_target_pairs={{0,96},{32,0},{64,32},{96,64},{1,97},{33,1},{65,33},{97,65},{2,98}... | collective-permute-start | bytes 786440 | tf_op jit(solution)/shard_map/ppermute | solution.py:447
  67.7 29.2 %collective-permute-start.4 = (bf16[64,72,128]{2,1,0:T(8,128)(2,1)S(1)}, bf16[64,72,128]{2,1,0:T(8,128)(2,1)S(1)}, u32[]{:S(2)}, u32[]{:S(2)}) collective-permute-start(bf16[64,72,128]{2,1,0:T(8,128)(2,1)S(1)} %all-to-all-done.2), channel_id=1, source_target_pairs={{0,16},{16,0},{1,17},{17,1},{2,18},{18,2},{3,19},{19,3},{4,20},{20... | collective-permute-start | bytes 3538952 | tf_op jit(solution)/shard_map/ppermute | solution.py:452
  75.0 5.6 %collective-permute-start.8 = (bf16[4,1024,128]{2,1,0:T(8,128)(2,1)S(1)}, bf16[4,1024,128]{2,1,0:T(8,128)(2,1)S(1)}, u32[]{:S(2)}, u32[]{:S(2)}) collective-permute-start(bf16[4,1024,128]{2,1,0:T(8,128)(2,1)S(1)} %pad_maximum_fusion.mine), channel_id=1, source_target_pairs={{0,16},{16,0},{1,17},{17,1},{2,18},{18,2},{3,19},{19,3},{4,20},{20... | collective-permute-start | bytes 3145736 | tf_op jit(solution)/shard_map/ppermute | solution.py:452
  91.3 5.6 %copy-start.1 = (f32[1024,128]{1,0:T(8,128)S(1)}, f32[1024,128]{1,0:T(8,128)}, u32[]{:S(2)}) copy-start(f32[1024,128]{1,0:T(8,128)} %get-tuple-element.34.before) | copy-start | bytes 1572868
  91.3 5.6 %copy-start.2 = (bf16[128,768]{1,0:T(8,128)(2,1)S(1)}, bf16[128,768]{1,0:T(8,128)(2,1)}, u32[]{:S(2)}) copy-start(bf16[128,768]{1,0:T(8,128)(2,1)} %constant.54.clone.spread) | copy-start | bytes 589828
